TPU v7x, 32 devices: a whole 2x2x4 slice. The times are simulated.
32 devices in a mesh: groups: 2 (over y), level: 4 (over z), src: 2 (over x), phase: 2 (over core).
Axes of the slice: x: 2, y: 2, z: 4, core: 2. Of those that a mesh axis runs over, the one named last changes fastest.
Arguments:
- state_values: float32 [24, 8, 32, 16, 128], P(('groups', 'level'), 'src', 'phase'), parts along dimension 0, may hold values from -6 to 6
- phase_rates: float32 [64, 32], P('groups'), parts along dimension 0, may hold values from 0.05 to 2
- batch_rates: float32 [32, 32, 32], P('groups'), parts along dimension 0, may hold values from 0.02 to 1
- service_rates: float32 [4], P('groups'), parts along dimension 0, may hold values from 20 to 60
- source_rates: float32 [6, 3], P('groups'), parts along dimension 0, may hold values from 2 to 30
- tile_levels: int32 [16, 2], P('groups'), parts along dimension 0, may hold values from 0 to 3, as said below
- routes: int32 [16, 5], P('groups'), parts along dimension 0, may hold values from -1 to 7, as said below
- tile_owner: int32 [16], P('groups'), parts along dimension 0, may hold values from 0 to 11, as said below
Outputs:
- stepped_values: float32 [24, 8, 32, 16, 128], P(('groups', 'level'), 'src', 'phase'), parts along dimension 0
There are 2 independent parts, one for each index of `groups`. A program takes and returns all parts, laid end to end along the dimension named above; each array names one. Nothing has to cross between parts.
Inputs may be any that keep to these rules, and one draw needn't show every extreme that they name: `tile_levels`: row t is the tile (a, c) covering buffer-one levels a * 128 to a * 128 + 127 and buffer-two levels c * 16 to c * 16 + 15; tiles are numbered column by column (c rising, then a rising), every c from 0 to 3 has tiles a = 0, 1, ... up to its own height, and the tallest column has 3 tiles. routes[t] lists the tiles (a - 1, c), (a + 1, c), (a, c - 1), (a, c + 1) and (a + 1, c - 1) of tile t = (a, c), or -1 where no such tile exists. `tile_owner`: each tile has its own slot; slots d * 3 to d * 3 + 2 belong to index d of level. Every index holds 1 to 3 tiles, the busiest exactly 3, with consecutive tile numbers in its first slots in order. Slots that hold no tile are ignored.
All inputs are finite; a program needn't handle non-finite values.
Results may differ from a plain program's by a relative error of at most 0.0001.
Values sent between devices are 32-bit elements; how exact they have to be, the bound alone decides.
No kernel may reach another device: no remote copies, remote signals or barrier semaphores. Data moves between devices by JAX's collectives and lax.ppermute only.
A program may use at most 128 MiB of HBM per device.

v0:
```python
import jax
import jax.numpy as jnp
from jax import lax
from jax.sharding import PartitionSpec as P

BATCH = 16
SOURCES = 3


PRECISE = lax.Precision.HIGHEST


def from_partner(x, axis, bit):
    return lax.ppermute(x, axis, [(i, i ^ 1 << bit) for i in range(lax.axis_size(axis))])


def phase_tables(phase_rates, batch_rates):
    phases = phase_rates.shape[0]
    unit_matrix = jnp.eye(phases, dtype=phase_rates.dtype)
    moving = phase_rates * (1.0 - unit_matrix)
    leaving = jnp.sum(moving, axis=1) + jnp.sum(batch_rates, axis=(0, 2))
    stacked = jnp.concatenate(
        [(moving - unit_matrix * leaving[:, None])[None], batch_rates], axis=0
    )
    return (stacked, jnp.max(leaving))


def uniform_rate(top_leaving, service_rates, source_rates):
    sources_top = jnp.sum(jnp.maximum(source_rates[:, 2] + source_rates[:, 1], source_rates[:, 0]))
    return top_leaving + service_rates[0] + service_rates[1] + sources_top


def source_terms(states, source_rates):
    powers = jnp.cumprod(jnp.full((SOURCES,), 2, jnp.int32)) // 2
    on_bits = (states[:, None] // powers[None, :] % 2).astype(source_rates.dtype)
    turn_on = source_rates[:, 0][None, :]
    turn_off = source_rates[:, 1][None, :]
    arrive = source_rates[:, 2][None, :]
    feeding = jnp.sum(on_bits * arrive, axis=1)
    incoming = on_bits * turn_on + (1.0 - on_bits) * turn_off
    outgoing = jnp.sum(on_bits * turn_off + (1.0 - on_bits) * turn_on, axis=1)
    return (feeding, incoming, outgoing)


def table_rows(lookup_table, wanted):
    flattened = lookup_table.reshape(lookup_table.shape[0], -1)
    matches = wanted[:, None] == jnp.arange(lookup_table.shape[0], dtype=jnp.int32)[None, :]
    picked = jnp.sum(jnp.where(matches[:, :, None], flattened[None, :, :], 0), axis=1)
    return picked.reshape(wanted.shape + lookup_table.shape[1:])


def edge_parts(tile_block, lower_row, upper_row, rim_depth):
    top_part = tile_block[..., tile_block.shape[-1] - rim_depth :]
    top_part = top_part.reshape(tile_block.shape[:3] + (tile_block.shape[3] * rim_depth,))
    bottom_part = jnp.concatenate([lower_row[..., 0][..., None], tile_block[..., 0]], axis=-1)
    return (top_part, bottom_part, lower_row, upper_row, lower_row[..., 0])


def pick_rows(wanted, pieces):
    row_count = pieces.shape[0]
    matches = (wanted[:, None] == jnp.arange(row_count, dtype=jnp.int32)[None, :]).astype(
        pieces.dtype
    )
    flattened = pieces.reshape(row_count, -1)
    picked = jnp.dot(matches, flattened, precision=PRECISE)
    return picked.reshape((wanted.shape[0],) + pieces.shape[1:])


def body(
    state_values,
    phase_rates,
    batch_rates,
    service_rates,
    source_rates,
    tile_levels,
    routes,
    tile_owner,
):
    slot_count, local_states, local_phases, width_two, width_one = state_values.shape
    src_rank = lax.axis_index("src")
    tables, top_leaving = phase_tables(phase_rates, batch_rates)
    uniform = uniform_rate(top_leaving, service_rates, source_rates)
    phase_start = lax.axis_index("phase") * local_phases
    tables_local = lax.dynamic_slice_in_dim(tables, phase_start, local_phases, 2)
    current = state_values
    states = src_rank * local_states + jnp.arange(local_states, dtype=jnp.int32)
    row_ids = jnp.arange(width_two, dtype=jnp.int32)
    block_states = current.shape[1]
    local_bits = block_states.bit_length() - 1
    feeding, incoming, outgoing = source_terms(states, source_rates)
    holders = lax.axis_index("level") * slot_count + jnp.arange(slot_count, dtype=jnp.int32)
    owned_here = tile_owner[None, :] == holders[:, None]
    filled = jnp.any(owned_here, axis=1)
    tile_ids = jnp.arange(tile_owner.shape[0], dtype=jnp.int32)
    my_tiles = jnp.sum(jnp.where(owned_here, tile_ids[None, :], 0), axis=1)
    my_routes = table_rows(routes, my_tiles)
    my_levels = table_rows(tile_levels, my_tiles)
    route_slots = table_rows(tile_owner, jnp.maximum(my_routes, 0).reshape(-1)).reshape(
        my_routes.shape
    )
    wanted = jnp.where((my_routes >= 0) & filled[:, None], route_slots, -1)
    first_pos = my_levels[:, 0:1] * width_one + jnp.arange(width_one, dtype=jnp.int32)[None, :] > 0
    second_pos = my_levels[:, 1:2] * width_two + row_ids[None, :] > 0
    leaving_rate = (
        service_rates[0] * first_pos[:, None, None, None, :]
        + service_rates[1] * second_pos[:, None, None, :, None]
        + (feeding + outgoing)[None, :, None, None, None]
    )
    for repeat in range(2):
        lower_row = current[..., -1, :]
        upper_row = current[..., 0, :]
        edge_sets = edge_parts(current, lower_row, upper_row, BATCH)
        pieces = (
            lax.all_gather(edge_sets[0], "level", axis=0, tiled=True),
            lax.all_gather(edge_sets[1], "level", axis=0, tiled=True),
            lax.all_gather(edge_sets[2], "level", axis=0, tiled=True),
            lax.all_gather(edge_sets[3], "level", axis=0, tiled=True),
            lax.all_gather(edge_sets[4], "level", axis=0, tiled=True),
        )
        picked = tuple((pick_rows(wanted[:, index], pieces[index]) for index in range(5)))
        full_values = lax.all_gather(current, "phase", axis=2, tiled=True)
        top_full = lax.all_gather(picked[0], "phase", axis=2, tiled=True)
        above_ext = picked[1]
        left_last = picked[2]
        right_first = picked[3]
        corner_cell = picked[4]
        above_bottom = above_ext[..., 1:]
        top_full = top_full.reshape(full_values.shape[:4] + (BATCH,))
        extended = jnp.concatenate([top_full, full_values], axis=-1)
        change = jnp.zeros(current.shape, jnp.float32)
        for offset in range(BATCH + 1):
            window = extended[..., BATCH - offset : BATCH - offset + width_one]
            change = change + jnp.einsum(
                "cspuv,pq->csquv", window, tables_local[offset], precision=PRECISE
            )
        row_ext = jnp.concatenate([current, above_bottom[..., None]], axis=-1)
        side_ext = jnp.concatenate([left_last, corner_cell[..., None]], axis=-1)
        joined = jnp.concatenate([side_ext[..., None, :], row_ext], axis=-2)
        service_one = joined[..., :width_two, 1:]
        service_two = jnp.concatenate([current, right_first[..., None, :]], axis=-2)[..., 1:, :]
        feed_two = jnp.concatenate([left_last[..., None, :], current], axis=-2)[..., :width_two, :]
        for source_bit in range(SOURCES):
            if source_bit < local_bits:
                stride = 2**source_bit
                shaped = current.reshape(
                    (slot_count, block_states // (2 * stride), 2, stride) + current.shape[2:]
                )
                partner = jnp.flip(shaped, axis=2).reshape(current.shape)
            else:
                partner = from_partner(current, "src", source_bit - local_bits)
            change = change + incoming[:, source_bit][None, :, None, None, None] * partner
        change = (
            change
            + service_rates[0] * service_one
            + service_rates[1] * service_two
            + feeding[None, :, None, None, None] * feed_two
            - leaving_rate * current
        )
        stepped = current + change / uniform
        current = jnp.where(filled[:, None, None, None, None], stepped, 0.0)
    return current


def solution(mesh):
    placed = (
        P(("groups", "level"), "src", "phase", None, None),
        P("groups", None),
        P("groups", None, None),
        P("groups"),
        P("groups", None),
        P("groups", None),
        P("groups", None),
        P("groups"),
    )
    return jax.shard_map(
        body,
        mesh=mesh,
        in_specs=placed,
        out_specs=P(("groups", "level"), "src", "phase", None, None),
        check_vma=False,
    )
```

profile of v0, /device:TPU:0, one launch (start us, length us, event | category | flops | bytes accessed | tf_op | source)
XLA Modules:
  0.0 388.2 jit_solution(14093897819066521582)
XLA Ops:
  19.1 13.4 %all-gather.1 = f32[12,4,16,1]{2,1,3,0:T(4,128)S(1)} all-gather(f32[3,4,16,1]{2,1,3,0:T(4,128)S(1)} %copy.212), channel_id=3, replica_groups=mesh['groups'=2,'level'=4,'src'=2,'phase'=2] {'level'}, dimensions={0}, use_global_device_ids=true | all-gather | bytes 3840 | tf_op jit(solution)/shard_map/all_gather | solution.py:118
  35.0 15.1 %all_gather.47 = f32[12,4,16,17]{3,2,1,0:T(8,128)S(1)} all-gather(f32[3,4,16,17]{3,2,1,0:T(8,128)S(1)} %pad_maximum_fusion.14), channel_id=1, replica_groups=mesh['groups'=2,'level'=4,'src'=2,'phase'=2] {'level'}, dimensions={0}, use_global_device_ids=true | all-gather | bytes 65280 | tf_op jit(solution)/shard_map/all_gather | solution.py:115
  54.1 15.5 %all-gather = f32[12,4,16,1,128]{4,2,3,1,0:T(8,128)S(1)} all-gather(f32[3,4,16,1,128]{4,2,3,1,0:T(8,128)} %bitcast.368), channel_id=2, replica_groups=mesh['groups'=2,'level'=4,'src'=2,'phase'=2] {'level'}, dimensions={0}, use_global_device_ids=true | all-gather | bytes 491520 | tf_op jit(solution)/shard_map/all_gather | solution.py:116
  70.9 15.5 %all-gather.2 = f32[12,4,16,1,128]{4,2,3,1,0:T(8,128)} all-gather(f32[3,4,16,1,128]{4,2,3,1,0:T(8,128)S(1)} %copy-done.12), channel_id=4, replica_groups=mesh['groups'=2,'level'=4,'src'=2,'phase'=2] {'level'}, dimensions={0}, use_global_device_ids=true | all-gather | bytes 491520 | tf_op jit(solution)/shard_map/all_gather | solution.py:117
  87.7 16.2 %all_gather.43 = f32[12,4,16,256]{3,2,1,0:T(8,128)S(1)} all-gather(f32[3,4,16,256]{3,2,1,0:T(8,128)} %reshape.284), channel_id=1, replica_groups=mesh['groups'=2,'level'=4,'src'=2,'phase'=2] {'level'}, dimensions={0}, use_global_device_ids=true | all-gather | bytes 983040 | tf_op jit(solution)/shard_map/all_gather | solution.py:114
  132.2 6.1 %fusion.49 = f32[16,3,4,16,128]{4,0,3,2,1:T(8,128)} fusion(f32[3,4,32,16,16]{4,2,3,1,0:T(8,128)S(1)} %copy.206, f32[3,4,32,16,128]{4,2,3,1,0:T(8,128)} %all-gather.9.cloned.1.call-done, f32[17,32,16]{1,2,0:T(8,128)S(1)} %fusion.128), kind=kOutput, calls=%fused_computation.93 | convolution fusion | flops 151781376 | bytes 7872512 | tf_op jit(solution)/shard_map/cspuv,pq->csquv/dot_general | solution.py:133
  138.3 4.1 %fusion.52 = f32[16,3,4,16,128]{4,0,3,2,1:T(8,128)} fusion(f32[3,4,32,16,16]{4,2,3,1,0:T(8,128)S(1)} %copy.206, f32[3,4,32,16,128]{4,2,3,1,0:T(8,128)S(1)} %copy-done, f32[17,32,16]{1,2,0:T(8,128)S(1)} %fusion.128), kind=kOutput, calls=%fused_computation.95 | convolution fusion | flops 151781376 | bytes 7872512 | tf_op jit(solution)/shard_map/cspuv,pq->csquv/dot_general | solution.py:133
  142.3 4.0 %fusion.55 = f32[16,3,4,16,128]{4,0,3,2,1:T(8,128)} fusion(f32[3,4,32,16,16]{4,2,3,1,0:T(8,128)S(1)} %copy.206, f32[3,4,32,16,128]{4,2,3,1,0:T(8,128)S(1)} %copy-done, f32[17,32,16]{1,2,0:T(8,128)S(1)} %fusion.128), kind=kOutput, calls=%fused_computation.97 | convolution fusion | flops 151781376 | bytes 7872512 | tf_op jit(solution)/shard_map/cspuv,pq->csquv/dot_general | solution.py:133
  146.3 4.3 %fusion.58 = f32[16,3,4,16,128]{4,0,3,2,1:T(8,128)} fusion(f32[3,4,32,16,16]{4,2,3,1,0:T(8,128)S(1)} %copy.206, f32[3,4,32,16,128]{4,2,3,1,0:T(8,128)S(1)} %copy-done, f32[17,32,16]{1,2,0:T(8,128)S(1)} %fusion.128), kind=kOutput, calls=%fused_computation.99 | convolution fusion | flops 151781376 | bytes 7872512 | tf_op jit(solution)/shard_map/cspuv,pq->csquv/dot_general | solution.py:133
  150.7 4.0 %fusion.61 = f32[16,3,4,16,128]{4,0,3,2,1:T(8,128)} fusion(f32[3,4,32,16,16]{4,2,3,1,0:T(8,128)S(1)} %copy.206, f32[3,4,32,16,128]{4,2,3,1,0:T(8,128)S(1)} %copy-done, f32[17,32,16]{1,2,0:T(8,128)S(1)} %fusion.128), kind=kOutput, calls=%fused_computation.101 | convolution fusion | flops 151781376 | bytes 7872512 | tf_op jit(solution)/shard_map/cspuv,pq->csquv/dot_general | solution.py:133
  154.7 4.1 %fusion.64 = f32[16,3,4,16,128]{4,0,3,2,1:T(8,128)} fusion(f32[3,4,32,16,16]{4,2,3,1,0:T(8,128)S(1)} %copy.206, f32[3,4,32,16,128]{4,2,3,1,0:T(8,128)S(1)} %copy-done, f32[17,32,16]{1,2,0:T(8,128)S(1)} %fusion.128), kind=kOutput, calls=%fused_computation.103 | convolution fusion | flops 151781376 | bytes 7872512 | tf_op jit(solution)/shard_map/cspuv,pq->csquv/dot_general | solution.py:133
  158.7 4.0 %fusion.67 = f32[16,3,4,16,128]{4,0,3,2,1:T(8,128)} fusion(f32[3,4,32,16,16]{4,2,3,1,0:T(8,128)S(1)} %copy.206, f32[3,4,32,16,128]{4,2,3,1,0:T(8,128)S(1)} %copy-done, f32[17,32,16]{1,2,0:T(8,128)S(1)} %fusion.128), kind=kOutput, calls=%fused_computation.105 | convolution fusion | flops 151781376 | bytes 7872512 | tf_op jit(solution)/shard_map/cspuv,pq->csquv/dot_general | solution.py:133
  162.7 4.4 %fusion.70 = f32[16,3,4,16,128]{4,0,3,2,1:T(8,128)} fusion(f32[3,4,32,16,16]{4,2,3,1,0:T(8,128)S(1)} %copy.206, f32[3,4,32,16,128]{4,2,3,1,0:T(8,128)S(1)} %copy-done, f32[17,32,16]{1,2,0:T(8,128)S(1)} %fusion.128), kind=kOutput, calls=%fused_computation.107 | convolution fusion | flops 151781376 | bytes 7872512 | tf_op jit(solution)/shard_map/cspuv,pq->csquv/dot_general | solution.py:133
  167.2 4.0 %fusion.73 = f32[16,3,4,16,128]{4,0,3,2,1:T(8,128)} fusion(f32[3,4,32,16,16]{4,2,3,1,0:T(8,128)S(1)} %copy.206, f32[3,4,32,16,128]{4,2,3,1,0:T(8,128)S(1)} %copy-done, f32[17,32,16]{1,2,0:T(8,128)S(1)} %fusion.128), kind=kOutput, calls=%fused_computation.109 | convolution fusion | flops 151781376 | bytes 7872512 | tf_op jit(solution)/shard_map/cspuv,pq->csquv/dot_general | solution.py:133
  171.2 4.0 %fusion.76 = f32[16,3,4,16,128]{4,0,3,2,1:T(8,128)} fusion(f32[3,4,32,16,16]{4,2,3,1,0:T(8,128)S(1)} %copy.206, f32[3,4,32,16,128]{4,2,3,1,0:T(8,128)S(1)} %copy-done, f32[17,32,16]{1,2,0:T(8,128)S(1)} %fusion.128), kind=kOutput, calls=%fused_computation.111 | convolution fusion | flops 151781376 | bytes 7872512 | tf_op jit(solution)/shard_map/cspuv,pq->csquv/dot_general | solution.py:133
  175.2 4.0 %fusion.79 = f32[16,3,4,16,128]{4,0,3,2,1:T(8,128)} fusion(f32[3,4,32,16,16]{4,2,3,1,0:T(8,128)S(1)} %copy.206, f32[3,4,32,16,128]{4,2,3,1,0:T(8,128)S(1)} %copy-done, f32[17,32,16]{1,2,0:T(8,128)S(1)} %fusion.128), kind=kOutput, calls=%fused_computation.113 | convolution fusion | flops 151781376 | bytes 7872512 | tf_op jit(solution)/shard_map/cspuv,pq->csquv/dot_general | solution.py:133
  179.2 4.0 %fusion.82 = f32[16,3,4,16,128]{4,0,3,2,1:T(8,128)} fusion(f32[3,4,32,16,16]{4,2,3,1,0:T(8,128)S(1)} %copy.206, f32[3,4,32,16,128]{4,2,3,1,0:T(8,128)S(1)} %copy-done, f32[17,32,16]{1,2,0:T(8,128)S(1)} %fusion.128), kind=kOutput, calls=%fused_computation.115 | convolution fusion | flops 151781376 | bytes 7872512 | tf_op jit(solution)/shard_map/cspuv,pq->csquv/dot_general | solution.py:133
  183.2 4.2 %fusion.85 = f32[16,3,4,16,128]{4,0,3,2,1:T(8,128)} fusion(f32[3,4,32,16,16]{4,2,3,1,0:T(8,128)S(1)} %copy.206, f32[3,4,32,16,128]{4,2,3,1,0:T(8,128)S(1)} %copy-done, f32[17,32,16]{1,2,0:T(8,128)S(1)} %fusion.128), kind=kOutput, calls=%fused_computation.117 | convolution fusion | flops 151781376 | bytes 7872512 | tf_op jit(solution)/shard_map/cspuv,pq->csquv/dot_general | solution.py:133
  187.4 4.0 %fusion.88 = f32[16,3,4,16,128]{4,0,3,2,1:T(8,128)} fusion(f32[3,4,32,16,16]{4,2,3,1,0:T(8,128)S(1)} %copy.206, f32[3,4,32,16,128]{4,2,3,1,0:T(8,128)S(1)} %copy-done, f32[17,32,16]{1,2,0:T(8,128)S(1)} %fusion.128), kind=kOutput, calls=%fused_computation.119 | convolution fusion | flops 151781376 | bytes 7872512 | tf_op jit(solution)/shard_map/cspuv,pq->csquv/dot_general | solution.py:133
  191.4 4.0 %fusion.46 = f32[16,3,4,16,128]{4,0,3,2,1:T(8,128)} fusion(f32[3,4,32,16,16]{4,2,3,1,0:T(8,128)S(1)} %copy.206, f32[3,4,32,16,128]{4,2,3,1,0:T(8,128)S(1)} %copy-done, f32[17,32,16]{1,2,0:T(8,128)S(1)} %fusion.128), kind=kOutput, calls=%fused_computation.91 | convolution fusion | flops 151781376 | bytes 7872512 | tf_op jit(solution)/shard_map/cspuv,pq->csquv/dot_general | solution.py:133
  198.2 15.3 %fusion.109 = f32[3,4,16,16,128]{4,2,3,1,0:T(8,128)} fusion(f32[3,4,16,16,128]{4,2,3,1,0:T(8,128)S(1)} %copy-done.3, f32[3,4,16,1,128]{4,2,3,1,0:T(8,128)S(1)} %bitcast.372, f32[3,4,16,1,128]{4,2,3,1,0:T(8,128)} %bitcast.377, f32[3,4,16,1,129]{4,2,3,1,0:T(8,128)} %maximum_bitcast_fusion, f32[3,4,16,16,1]{4,2,3,1,0:T(8,128)} %copy.220, ...), kind=kOutput, calls=%fused_computation.146 | convolution fusion | flops 166330368 | bytes 39738636 | tf_op jit(solution)/shard_map/cspuv,pq->csquv/dot_general | solution.py:133
  219.7 13.2 %all-gather.4 = f32[12,4,16,1]{2,1,3,0:T(4,128)S(1)} all-gather(f32[3,4,16,1]{2,1,3,0:T(4,128)S(1)} %copy.232), channel_id=6, replica_groups=mesh['groups'=2,'level'=4,'src'=2,'phase'=2] {'level'}, dimensions={0}, use_global_device_ids=true | all-gather | bytes 3840 | tf_op jit(solution)/shard_map/all_gather | solution.py:118
  234.2 15.1 %all_gather.54 = f32[12,4,16,17]{3,2,1,0:T(8,128)S(1)} all-gather(f32[3,4,16,17]{3,2,1,0:T(8,128)S(1)} %pad_maximum_fusion.15), channel_id=1, replica_groups=mesh['groups'=2,'level'=4,'src'=2,'phase'=2] {'level'}, dimensions={0}, use_global_device_ids=true | all-gather | bytes 65280 | tf_op jit(solution)/shard_map/all_gather | solution.py:115
  250.1 15.2 %all-gather.5 = f32[12,4,16,1,128]{4,2,3,1,0:T(8,128)S(1)} all-gather(f32[3,4,16,1,128]{4,2,3,1,0:T(8,128)S(1)} %get-tuple-element.15), channel_id=7, replica_groups=mesh['groups'=2,'level'=4,'src'=2,'phase'=2] {'level'}, dimensions={0}, use_global_device_ids=true | all-gather | bytes 491520 | tf_op jit(solution)/shard_map/all_gather | solution.py:117
  266.5 14.3 %all-gather.3 = f32[12,4,16,1,128]{4,2,3,1,0:T(8,128)S(1)} all-gather(f32[3,4,16,1,128]{4,2,3,1,0:T(8,128)S(1)} %get-tuple-element.16), channel_id=5, replica_groups=mesh['groups'=2,'level'=4,'src'=2,'phase'=2] {'level'}, dimensions={0}, use_global_device_ids=true | all-gather | bytes 491520 | tf_op jit(solution)/shard_map/all_gather | solution.py:116
  290.9 15.8 %all_gather.50 = f32[12,4,16,256]{3,2,1,0:T(8,128)S(1)} all-gather(f32[3,4,16,256]{3,2,1,0:T(8,128)S(1)} %reshape.298), channel_id=1, replica_groups=mesh['groups'=2,'level'=4,'src'=2,'phase'=2] {'level'}, dimensions={0}, use_global_device_ids=true | all-gather | bytes 983040 | tf_op jit(solution)/shard_map/all_gather | solution.py:114
  315.6 4.9 %fusion.4 = f32[16,3,4,16,128]{4,0,3,2,1:T(8,128)S(1)} fusion(f32[3,4,32,16,16]{4,2,3,1,0:T(8,128)S(1)} %copy.231, f32[3,4,32,16,128]{4,2,3,1,0:T(8,128)} %all-gather.11.cloned.1.call-done, f32[17,32,16]{1,2,0:T(8,128)S(1)} %fusion.128), kind=kOutput, calls=%fused_computation.63 | convolution fusion | flops 151781376 | bytes 7872512 | tf_op jit(solution)/shard_map/cspuv,pq->csquv/dot_general | solution.py:133
  352.8 4.2 %fusion.40 = f32[16,3,4,16,128]{4,0,3,2,1:T(8,128)} fusion(f32[3,4,32,16,16]{4,2,3,1,0:T(8,128)S(1)} %copy.231, f32[3,4,32,16,128]{4,2,3,1,0:T(8,128)S(1)} %copy-done.1, f32[17,32,16]{1,2,0:T(8,128)S(1)} %fusion.128), kind=kOutput, calls=%fused_computation.87 | convolution fusion | flops 151781376 | bytes 7872512 | tf_op jit(solution)/shard_map/cspuv,pq->csquv/dot_general | solution.py:133
  357.1 4.0 %fusion.43 = f32[16,3,4,16,128]{4,0,3,2,1:T(8,128)} fusion(f32[3,4,32,16,16]{4,2,3,1,0:T(8,128)S(1)} %copy.231, f32[3,4,32,16,128]{4,2,3,1,0:T(8,128)S(1)} %copy-done.1, f32[17,32,16]{1,2,0:T(8,128)S(1)} %fusion.128), kind=kOutput, calls=%fused_computation.89 | convolution fusion | flops 151781376 | bytes 7872512 | tf_op jit(solution)/shard_map/cspuv,pq->csquv/dot_general | solution.py:133
  361.1 3.3 fusion.90
  364.4 4.0 %fusion.1 = f32[16,3,4,16,128]{4,0,3,2,1:T(8,128)} fusion(f32[3,4,32,16,16]{4,2,3,1,0:T(8,128)S(1)} %copy.231, f32[3,4,32,16,128]{4,2,3,1,0:T(8,128)S(1)} %copy-done.1, f32[17,32,16]{1,2,0:T(8,128)S(1)} %fusion.128), kind=kOutput, calls=%fused_computation.61 | convolution fusion | flops 151781376 | bytes 7872512 | tf_op jit(solution)/shard_map/cspuv,pq->csquv/dot_general | solution.py:133
  370.8 8.7 %fusion.99 = f32[3,4,16,16,128]{4,2,3,1,0:T(8,128)S(1)} fusion(f32[3,4,16,16,128]{4,2,3,1,0:T(8,128)} %fusion.109, f32[3,4,16,1,128]{4,2,3,1,0:T(8,128)S(1)} %bitcast.374, f32[3,4,16,1,128]{4,2,3,1,0:T(8,128)} %bitcast.378, f32[3,4,16,1,129]{4,2,3,1,0:T(8,128)} %maximum_bitcast_fusion.1, f32[3,4,16,16,1]{4,2,3,1,0:T(8,128)S(1)} %copy-done.6, ...), kind=kLoop, calls=%fused_computation.132 | loop fusion | flops 14548992 | bytes 35009360 | tf_op jit(solution)/shard_map/jit(_where)/select_n | solution.py:160
  (186 shorter events, 114.3 us)
Async XLA Ops:
  6.5 6.7 %copy-start.2 = (f32[3,4,16,16,128]{4,3,2,1,0:T(8,128)S(1)}, f32[3,4,16,16,128]{4,3,2,1,0:T(8,128)}, u32[]{:S(2)}) copy-start(f32[3,4,16,16,128]{4,3,2,1,0:T(8,128)} %param.8) | copy-start | bytes 4718596
  6.5 6.3 %copy-start.32 = (s32[8]{0:T(128)S(1)}, s32[8]{0:T(128)}, u32[]{:S(2)}) copy-start(s32[8]{0:T(128)} %param.15) | copy-start | bytes 100
  6.5 125.6 %all-gather.9.cloned.1.call-start = ((), (), s32[]{:S(2)}) async-start(), calls=%async_computation | async-start | bytes 4718592 | tf_op jit(solution)/shard_map/all_gather | solution.py:121
  9.7 5.7 %copy-start.10 = (f32[16,32,32]{2,1,0:T(8,128)S(1)}, f32[16,32,32]{2,1,0:T(8,128)}, u32[]{:S(2)}) copy-start(f32[16,32,32]{2,1,0:T(8,128)} %param.10) | copy-start | bytes 196612
  9.7 7.3 %copy-start.23 = (s32[8,5]{1,0:T(8,128)S(1)}, s32[8,5]{1,0:T(8,128)}, u32[]{:S(2)}) copy-start(s32[8,5]{1,0:T(8,128)} %param.14) | copy-start | bytes 484
  9.7 8.5 %copy-start.15 = (f32[32,32]{1,0:T(8,128)S(1)}, f32[32,32]{1,0:T(8,128)}, u32[]{:S(2)}) copy-start(f32[32,32]{1,0:T(8,128)} %param.9) | copy-start | bytes 12292
  9.7 305.9 %all-gather.11.cloned.1.call-start = ((), (), s32[]{:S(2)}) async-start(), calls=%async_computation.1 | async-start | bytes 4718592 | tf_op jit(solution)/shard_map/all_gather | solution.py:121
  9.8 188.4 %collective-permute-start = (f32[3,4,16,16,128]{4,2,3,1,0:T(8,128)}, f32[3,4,16,16,128]{4,2,3,1,0:T(8,128)}, u32[]{:S(2)}, u32[]{:S(2)}) collective-permute-start(f32[3,4,16,16,128]{4,2,3,1,0:T(8,128)} %copy.227), channel_id=1, source_target_pairs={{0,2},{2,0},{1,3},{3,1},{4,6},{6,4},{5,7},{7,5},{8,10},{10,8},{9,1... | collective-permute-start | bytes 4718600 | tf_op jit(solution)/shard_map/ppermute | solution.py:14
  13.3 21.6 %copy-start.7 = (f32[3,4,16,1,128]{4,3,2,1,0:T(1,128)}, f32[3,4,16,1,128]{4,3,2,1,0:T(1,128)S(1)}, u32[]{:S(2)}) copy-start(f32[3,4,16,1,128]{4,3,2,1,0:T(1,128)S(1)} %slice.324) | copy-start | bytes 294916
  15.4 19.4 %copy-start.25 = (pred[3,8]{1,0:T(4,128)(4,1)}, pred[3,8]{1,0:T(4,128)(4,1)S(1)}, u32[]{:S(2)}) copy-start(pred[3,8]{1,0:T(4,128)(4,1)S(1)} %iota_compare_fusion.9) | copy-start | bytes 76
  18.2 16.6 %copy-start.29 = (s32[3]{0:T(128)}, s32[3]{0:T(128)S(1)}, u32[]{:S(2)}) copy-start(s32[3]{0:T(128)S(1)} %get-tuple-element.20) | copy-start | bytes 40
  18.2 51.7 %copy-start.20 = (s32[3]{0:T(128)}, s32[3]{0:T(128)S(1)}, u32[]{:S(2)}) copy-start(s32[3]{0:T(128)S(1)} %get-tuple-element.21) | copy-start | bytes 40
  18.2 87.2 %copy-start.16 = (s32[3]{0:T(128)}, s32[3]{0:T(128)S(1)}, u32[]{:S(2)}) copy-start(s32[3]{0:T(128)S(1)} %get-tuple-element.17) | copy-start | bytes 40
  18.2 88.8 %copy-start.18 = (s32[3]{0:T(128)}, s32[3]{0:T(128)S(1)}, u32[]{:S(2)}) copy-start(s32[3]{0:T(128)S(1)} %get-tuple-element.19) | copy-start | bytes 40
  52.9 18.0 %copy-start.12 = (f32[3,4,16,1,128]{4,2,3,1,0:T(8,128)S(1)}, f32[3,4,16,1,128]{4,2,3,1,0:T(8,128)}, u32[]{:S(2)}) copy-start(f32[3,4,16,1,128]{4,2,3,1,0:T(8,128)} %slice.415) | copy-start | bytes 294916
  116.5 4.1 %copy-start.14 = (f32[3,3]{1,0:T(4,128)S(1)}, f32[3,3]{1,0:T(4,128)}, u32[]{:S(2)}) copy-start(f32[3,3]{1,0:T(4,128)} %param.12) | copy-start | bytes 112
  116.5 4.3 %copy-start.31 = (s32[3]{0:T(128)S(1)}, s32[3]{0:T(128)}, u32[]{:S(2)}) copy-start(s32[3]{0:T(128)} %constant.114.clone.1) | copy-start | bytes 40
  116.5 5.7 %copy-start.27 = (f32[2]{0:T(128)S(1)}, f32[2]{0:T(128)}, u32[]{:S(2)}) copy-start(f32[2]{0:T(128)} %param.11) | copy-start | bytes 28
  116.5 6.4 %copy-start.13 = (f32[32,32]{0,1:T(8,128)S(1)}, f32[32,32]{0,1:T(8,128)}, u32[]{:S(2)}) copy-start(f32[32,32]{0,1:T(8,128)} %copy.198) | copy-start | bytes 12292
  116.5 6.4 %copy-start.24 = (f32[32]{0:T(128)S(1)}, f32[32]{0:T(128)}, u32[]{:S(2)}) copy-start(f32[32]{0:T(128)} %reduce_sum.82) | copy-start | bytes 388
  116.5 10.5 %copy-start.26 = (pred[3,8]{1,0:T(4,128)(4,1)S(1)}, pred[3,8]{1,0:T(4,128)(4,1)}, u32[]{:S(2)}) copy-start(pred[3,8]{1,0:T(4,128)(4,1)} %copy-done.25) | copy-start | bytes 76
  116.5 10.5 %copy-start.28 = (s32[8,2]{0,1:T(2,128)S(1)}, s32[8,2]{0,1:T(2,128)}, u32[]{:S(2)}) copy-start(s32[8,2]{0,1:T(2,128)} %param.13) | copy-start | bytes 196
  116.5 10.9 %copy-start.9 = (f32[16,32,32]{1,2,0:T(8,128)S(1)}, f32[16,32,32]{1,2,0:T(8,128)}, u32[]{:S(2)}) copy-start(f32[16,32,32]{1,2,0:T(8,128)} %copy.199) | copy-start | bytes 196612
  132.2 6.1 %copy-start = (f32[3,4,32,16,128]{4,2,3,1,0:T(8,128)S(1)}, f32[3,4,32,16,128]{4,2,3,1,0:T(8,128)}, u32[]{:S(2)}) copy-start(f32[3,4,32,16,128]{4,2,3,1,0:T(8,128)} %all-gather.9.cloned.1.call-done) | copy-start | bytes 9437188
  195.4 2.8 copy-start.11
  213.5 19.6 %copy-start.30 = (s32[3]{0:T(128)S(1)}, s32[3]{0:T(128)}, u32[]{:S(2)}) copy-start(s32[3]{0:T(128)} %copy-done.29) | copy-start | bytes 40
  215.4 49.9 %copy-start.22 = (s32[3]{0:T(128)S(1)}, s32[3]{0:T(128)}, u32[]{:S(2)}) copy-start(s32[3]{0:T(128)} %get-tuple-element.18) | copy-start | bytes 40
  215.4 154.7 %collective-permute-start.1 = (f32[3,4,16,16,128]{4,2,3,1,0:T(8,128)}, f32[3,4,16,16,128]{4,2,3,1,0:T(8,128)}, u32[]{:S(2)}, u32[]{:S(2)}) collective-permute-start(f32[3,4,16,16,128]{4,2,3,1,0:T(8,128)} %fusion.109), channel_id=1, source_target_pairs={{0,2},{2,0},{1,3},{3,1},{4,6},{6,4},{5,7},{7,5},{8,10},{10,8},{9,1... | collective-permute-start | bytes 4718600 | tf_op jit(solution)/shard_map/ppermute | solution.py:14
  234.1 47.1 %copy-start.21 = (s32[3]{0:T(128)S(1)}, s32[3]{0:T(128)}, u32[]{:S(2)}) copy-start(s32[3]{0:T(128)} %copy-done.20) | copy-start | bytes 40
  249.3 32.2 %copy-start.19 = (s32[3]{0:T(128)S(1)}, s32[3]{0:T(128)}, u32[]{:S(2)}) copy-start(s32[3]{0:T(128)} %copy-done.18) | copy-start | bytes 40
  289.7 17.0 %copy-start.17 = (s32[3]{0:T(128)S(1)}, s32[3]{0:T(128)}, u32[]{:S(2)}) copy-start(s32[3]{0:T(128)} %copy-done.16) | copy-start | bytes 40
  315.6 4.9 %copy-start.1 = (f32[3,4,32,16,128]{4,2,3,1,0:T(8,128)S(1)}, f32[3,4,32,16,128]{4,2,3,1,0:T(8,128)}, u32[]{:S(2)}) copy-start(f32[3,4,32,16,128]{4,2,3,1,0:T(8,128)} %all-gather.11.cloned.1.call-done) | copy-start | bytes 9437188
  (5 other events, 10.5 us)
Sparse Core Ops, SparseCore 0:
  9.9 14.8 all-gather.8
  213.6 12.5 all-gather.10
where the time goes:
time: 396 us; the launch traced here: 388 us
  blocking collectives  154 us (39%)
  matrix products  142 us (36%)
  local copies, waits for them, and re-layouts  52.6 us (13%)
  other arithmetic  19 us (5%)
  between operations  16.9 us (4%)
    dot_general x34, matrix products, body(): jnp.einsum('cspuv,pq->csquv', window, tables_local[offset], precision=PRE...  136 us
    all_gather x2, blocking collectives, body(): lax.all_gather(edge_sets[0], 'level', axis=0, tiled=True)  32 us
    all_gather x2, blocking collectives, body(): lax.all_gather(edge_sets[3], 'level', axis=0, tiled=True)  30.7 us
    all_gather x2, blocking collectives, body(): lax.all_gather(edge_sets[1], 'level', axis=0, tiled=True)  30.2 us
    all_gather x2, blocking collectives, body(): lax.all_gather(edge_sets[2], 'level', axis=0, tiled=True)  29.8 us
    all_gather x2, blocking collectives, body(): lax.all_gather(edge_sets[4], 'level', axis=0, tiled=True)  26.6 us
    select_n x1, other arithmetic, body(): current = jnp.where(filled[:, None, None, None, None], stepped, 0.0)  8.72 us
    unnamed x77, local copies, waits for them, and re-layouts  8.13 us
  transfers between devices with their start and end apart: 4, of which 0 were waited for; matrix products, arithmetic and copies ran while one was open for 47% of the time, Pallas kernels for 0%

commit v1 on v0

v1 whole, which is shorter than its diff:
```python
import functools

import jax
import jax.numpy as jnp
from jax import lax
from jax.experimental import pallas as pl
from jax.experimental.pallas import tpu as pltpu
from jax.sharding import PartitionSpec as P

BATCH = 16
SOURCES = 3
LANES = 128
F32 = jnp.float32
BF16 = jnp.bfloat16
VM = pltpu.VMEM
SM = pltpu.SMEM


def shift_from(x, axis, step):
    n = lax.axis_size(axis)
    return lax.ppermute(x, axis, [((i + step) % n, i) for i in range(n)])


def from_partner(x, axis, bit):
    return lax.ppermute(x, axis, [(i, i ^ 1 << bit) for i in range(lax.axis_size(axis))])


def batch_weights(phase_rates, batch_rates, service_rates, source_rates, phase_rank, local_phases):
    phases = phase_rates.shape[0]
    moving = phase_rates * (1.0 - jnp.eye(phases, dtype=F32))
    leaving = jnp.sum(moving, axis=1) + jnp.sum(batch_rates, axis=(0, 2))
    sources_top = jnp.sum(jnp.maximum(source_rates[:, 2] + source_rates[:, 1], source_rates[:, 0]))
    uniform = jnp.max(leaving) + service_rates[0] + service_rates[1] + sources_top
    inverse = 1.0 / uniform
    start = phase_rank * local_phases
    tables = jnp.concatenate([moving[None], batch_rates], axis=0) * inverse
    tables = lax.dynamic_slice_in_dim(tables, start, local_phases, 2)
    tables = jnp.concatenate([tables, tables], axis=1)
    tables = lax.dynamic_slice_in_dim(tables, start, phases, 1)
    tables = jnp.swapaxes(tables, 1, 2)
    rounded = lax.reduce_precision(tables, 8, 7)
    high, low = rounded.astype(BF16), (tables - rounded).astype(BF16)
    weights = jnp.concatenate([high, low, high], axis=2).reshape(-1, 3 * phases)
    exits = lax.dynamic_slice_in_dim(leaving, start, local_phases, 0) * inverse
    exits = jnp.broadcast_to(exits[:, None], (local_phases, LANES))
    return weights, exits, inverse.reshape(1)


class Shape:
    def __init__(self, block, tiles, levels):
        self.slots, self.states, self.phases, self.wide_two, self.wide_one = block
        self.tiles = tiles
        self.levels = levels
        self.rows = self.slots * self.states * self.phases * self.wide_two
        self.rim_group = LANES // BATCH
        self.rim_parts = self.wide_two // self.rim_group
        self.rim_rows = self.states * self.rim_parts * self.phases
        self.edge_rows = self.slots * self.states * self.phases
        self.lane_step = 2 * max(self.wide_two, BATCH)
        self.per_small = LANES // self.lane_step
        self.small_rows = -(-self.states // self.per_small) * self.phases
        self.message_rows = self.edge_rows + self.small_rows

    def native(self, slot, state, u):
        start = (slot * self.states + state) * self.phases * self.wide_two + u
        return pl.ds(start, self.phases, stride=self.wide_two)

    def by_level(self, slot, state, u):
        start = ((slot * self.states + state) * self.wide_two + u) * self.phases
        if not isinstance(start, int):
            start = pl.multiple_of(start, self.phases)
        return pl.ds(start, self.phases)

    def small_at(self, state):
        return (state // self.per_small) * self.phases, (state % self.per_small) * self.lane_step


def lane_ids(shape):
    return lax.broadcasted_iota(jnp.int32, shape, len(shape) - 1)


def tile_at(owner, slot, tiles):
    found = jnp.int32(-1)
    for t in range(tiles):
        found = jnp.where(owner[t] == slot, t, found)
    return found


def route_of(routes, owner, tile, direction, slots):
    known = jnp.maximum(tile, 0)
    target = jnp.where(tile >= 0, routes[known, direction], -1)
    slot = owner[jnp.maximum(target, 0)]
    device = lax.div(slot, jnp.int32(slots))
    return target >= 0, device, slot - device * slots


def pack_edges(sh, me, routes, owner, at, data, rim_out, edge_out):
    n, phases = sh.levels, sh.phases
    lane = lane_ids((phases, LANES))
    first = tile_at(owner, me * sh.slots, sh.tiles)
    count = jnp.int32(0)
    for k in range(sh.slots):
        count = count + jnp.where(tile_at(owner, me * sh.slots + k, sh.tiles) >= 0, 1, 0)
    last_slot = count - 1
    rims = []
    bottoms = [jnp.zeros((phases, LANES), F32) for _ in range(sh.small_rows // phases)]
    for s in range(sh.states):
        row, base = sh.small_at(s)
        for part in range(sh.rim_parts):
            packed = jnp.zeros((phases, LANES), F32)
            for q in range(sh.rim_group):
                u = part * sh.rim_group + q
                block = data[at(last_slot, s, u), :]
                moved = pltpu.roll(block, (q * BATCH - (sh.wide_one - BATCH)) % LANES, 1)
                packed = jnp.where(lax.div(lane, jnp.int32(BATCH)) == q, moved, packed)
            rims.append(packed)
        for u in range(sh.wide_two):
            moved = pltpu.roll(data[at(0, s, u), :], base + u, 1)
            i = row // phases
            bottoms[i] = jnp.where(lane == base + u, moved, bottoms[i])
    for step in range(1, n):
        there = lax.rem(me + step, jnp.int32(n))
        their_first = tile_at(owner, there * sh.slots, sh.tiles)
        lower = first < their_first
        found, device, _ = route_of(routes, owner, their_first, 0, sh.slots)
        wanted = jnp.where(jnp.logical_and(found, device == me), 1.0, 0.0).astype(F32)
        for i, packed in enumerate(rims):
            rim_out[step - 1, i * phases:(i + 1) * phases, :] = packed * wanted
        small = list(bottoms)
        for k in range(sh.slots):
            tile = tile_at(owner, there * sh.slots + k, sh.tiles)
            _, _, left = route_of(routes, owner, tile, 2, sh.slots)
            _, _, right = route_of(routes, owner, tile, 3, sh.slots)
            _, _, corner = route_of(routes, owner, tile, 4, sh.slots)
            slot = jnp.where(lower, left, right)
            u = jnp.where(lower, sh.wide_two - 1, 0)
            for s in range(sh.states):
                start = (k * sh.states + s) * phases
                edge_out[step - 1, start:start + phases, :] = data[at(slot, s, u), :]
                row, base = sh.small_at(s)
                i = row // phases
                place = base + sh.lane_step // 2 + k
                moved = pltpu.roll(data[at(corner, s, sh.wide_two - 1), :], place, 1)
                small[i] = jnp.where(lane == place, moved, small[i])
        for i, values in enumerate(small):
            start = sh.edge_rows + i * phases
            edge_out[step - 1, start:start + phases, :] = values


def pack_kernel(sh, at, routes, owner, data, rim_out, edge_out):
    pack_edges(sh, lax.axis_index("level"), routes, owner, at, data, rim_out, edge_out)


def source_scalars(sources, scale, state, bits):
    feed = jnp.float32(0.0)
    outflow = jnp.float32(0.0)
    inflow = []
    for k in range(SOURCES):
        on = lax.rem(lax.shift_right_logical(state, jnp.int32(k)), jnp.int32(2)) == 1
        turn_on, turn_off, arrive = sources[k, 0], sources[k, 1], sources[k, 2]
        feed = feed + jnp.where(on, arrive, 0.0)
        outflow = outflow + jnp.where(on, turn_off, turn_on)
        inflow.append(jnp.where(on, turn_on, turn_off) * scale)
    return feed * scale, outflow * scale, inflow


def product_kernel(sh, bits, cross, first, deferred, *refs):
    refs = list(refs)
    levels_t, routes, owner, service, sources, scale_ref = refs[:6]
    weights, exits = refs[6:8]
    refs = refs[8:]
    n, phases, half = sh.levels, sh.phases, sh.lane_step // 2
    own = refs.pop(0)
    other = refs.pop(0)
    rim_own = refs.pop(0)
    rim_other = refs.pop(0)
    edges = [refs.pop(0) for _ in range(n - 1)]
    partners = [refs.pop(0) for _ in range(cross)]
    start_values = refs.pop(0) if deferred and not first else None
    out = refs.pop(0)
    if first:
        sent = refs.pop(0) if deferred else None
        rim_out, edge_out = refs.pop(0), refs.pop(0)
    at = sh.native if first else sh.by_level
    at_out = sh.by_level if first else sh.native
    me = lax.axis_index("level")
    src_rank = lax.axis_index("src")
    scale = scale_ref[0]
    serve_one, serve_two = service[0] * scale, service[1] * scale
    lane = lane_ids((phases, LANES))
    group_lane = lax.rem(lane, jnp.int32(BATCH))

    def split(values):
        high = values.astype(BF16)
        low = (values - high.astype(F32)).astype(BF16)
        return jnp.concatenate([high, high, low], axis=0)

    def slot_state(index, carry):
        k = lax.div(index, jnp.int32(sh.states))
        s = index - k * sh.states
        tile = tile_at(owner, me * sh.slots + k, sh.tiles)
        known = jnp.maximum(tile, 0)
        a, c = levels_t[known, 0], levels_t[known, 1]
        routed = [route_of(routes, owner, tile, r, sh.slots) for r in range(5)]

        def remote(which, rows):
            found, device, slot = routed[which]
            value = jnp.zeros((phases, LANES), F32)
            for step in range(1, n):
                source = lax.rem(me + n - step, jnp.int32(n))
                take = jnp.logical_and(found, device == source)
                value = jnp.where(take, edges[step - 1][rows, :], value)
            return value

        def is_local(which):
            found, device, _ = routed[which]
            return jnp.logical_and(found, device == me)

        def local_slot(which):
            return jnp.minimum(routed[which][2], sh.slots - 1)

        edge_at = pl.ds(pl.multiple_of((k * sh.states + s) * phases, phases), phases)
        small_row = lax.div(s, jnp.int32(sh.per_small)) * phases
        small_base = lax.rem(s, jnp.int32(sh.per_small)) * sh.lane_step
        small_at = pl.ds(pl.multiple_of(sh.edge_rows + small_row, phases), phases)
        left_row = jnp.where(is_local(2), own[at(local_slot(2), s, sh.wide_two - 1), :], remote(2, edge_at))
        right_row = jnp.where(is_local(3), own[at(local_slot(3), s, 0), :], remote(3, edge_at))
        above_small = remote(1, small_at)
        above_local = is_local(1)
        corner_small = pltpu.roll(remote(4, small_at), LANES - (small_base + half + k), 1)
        corner = jnp.where(is_local(4), own[at(local_slot(4), s, sh.wide_two - 1), :], corner_small)

        state = src_rank * sh.states + s
        feed, outflow, inflow = source_scalars(sources, scale, state, bits)
        base_diag = 1.0 - feed - outflow
        diagonal = base_diag - exits[...]
        diagonal = diagonal - jnp.where(jnp.logical_or(lane > 0, a > 0), serve_one, 0.0)

        below_local = jnp.where(is_local(0), 1.0, 0.0).astype(F32)
        below_remote = jnp.where(jnp.logical_and(routed[0][0], jnp.logical_not(is_local(0))), 1.0, 0.0).astype(F32)
        rim_values = []
        for part in range(sh.rim_parts):
            halves = []
            start = pl.multiple_of((s * sh.rim_parts + part) * phases, phases)
            for values, received in ((own, rim_own), (other, rim_other)):
                packed = jnp.zeros((phases, LANES), F32)
                for q in range(sh.rim_group):
                    u = part * sh.rim_group + q
                    block = values[at(local_slot(0), s, u), :]
                    moved = pltpu.roll(block, (q * BATCH - (sh.wide_one - BATCH)) % LANES, 1)
                    packed = jnp.where(lax.div(lane, jnp.int32(BATCH)) == q, moved, packed)
                halves.append(packed * below_local + received[pl.ds(start, phases), :] * below_remote)
            product = jnp.dot(weights[...], split(jnp.concatenate(halves, axis=0)), preferred_element_type=F32)
            total = jnp.zeros((phases, LANES), F32)
            for b in range(1, BATCH + 1):
                moved = pltpu.roll(product[b * phases:(b + 1) * phases], (b - BATCH) % LANES, 1)
                total = total + jnp.where(group_lane < b, moved, 0.0)
            rim_values.append(total)

        if deferred:
            other_state = lax.bitwise_xor(state, jnp.int32(1 << bits))
            feed_there, outflow_there, _ = source_scalars(sources, scale, other_state, bits)
            feed_more = feed_there - feed
            diag_more = (feed + outflow) - (feed_there + outflow_there)
            if not first:
                there = source_scalars(sources, scale, other_state, bits)[2][bits]
                square = inflow[bits] * there

        for pair in range(sh.wide_two // 2):
            columns = []
            for u in (2 * pair, 2 * pair + 1):
                columns.append(split(jnp.concatenate([own[at(k, s, u), :], other[at(k, s, u), :]], axis=0)))
            product = jnp.dot(weights[...], jnp.concatenate(columns, axis=1), preferred_element_type=F32)
            for j, u in enumerate((2 * pair, 2 * pair + 1)):
                lanes = slice(j * LANES, (j + 1) * LANES)
                part, q = u // sh.rim_group, u % sh.rim_group
                total = product[0:phases, lanes]
                for b in range(1, BATCH + 1):
                    moved = pltpu.roll(product[b * phases:(b + 1) * phases, lanes], b, 1)
                    total = total + jnp.where(lane >= b, moved, 0.0)
                rim = rim_values[part]
                if q:
                    rim = pltpu.roll(rim, LANES - q * BATCH, 1)
                total = total + jnp.where(lane < BATCH, rim, 0.0)
                here = own[at(k, s, u), :]
                if u:
                    before = own[at(k, s, u - 1), :]
                    beyond = jnp.where(
                        above_local,
                        own[at(local_slot(1), s, u - 1), :],
                        pltpu.roll(above_small, LANES - (small_base + u - 1), 1),
                    )
                else:
                    before, beyond = left_row, corner
                after = own[at(k, s, u + 1), :] if u + 1 < sh.wide_two else right_row
                shifted = pltpu.roll(jnp.where(lane == 0, beyond, before), LANES - 1, 1)
                two = jnp.where(jnp.logical_or(u > 0, c > 0), serve_two, 0.0)
                total = total + (diagonal - two) * here
                total = total + serve_one * shifted + serve_two * after + feed * before
                for bit in range(bits):
                    flipped = lax.bitwise_xor(s, jnp.int32(1 << bit))
                    total = total + inflow[bit] * own[at(k, flipped, u), :]
                for bit, values in enumerate(partners):
                    total = total + inflow[bits + bit] * values[at(k, s, u), :]
                if deferred and not first:
                    total = total + square * start_values[sh.native(k, s, u), :]
                if not first:
                    total = jnp.where(tile >= 0, total, 0.0)
                out[at_out(k, s, u), :] = total
                if deferred and first:
                    sent[sh.native(k, s, u), :] = 2.0 * total + feed_more * before + diag_more * here
        return carry

    lax.fori_loop(0, sh.slots * sh.states, slot_state, 0)
    if first:
        pack_edges(sh, me, routes, owner, sh.by_level, out, rim_out, edge_out)


def join_kernel(sh, bits, owner, sources, scale_ref, stepped, received, out):
    me = lax.axis_index("level")
    src_rank = lax.axis_index("src")
    k = pl.program_id(0)
    filled = tile_at(owner, me * sh.slots + k, sh.tiles) >= 0
    inflow = source_scalars(sources, scale_ref[0], src_rank * sh.states, bits)[2][bits]
    out[...] = jnp.where(filled, stepped[...] + inflow * received[...], 0.0)


def body(
    state_values,
    phase_rates,
    batch_rates,
    service_rates,
    source_rates,
    tile_levels,
    routes,
    tile_owner,
):
    block = state_values.shape
    sh = Shape(block, tile_owner.shape[0], lax.axis_size("level"))
    bits = sh.states.bit_length() - 1
    cross = SOURCES - bits
    deferred = cross == 1
    n = sh.levels
    flat = state_values.reshape(sh.rows, LANES)
    weights, exits, scale = batch_weights(
        phase_rates, batch_rates, service_rates, source_rates, lax.axis_index("phase"), sh.phases
    )
    smem, vmem = pl.BlockSpec(memory_space=SM), pl.BlockSpec(memory_space=VM)
    rows_shape = jax.ShapeDtypeStruct((sh.rows, LANES), F32)
    edge_shapes = (
        jax.ShapeDtypeStruct((n - 1, sh.rim_rows, LANES), F32),
        jax.ShapeDtypeStruct((n - 1, sh.message_rows, LANES), F32),
    )
    rims, edges = pl.pallas_call(
        functools.partial(pack_kernel, sh, sh.native),
        out_shape=edge_shapes,
        in_specs=[smem, smem, vmem],
        out_specs=(vmem, vmem),
    )(routes, tile_owner, flat)

    def exchange(values, rims, edges):
        other = shift_from(values, "phase", 1)
        rim_got = sum(shift_from(rims[i], "level", -(i + 1)) for i in range(n - 1))
        rim_other = shift_from(rim_got, "phase", 1)
        edge_got = [shift_from(edges[i], "level", -(i + 1)) for i in range(n - 1)]
        return [values, other, rim_got, rim_other] + edge_got

    def product(first, inputs, extra):
        operands = [tile_levels, routes, tile_owner, service_rates, source_rates, scale, weights, exits] + inputs + extra
        shapes = [rows_shape]
        if first:
            shapes += ([rows_shape] if deferred else []) + list(edge_shapes)
        return pl.pallas_call(
            functools.partial(product_kernel, sh, bits, 0 if deferred else cross, first, deferred),
            out_shape=tuple(shapes),
            in_specs=[smem] * 6 + [vmem] * (len(operands) - 6),
            out_specs=tuple([vmem] * len(shapes)),
        )(*operands)

    extra = [] if deferred else [from_partner(flat, "src", bit) for bit in range(cross)]
    outs = product(True, exchange(flat, rims, edges), extra)
    if deferred:
        once, sent, rims, edges = outs
        received = from_partner(sent, "src", 0)
        (twice,) = product(False, exchange(once, rims, edges), [flat])
        tile_spec = pl.BlockSpec((sh.rows // sh.slots, LANES), lambda k: (k, 0))
        result = pl.pallas_call(
            functools.partial(join_kernel, sh, bits),
            grid=(sh.slots,),
            out_shape=rows_shape,
            in_specs=[smem, smem, smem, tile_spec, tile_spec],
            out_specs=tile_spec,
        )(tile_owner, source_rates, scale, twice, received)
    else:
        once, rims, edges = outs
        extra = [from_partner(once, "src", bit) for bit in range(cross)]
        (result,) = product(False, exchange(once, rims, edges), extra)
    return result.reshape(block)


def solution(mesh):
    placed = (
        P(("groups", "level"), "src", "phase", None, None),
        P("groups", None),
        P("groups", None, None),
        P("groups"),
        P("groups", None),
        P("groups", None),
        P("groups", None),
        P("groups"),
    )
    return jax.shard_map(
        body,
        mesh=mesh,
        in_specs=placed,
        out_specs=P(("groups", "level"), "src", "phase", None, None),
        check_vma=False,
    )
```

time: 396 us -> 99.7 us (0.25); the launches traced: 388 us -> 99.3 us
  blocking collectives: 154 us -> 0 us
  matrix products: 142 us -> 0 us
  Pallas kernels: 0 us -> 49 us
  local copies, waits for them, and re-layouts: 52.6 us -> 9.62 us
  waiting for transfers between devices: 0.05 us -> 18.3 us
  other arithmetic: 19 us -> 2.49 us
  between operations: 16.9 us -> 2.78 us
  starting transfers between devices: 3.67 us -> 17.1 us
    all_gather x12 -> x0, blocking collectives: 154 us -> none  [the longest x2 32 us: body(): lax.all_gather(edge_sets[0], 'level', axis=0, tiled=True)]
    dot_general x44 -> x0, matrix products: 142 us -> none  [the longest x34 136 us: body(): jnp.einsum('cspuv,pq->csquv', window, tables_local[offset], precision=PRE...]
    pallas_call x0 -> x4, Pallas kernels: none -> 49 us  [the longest x2 42.3 us: product(): pl.pallas_call(functools.partial(product_kernel, sh, bits, 0 if deferred...]
    ppermute x0 -> x16, waiting for transfers between devices: none -> 18.3 us  [shift_from(): return lax.ppermute(x, axis, [((i + step) % n, i) for i in range(n)])]
    ppermute x0 -> x16, starting transfers between devices: none -> 15.6 us  [shift_from(): return lax.ppermute(x, axis, [((i + step) % n, i) for i in range(n)])]
    reshape x10 -> x0, local copies, waits for them, and re-layouts: 9.07 us -> none  [the longest x2 4.88 us: body(): top_full = top_full.reshape(full_values.shape[:4] + (BATCH,))]
    slice x12 -> x1, local copies, waits for them, and re-layouts: 9.63 us -> 0.66 us  [batch_weights(): service_rates[1]]
    select_n x2 -> x0, other arithmetic: 8.73 us -> none  [the longest x1 8.72 us: body(): current = jnp.where(filled[:, None, None, None, None], stepped, 0.0)]
  transfers between devices with their start and end apart: 4 -> 17, of which waited for: 0 -> 4; matrix products, arithmetic and copies ran while one was open for 47% -> 8% of each run, Pallas kernels for 0% -> 24%
where the time goes in v1:
time: 99.7 us; the launch traced here: 99.3 us
  Pallas kernels  49 us (49%)
  waiting for transfers between devices  18.3 us (18%)
  starting transfers between devices  17.1 us (17%)
  local copies, waits for them, and re-layouts  9.62 us (10%)
  between operations  2.78 us (3%)
  other arithmetic  2.49 us (2%)
    pallas_call x2, Pallas kernels, product(): pl.pallas_call(functools.partial(product_kernel, sh, bits, 0 if deferred...  42.3 us
    ppermute x16, waiting for transfers between devices, shift_from(): return lax.ppermute(x, axis, [((i + step) % n, i) for i in range(n)])  18.3 us
    ppermute x16, starting transfers between devices, shift_from(): return lax.ppermute(x, axis, [((i + step) % n, i) for i in range(n)])  15.6 us
    unnamed x39, local copies, waits for them, and re-layouts  4.28 us
    pallas_call x1, Pallas kernels, body(): pl.pallas_call(functools.partial(join_kernel, sh, bits), grid=(sh.slots,)...  3.81 us
    pallas_call x1, Pallas kernels, body(): pl.pallas_call(functools.partial(pack_kernel, sh, sh.native), out_shape=e...  2.91 us
    squeeze x2, local copies, waits for them, and re-layouts, exchange(): edge_got = [shift_from(edges[i], 'level', -(i + 1)) for i in range(n - 1)]  2.04 us
  transfers between devices with their start and end apart: 17, of which 4 were waited for; matrix products, arithmetic and copies ran while one was open for 8% of the time, Pallas kernels for 24%

profile of v1, /device:TPU:0, one launch (start us, length us, event | category | flops | bytes accessed | tf_op | source)
XLA Modules:
  0.0 99.3 jit_solution(11563443451782175790)
XLA Ops:
  0.0 0.6 collective-permute-start
  0.6 2.9 %shard_map.82 = (f32[3,128,128]{2,1,0:T(8,128)}, f32[3,208,128]{2,1,0:T(8,128)}) custom-call(s32[8,5]{1,0:T(8,128)} %refs_1_.3, s32[8]{0:T(128)} %owner.3, f32[3072,128]{1,0:T(8,128)} %bitcast.39), custom_call_target="tpu_custom_call" | custom-call | tf_op jit(solution)/shard_map/pallas_call | solution.py:354
  3.5 0.9 slice_bitcast_fusion.10
  4.4 3.7 %collective-permute-start.2 = (f32[128,128]{1,0:T(8,128)S(1)}, f32[128,128]{1,0:T(8,128)S(1)}, u32[]{:S(2)}, u32[]{:S(2)}) collective-permute-start(f32[128,128]{1,0:T(8,128)S(1)} %get-tuple-element.28), channel_id=1, source_target_pairs={{8,0},{12,4},{0,8},{4,12},{9,1},{13,5},{1,9},{5,13},{10,2},{14,6},... | collective-permute-start | bytes 196616 | tf_op jit(solution)/shard_map/ppermute | solution.py:21
  8.1 1.3 %collective-permute-start.3 = (f32[128,128]{1,0:T(8,128)S(1)}, f32[128,128]{1,0:T(8,128)S(1)}, u32[]{:S(2)}, u32[]{:S(2)}) collective-permute-start(f32[128,128]{1,0:T(8,128)S(1)} %get-tuple-element.29), channel_id=1, source_target_pairs={{4,0},{8,4},{12,8},{0,12},{5,1},{9,5},{13,9},{1,13},{6,2},{10,6},{... | collective-permute-start | bytes 196616 | tf_op jit(solution)/shard_map/ppermute | solution.py:21
  9.4 0.7 collective-permute-start.1
  10.1 1.0 %slice_bitcast_fusion.3 = (f32[208,128]{1,0:T(8,128)S(1)}, f32[208,128]{1,0:T(8,128)S(1)}, f32[208,128]{1,0:T(8,128)S(1)}) fusion(f32[3,208,128]{2,1,0:T(8,128)} %get-tuple-element.12), kind=kLoop, calls=%fused_computation.12 | loop fusion | bytes 638976 | tf_op jit(solution)/shard_map/squeeze | solution.py:365
  11.1 3.2 %collective-permute-start.7 = (f32[208,128]{1,0:T(8,128)S(1)}, f32[208,128]{1,0:T(8,128)S(1)}, u32[]{:S(2)}, u32[]{:S(2)}) collective-permute-start(f32[208,128]{1,0:T(8,128)S(1)} %get-tuple-element.22), channel_id=1, source_target_pairs={{4,0},{8,4},{12,8},{0,12},{5,1},{9,5},{13,9},{1,13},{6,2},{10,6},{... | collective-permute-start | bytes 319496 | tf_op jit(solution)/shard_map/ppermute | solution.py:21
  14.6 0.7 copy.15.refs_0_
  15.4 0.7 fusion.7
  16.0 0.6 fusion.6
  18.5 0.7 maximum_reduce_fusion
  20.1 0.7 pad_maximum_fusion
  20.9 0.6 collective-permute-start.5
  21.7 7.7 %collective-permute-done.6.refs_13_ = f32[208,128]{1,0:T(8,128)S(1)} collective-permute-done((f32[208,128]{1,0:T(8,128)S(1)}, f32[208,128]{1,0:T(8,128)S(1)}, u32[]{:S(2)}, u32[]{:S(2)}) %collective-permute-start.6) | collective-permute-done | bytes 106528 | tf_op jit(solution)/shard_map/ppermute | solution.py:21
  29.4 0.8 broadcast_in_dim.10.refs_7_
  30.6 21.8 %shard_map.83 = (f32[3072,128]{1,0:T(8,128)}, f32[3072,128]{1,0:T(8,128)}, f32[3,128,128]{2,1,0:T(8,128)}, f32[3,208,128]{2,1,0:T(8,128)}) custom-call(s32[8,2]{1,0:T(8,128)} %copy.15.refs_0_, s32[8,5]{1,0:T(8,128)} %refs_1_.3, s32[8]{0:T(128)} %owner.3, f32[2]{0:T(128)} %refs_3_.3, f32[3,3]{1,0:T(4,128)} %sources.1, f32[1]{0:T(128)} %bitcast.2.refs_5_.scale_ref, ...), custom_call_target="tpu_custom_call" | custom-call | tf_op jit(solution)/shard_map/pallas_call | solution.py:373
  52.4 1.5 %collective-permute-start.16 = (f32[3072,128]{1,0:T(8,128)}, f32[3072,128]{1,0:T(8,128)S(1)}, u32[]{:S(2)}, u32[]{:S(2)}) collective-permute-start(f32[3072,128]{1,0:T(8,128)} %get-tuple-element.16), channel_id=1, source_target_pairs={{0,2},{2,0},{1,3},{3,1},{4,6},{6,4},{5,7},{7,5},{8,10},{10,8},{9,1... | collective-permute-start | bytes 4718600 | tf_op jit(solution)/shard_map/ppermute | solution.py:25
  53.9 0.9 slice_bitcast_fusion.7
  54.9 0.7 collective-permute-start.10
  56.0 1.6 %collective-permute-start.9 = (f32[128,128]{1,0:T(8,128)S(1)}, f32[128,128]{1,0:T(8,128)S(1)}, u32[]{:S(2)}, u32[]{:S(2)}) collective-permute-start(f32[128,128]{1,0:T(8,128)S(1)} %get-tuple-element.27), channel_id=1, source_target_pairs={{12,0},{0,4},{4,8},{8,12},{13,1},{1,5},{5,9},{9,13},{14,2},{2,6},{... | collective-permute-start | bytes 196616 | tf_op jit(solution)/shard_map/ppermute | solution.py:21
  57.5 1.0 %slice_bitcast_fusion = (f32[208,128]{1,0:T(8,128)S(1)}, f32[208,128]{1,0:T(8,128)S(1)}, f32[208,128]{1,0:T(8,128)S(1)}) fusion(f32[3,208,128]{2,1,0:T(8,128)} %get-tuple-element.15), kind=kLoop, calls=%fused_computation.9 | loop fusion | bytes 638976 | tf_op jit(solution)/shard_map/squeeze | solution.py:365
  58.6 2.9 %collective-permute-done.10 = f32[128,128]{1,0:T(8,128)S(1)} collective-permute-done((f32[128,128]{1,0:T(8,128)S(1)}, f32[128,128]{1,0:T(8,128)S(1)}, u32[]{:S(2)}, u32[]{:S(2)}) %collective-permute-start.10) | collective-permute-done | bytes 65568 | tf_op jit(solution)/shard_map/ppermute | solution.py:21
  61.4 1.3 %collective-permute-start.15 = (f32[208,128]{1,0:T(8,128)S(1)}, f32[208,128]{1,0:T(8,128)S(1)}, u32[]{:S(2)}, u32[]{:S(2)}) collective-permute-start(f32[208,128]{1,0:T(8,128)S(1)} %get-tuple-element.19), channel_id=1, source_target_pairs={{4,0},{8,4},{12,8},{0,12},{5,1},{9,5},{13,9},{1,13},{6,2},{10,6},{... | collective-permute-start | bytes 319496 | tf_op jit(solution)/shard_map/ppermute | solution.py:21
  63.0 1.2 %collective-permute-start.13 = (f32[208,128]{1,0:T(8,128)S(1)}, f32[208,128]{1,0:T(8,128)S(1)}, u32[]{:S(2)}, u32[]{:S(2)}) collective-permute-start(f32[208,128]{1,0:T(8,128)S(1)} %get-tuple-element.21), channel_id=1, source_target_pairs={{12,0},{0,4},{4,8},{8,12},{13,1},{1,5},{5,9},{9,13},{14,2},{2,6},{... | collective-permute-start | bytes 319496 | tf_op jit(solution)/shard_map/ppermute | solution.py:21
  64.2 2.3 %collective-permute-done.15.refs_14_ = f32[208,128]{1,0:T(8,128)S(1)} collective-permute-done((f32[208,128]{1,0:T(8,128)S(1)}, f32[208,128]{1,0:T(8,128)S(1)}, u32[]{:S(2)}, u32[]{:S(2)}) %collective-permute-start.15) | collective-permute-done | bytes 106528 | tf_op jit(solution)/shard_map/ppermute | solution.py:21
  66.6 5.4 %collective-permute-done.14.refs_13_ = f32[208,128]{1,0:T(8,128)S(1)} collective-permute-done((f32[208,128]{1,0:T(8,128)S(1)}, f32[208,128]{1,0:T(8,128)S(1)}, u32[]{:S(2)}, u32[]{:S(2)}) %collective-permute-start.14) | collective-permute-done | bytes 106528 | tf_op jit(solution)/shard_map/ppermute | solution.py:21
  71.9 0.7 copy-done.14
  72.7 1.1 %copy-done.2 = f32[3072,128]{1,0:T(8,128)} copy-done((f32[3072,128]{1,0:T(8,128)}, f32[3072,128]{1,0:T(8,128)S(1)}, u32[]{:S(2)}) %copy-start.2) | copy-done | bytes 1572888
  73.8 20.5 %shard_map.84.stepped = f32[3072,128]{1,0:T(8,128)} custom-call(s32[8,2]{1,0:T(8,128)} %copy.15.refs_0_, s32[8,5]{1,0:T(8,128)} %refs_1_.3, s32[8]{0:T(128)} %owner.3, f32[2]{0:T(128)} %refs_3_.3, f32[3,3]{1,0:T(4,128)} %sources.1, f32[1]{0:T(128)} %bitcast.2.refs_5_.scale_ref, bf16[272,96]{1,0:T(8,128)(2,1)} %bitcast.43, ...), custom_call_target="tpu_custom_call" | custom-call | tf_op jit(solution)/shard_map/pallas_call | solution.py:373
  94.3 1.2 %copy-done.1 = f32[3072,128]{1,0:T(8,128)} copy-done((f32[3072,128]{1,0:T(8,128)}, f32[3072,128]{1,0:T(8,128)S(1)}, u32[]{:S(2)}) %copy-start.1) | copy-done | bytes 1572888
  95.5 3.8 %shard_map.85 = f32[3072,128]{1,0:T(8,128)} custom-call(s32[8]{0:T(128)} %owner.3, f32[3,3]{1,0:T(4,128)} %sources.1, f32[1]{0:T(128)} %bitcast.2.refs_5_.scale_ref, f32[3072,128]{1,0:T(8,128)} %shard_map.84.stepped, f32[3072,128]{1,0:T(8,128)} %copy-done.1), custom_call_target="tpu_custom_call" | custom-call | tf_op jit(solution)/shard_map/pallas_call | solution.py:387
  (61 shorter events, 1.9 us)
Async XLA Ops:
  0.0 14.3 %copy-start.3 = (f32[16,32,32]{2,1,0:T(8,128)S(1)}, f32[16,32,32]{2,1,0:T(8,128)}, u32[]{:S(2)}) copy-start(f32[16,32,32]{2,1,0:T(8,128)} %param.10) | copy-start | bytes 196612
  0.0 14.6 %copy-start.17 = (s32[8,2]{0,1:T(2,128)S(1)}, s32[8,2]{0,1:T(2,128)}, u32[]{:S(2)}) copy-start(s32[8,2]{0,1:T(2,128)} %param.13) | copy-start | bytes 196
  0.0 15.3 %copy-start.15 = (f32[32,32]{1,0:T(8,128)S(1)}, f32[32,32]{1,0:T(8,128)}, u32[]{:S(2)}) copy-start(f32[32,32]{1,0:T(8,128)} %param.9) | copy-start | bytes 12292
  0.0 15.3 %copy-start.16 = (f32[2]{0:T(128)S(1)}, f32[2]{0:T(128)}, u32[]{:S(2)}) copy-start(f32[2]{0:T(128)} %refs_3_.3) | copy-start | bytes 28
  0.0 18.5 %copy-start.12 = (f32[3,3]{1,0:T(4,128)S(1)}, f32[3,3]{1,0:T(4,128)}, u32[]{:S(2)}) copy-start(f32[3,3]{1,0:T(4,128)} %sources.1) | copy-start | bytes 112
  0.0 29.4 %collective-permute-start = (f32[3072,128]{1,0:T(8,128)}, f32[3072,128]{1,0:T(8,128)S(1)}, u32[]{:S(2)}, u32[]{:S(2)}) collective-permute-start(f32[3072,128]{1,0:T(8,128)} %bitcast.38), channel_id=1, source_target_pairs={{1,0},{0,1},{3,2},{2,3},{5,4},{4,5},{7,6},{6,7},{9,8},{8,9},{11,10... | collective-permute-start | bytes 4718600 | tf_op jit(solution)/shard_map/ppermute | solution.py:21
  4.4 16.5 %collective-permute-start.2 = (f32[128,128]{1,0:T(8,128)S(1)}, f32[128,128]{1,0:T(8,128)S(1)}, u32[]{:S(2)}, u32[]{:S(2)}) collective-permute-start(f32[128,128]{1,0:T(8,128)S(1)} %get-tuple-element.28), channel_id=1, source_target_pairs={{8,0},{12,4},{0,8},{4,12},{9,1},{13,5},{1,9},{5,13},{10,2},{14,6},... | collective-permute-start | bytes 196616 | tf_op jit(solution)/shard_map/ppermute | solution.py:21
  8.1 12.8 %collective-permute-start.3 = (f32[128,128]{1,0:T(8,128)S(1)}, f32[128,128]{1,0:T(8,128)S(1)}, u32[]{:S(2)}, u32[]{:S(2)}) collective-permute-start(f32[128,128]{1,0:T(8,128)S(1)} %get-tuple-element.29), channel_id=1, source_target_pairs={{4,0},{8,4},{12,8},{0,12},{5,1},{9,5},{13,9},{1,13},{6,2},{10,6},{... | collective-permute-start | bytes 196616 | tf_op jit(solution)/shard_map/ppermute | solution.py:21
  9.4 12.0 %collective-permute-start.1 = (f32[128,128]{1,0:T(8,128)S(1)}, f32[128,128]{1,0:T(8,128)S(1)}, u32[]{:S(2)}, u32[]{:S(2)}) collective-permute-start(f32[128,128]{1,0:T(8,128)S(1)} %get-tuple-element.30), channel_id=1, source_target_pairs={{12,0},{0,4},{4,8},{8,12},{13,1},{1,5},{5,9},{9,13},{14,2},{2,6},{... | collective-permute-start | bytes 196616 | tf_op jit(solution)/shard_map/ppermute | solution.py:21
  11.1 10.5 %collective-permute-start.7 = (f32[208,128]{1,0:T(8,128)S(1)}, f32[208,128]{1,0:T(8,128)S(1)}, u32[]{:S(2)}, u32[]{:S(2)}) collective-permute-start(f32[208,128]{1,0:T(8,128)S(1)} %get-tuple-element.22), channel_id=1, source_target_pairs={{4,0},{8,4},{12,8},{0,12},{5,1},{9,5},{13,9},{1,13},{6,2},{10,6},{... | collective-permute-start | bytes 319496 | tf_op jit(solution)/shard_map/ppermute | solution.py:21
  20.9 8.5 %collective-permute-start.6 = (f32[208,128]{1,0:T(8,128)S(1)}, f32[208,128]{1,0:T(8,128)S(1)}, u32[]{:S(2)}, u32[]{:S(2)}) collective-permute-start(f32[208,128]{1,0:T(8,128)S(1)} %get-tuple-element.23), channel_id=1, source_target_pairs={{8,0},{12,4},{0,8},{4,12},{9,1},{13,5},{1,9},{5,13},{10,2},{14,6},... | collective-permute-start | bytes 319496 | tf_op jit(solution)/shard_map/ppermute | solution.py:21
  20.9 8.5 %collective-permute-start.5 = (f32[208,128]{1,0:T(8,128)S(1)}, f32[208,128]{1,0:T(8,128)S(1)}, u32[]{:S(2)}, u32[]{:S(2)}) collective-permute-start(f32[208,128]{1,0:T(8,128)S(1)} %get-tuple-element.24), channel_id=1, source_target_pairs={{12,0},{0,4},{4,8},{8,12},{13,1},{1,5},{5,9},{9,13},{14,2},{2,6},{... | collective-permute-start | bytes 319496 | tf_op jit(solution)/shard_map/ppermute | solution.py:21
  21.5 8.7 %copy-start.4 = (f32[128,128]{1,0:T(8,128)}, f32[128,128]{1,0:T(8,128)S(1)}, u32[]{:S(2)}) copy-start(f32[128,128]{1,0:T(8,128)S(1)} %add_add_fusion.1.refs_10_) | copy-start | bytes 196612
  21.5 7.9 %collective-permute-start.4 = (f32[128,128]{1,0:T(8,128)S(1)}, f32[128,128]{1,0:T(8,128)S(1)}, u32[]{:S(2)}, u32[]{:S(2)}) collective-permute-start(f32[128,128]{1,0:T(8,128)S(1)} %add_add_fusion.1.refs_10_), channel_id=1, source_target_pairs={{1,0},{0,1},{3,2},{2,3},{5,4},{4,5},{7,6},{6,7},{9,8},{8,9},{11,10... | collective-permute-start | bytes 196616 | tf_op jit(solution)/shard_map/ppermute | solution.py:21
  21.7 8.6 %copy-start.6 = (f32[208,128]{1,0:T(8,128)}, f32[208,128]{1,0:T(8,128)S(1)}, u32[]{:S(2)}) copy-start(f32[208,128]{1,0:T(8,128)S(1)} %collective-permute-done.7.refs_14_) | copy-start | bytes 319492
  29.4 0.9 copy-start.7
  29.4 0.9 copy-start.9
  29.4 0.9 copy-start.13
  29.4 1.2 %copy-start = (f32[3072,128]{1,0:T(8,128)}, f32[3072,128]{1,0:T(8,128)S(1)}, u32[]{:S(2)}) copy-start(f32[3072,128]{1,0:T(8,128)S(1)} %collective-permute-done.refs_9_) | copy-start | bytes 4718596
  52.4 20.2 %collective-permute-start.8 = (f32[3072,128]{1,0:T(8,128)}, f32[3072,128]{1,0:T(8,128)S(1)}, u32[]{:S(2)}, u32[]{:S(2)}) collective-permute-start(f32[3072,128]{1,0:T(8,128)} %get-tuple-element.13.refs_8_), channel_id=1, source_target_pairs={{1,0},{0,1},{3,2},{2,3},{5,4},{4,5},{7,6},{6,7},{9,8},{8,9},{11,10... | collective-permute-start | bytes 4718600 | tf_op jit(solution)/shard_map/ppermute | solution.py:21
  52.4 41.9 %collective-permute-start.16 = (f32[3072,128]{1,0:T(8,128)}, f32[3072,128]{1,0:T(8,128)S(1)}, u32[]{:S(2)}, u32[]{:S(2)}) collective-permute-start(f32[3072,128]{1,0:T(8,128)} %get-tuple-element.16), channel_id=1, source_target_pairs={{0,2},{2,0},{1,3},{3,1},{4,6},{6,4},{5,7},{7,5},{8,10},{10,8},{9,1... | collective-permute-start | bytes 4718600 | tf_op jit(solution)/shard_map/ppermute | solution.py:25
  54.9 6.6 %collective-permute-start.10 = (f32[128,128]{1,0:T(8,128)S(1)}, f32[128,128]{1,0:T(8,128)S(1)}, u32[]{:S(2)}, u32[]{:S(2)}) collective-permute-start(f32[128,128]{1,0:T(8,128)S(1)} %get-tuple-element.25), channel_id=1, source_target_pairs={{8,0},{12,4},{0,8},{4,12},{9,1},{13,5},{1,9},{5,13},{10,2},{14,6},... | collective-permute-start | bytes 196616 | tf_op jit(solution)/shard_map/ppermute | solution.py:21
  55.5 7.3 %collective-permute-start.11 = (f32[128,128]{1,0:T(8,128)S(1)}, f32[128,128]{1,0:T(8,128)S(1)}, u32[]{:S(2)}, u32[]{:S(2)}) collective-permute-start(f32[128,128]{1,0:T(8,128)S(1)} %get-tuple-element.26), channel_id=1, source_target_pairs={{4,0},{8,4},{12,8},{0,12},{5,1},{9,5},{13,9},{1,13},{6,2},{10,6},{... | collective-permute-start | bytes 196616 | tf_op jit(solution)/shard_map/ppermute | solution.py:21
  56.0 7.0 %collective-permute-start.9 = (f32[128,128]{1,0:T(8,128)S(1)}, f32[128,128]{1,0:T(8,128)S(1)}, u32[]{:S(2)}, u32[]{:S(2)}) collective-permute-start(f32[128,128]{1,0:T(8,128)S(1)} %get-tuple-element.27), channel_id=1, source_target_pairs={{12,0},{0,4},{4,8},{8,12},{13,1},{1,5},{5,9},{9,13},{14,2},{2,6},{... | collective-permute-start | bytes 196616 | tf_op jit(solution)/shard_map/ppermute | solution.py:21
  61.4 5.1 %collective-permute-start.15 = (f32[208,128]{1,0:T(8,128)S(1)}, f32[208,128]{1,0:T(8,128)S(1)}, u32[]{:S(2)}, u32[]{:S(2)}) collective-permute-start(f32[208,128]{1,0:T(8,128)S(1)} %get-tuple-element.19), channel_id=1, source_target_pairs={{4,0},{8,4},{12,8},{0,12},{5,1},{9,5},{13,9},{1,13},{6,2},{10,6},{... | collective-permute-start | bytes 319496 | tf_op jit(solution)/shard_map/ppermute | solution.py:21
  62.8 9.1 %collective-permute-start.14 = (f32[208,128]{1,0:T(8,128)S(1)}, f32[208,128]{1,0:T(8,128)S(1)}, u32[]{:S(2)}, u32[]{:S(2)}) collective-permute-start(f32[208,128]{1,0:T(8,128)S(1)} %get-tuple-element.20), channel_id=1, source_target_pairs={{8,0},{12,4},{0,8},{4,12},{9,1},{13,5},{1,9},{5,13},{10,2},{14,6},... | collective-permute-start | bytes 319496 | tf_op jit(solution)/shard_map/ppermute | solution.py:21
  63.0 8.9 %collective-permute-start.13 = (f32[208,128]{1,0:T(8,128)S(1)}, f32[208,128]{1,0:T(8,128)S(1)}, u32[]{:S(2)}, u32[]{:S(2)}) collective-permute-start(f32[208,128]{1,0:T(8,128)S(1)} %get-tuple-element.21), channel_id=1, source_target_pairs={{12,0},{0,4},{4,8},{8,12},{13,1},{1,5},{5,9},{9,13},{14,2},{2,6},{... | collective-permute-start | bytes 319496 | tf_op jit(solution)/shard_map/ppermute | solution.py:21
  64.2 8.4 %copy-start.5 = (f32[128,128]{1,0:T(8,128)}, f32[128,128]{1,0:T(8,128)S(1)}, u32[]{:S(2)}) copy-start(f32[128,128]{1,0:T(8,128)S(1)} %add_add_fusion.refs_10_) | copy-start | bytes 196612
  66.6 6.1 %copy-start.8 = (f32[208,128]{1,0:T(8,128)}, f32[208,128]{1,0:T(8,128)S(1)}, u32[]{:S(2)}) copy-start(f32[208,128]{1,0:T(8,128)S(1)} %collective-permute-done.15.refs_14_) | copy-start | bytes 319492
  66.6 5.4 %collective-permute-start.12 = (f32[128,128]{1,0:T(8,128)S(1)}, f32[128,128]{1,0:T(8,128)S(1)}, u32[]{:S(2)}, u32[]{:S(2)}) collective-permute-start(f32[128,128]{1,0:T(8,128)S(1)} %add_add_fusion.refs_10_), channel_id=1, source_target_pairs={{1,0},{0,1},{3,2},{2,3},{5,4},{4,5},{7,6},{6,7},{9,8},{8,9},{11,10... | collective-permute-start | bytes 196616 | tf_op jit(solution)/shard_map/ppermute | solution.py:21
  72.7 1.1 %copy-start.2 = (f32[3072,128]{1,0:T(8,128)}, f32[3072,128]{1,0:T(8,128)S(1)}, u32[]{:S(2)}) copy-start(f32[3072,128]{1,0:T(8,128)S(1)} %collective-permute-done.8.refs_9_) | copy-start | bytes 4718596
  94.3 1.2 %copy-start.1 = (f32[3072,128]{1,0:T(8,128)}, f32[3072,128]{1,0:T(8,128)S(1)}, u32[]{:S(2)}) copy-start(f32[3072,128]{1,0:T(8,128)S(1)} %collective-permute-done.16.received) | copy-start | bytes 4718596
  (3 other events, 2.1 us)

commit v2 on v0

v2 whole, which is shorter than its diff:
```python
import functools

import jax
import jax.numpy as jnp
from jax import lax
from jax.experimental import pallas as pl
from jax.experimental.pallas import tpu as pltpu
from jax.sharding import PartitionSpec as P

BATCH = 16
SOURCES = 3
LANES = 128
F32 = jnp.float32
BF16 = jnp.bfloat16
I32 = jnp.int32
VM = pltpu.VMEM
SM = pltpu.SMEM
GRANT = 24 << 20

FEED, STAY, FEED_MORE, STAY_MORE, SQUARE, INFLOW = 0, 1, 2, 3, 4, 5
TILE, LEVEL_ONE, LEVEL_TWO, ROUTES = 0, 1, 2, 3
BELOW, ABOVE, LEFT, RIGHT, CORNER = 0, 1, 2, 3, 4
ROW, WANTED, LAST, PICKS = 0, 1, 2, 3


def permute(x, axis, pairs_of):
    return lax.ppermute(x, axis, [(i, pairs_of(i)) for i in range(lax.axis_size(axis))])


def from_next(x, axis):
    n = lax.axis_size(axis)
    return permute(x, axis, lambda i: (i - 1) % n)


def from_partner(x, axis, bit):
    return permute(x, axis, lambda i: i ^ 1 << bit)


class Shape:
    def __init__(self, block, tiles, levels):
        self.slots, self.states, self.phases, self.wide_two, self.wide_one = block
        self.tiles = tiles
        self.levels = levels
        self.units = self.slots * self.states
        self.rows = self.units * self.phases * self.wide_two
        self.rim_group = LANES // BATCH
        self.rim_parts = self.wide_two // self.rim_group
        self.state_rim_rows = self.states * self.rim_parts * self.phases
        self.rim_rows = self.slots * self.state_rim_rows
        self.edge_rows = self.units * self.phases
        self.lane_step = 2 * max(self.wide_two, BATCH)
        self.per_small = LANES // self.lane_step
        self.small_blocks = -(-self.states // self.per_small)
        self.small_rows_at = self.state_rim_rows + self.edge_rows
        self.message_rows = self.small_rows_at + self.small_blocks * self.phases
        self.bits = self.states.bit_length() - 1
        self.cross = SOURCES - self.bits
        self.deferred = self.cross == 1
        self.raw_end = self.states
        self.mid_end = self.units - self.states
        self.raw_rows = self.raw_end * self.wide_two * self.phases
        self.mid_rows = (self.mid_end - self.raw_end) * self.wide_two * self.phases
        self.ends_at = self.states * self.wide_two * self.phases
        self.rims_at = self.ends_at + self.mid_end * 2 * self.phases
        self.columns_at = self.rims_at + self.mid_end * self.rim_parts * self.phases
        self.per_column = LANES // self.wide_two
        self.late_rows = self.columns_at + -(-self.mid_end // self.per_column) * self.phases
        self.power = levels & (levels - 1) == 0

    def at(self, start):
        if not isinstance(start, int):
            start = pl.multiple_of(start, self.phases)
        return pl.ds(start, self.phases)

    def native(self, unit, u):
        return pl.ds(unit * self.phases * self.wide_two + u, self.phases, stride=self.wide_two)

    def by_level(self, unit, u):
        return self.at((unit * self.wide_two + u) * self.phases)

    def rim_at(self, unit, part):
        return self.at((unit * self.rim_parts + part) * self.phases)

    def small_at(self, state):
        return state // self.per_small, (state % self.per_small) * self.lane_step

    def sends_to(self, me, step):
        return me ^ step if self.power else (me + step) % self.levels

    def takes_from(self, me, step):
        return me ^ step if self.power else (me + self.levels - step) % self.levels


def lane_ids(shape):
    return lax.broadcasted_iota(I32, shape, len(shape) - 1)


def tile_at(owner, slot, tiles):
    found = jnp.int32(-1)
    for t in range(tiles):
        found = jnp.where(owner[t] == slot, t, found)
    return found


def route_of(routes, owner, tile, direction, slots):
    known = jnp.maximum(tile, 0)
    target = jnp.where(tile >= 0, routes[known, direction], -1)
    slot = owner[jnp.maximum(target, 0)]
    device = lax.div(slot, jnp.int32(slots))
    return target >= 0, device, slot - device * slots


def peer(sh, me, step, sending):
    if sh.power:
        return lax.bitwise_xor(me, jnp.int32(step))
    return lax.rem(me + (step if sending else sh.levels - step), jnp.int32(sh.levels))


def fill_send_plan(sh, routes, owner, plan):
    me = lax.axis_index("level")
    first = tile_at(owner, me * sh.slots, sh.tiles)
    count = jnp.int32(0)
    for k in range(sh.slots):
        count = count + jnp.where(tile_at(owner, me * sh.slots + k, sh.tiles) >= 0, 1, 0)
    for step in range(1, sh.levels):
        there = peer(sh, me, step, True)
        their_first = tile_at(owner, there * sh.slots, sh.tiles)
        lower = first < their_first
        found, device, _ = route_of(routes, owner, their_first, BELOW, sh.slots)
        plan[step - 1, ROW] = jnp.where(lower, sh.wide_two - 1, 0)
        plan[step - 1, WANTED] = jnp.where(jnp.logical_and(found, device == me), 1, 0)
        plan[step - 1, LAST] = (count - 1) * sh.states
        for k in range(sh.slots):
            tile = tile_at(owner, there * sh.slots + k, sh.tiles)
            _, _, left = route_of(routes, owner, tile, LEFT, sh.slots)
            _, _, right = route_of(routes, owner, tile, RIGHT, sh.slots)
            _, _, corner = route_of(routes, owner, tile, CORNER, sh.slots)
            plan[step - 1, PICKS + 2 * k] = jnp.where(lower, left, right) * sh.states
            plan[step - 1, PICKS + 2 * k + 1] = corner * sh.states


def add_packed(sh, lane, rims, column, u, values):
    part, q = u // sh.rim_group, u % sh.rim_group
    moved = pltpu.roll(values, (q * BATCH - (sh.wide_one - BATCH)) % LANES, 1)
    rims[part] = jnp.where(lax.div(lane, jnp.int32(BATCH)) == q, moved, rims[part])
    moved = pltpu.roll(values, u, 1) if u else values
    return jnp.where(lane == u, moved, column)


def write_messages(sh, plan, data, rims, columns, messages):
    phases, last_u = sh.phases, sh.wide_two - 1
    lane = lane_ids((phases, LANES))
    bottoms = [jnp.zeros((phases, LANES), F32) for _ in range(sh.small_blocks)]
    for s in range(sh.states):
        block, base = sh.small_at(s)
        values = columns[sh.at(s * phases), :]
        bottoms[block] = bottoms[block] + (pltpu.roll(values, base, 1) if base else values)
    for step in range(1, sh.levels):
        row = plan[step - 1, ROW]
        wanted = jnp.where(plan[step - 1, WANTED] > 0, 1.0, 0.0).astype(F32)
        last = plan[step - 1, LAST]
        for s in range(sh.states):
            for part in range(sh.rim_parts):
                messages[step - 1][sh.rim_at(s, part), :] = rims[sh.rim_at(last + s, part), :] * wanted
        small = list(bottoms)
        for k in range(sh.slots):
            slot, corner = plan[step - 1, PICKS + 2 * k], plan[step - 1, PICKS + 2 * k + 1]
            for s in range(sh.states):
                messages[step - 1][sh.at(sh.state_rim_rows + (k * sh.states + s) * phases), :] = data[sh.by_level(slot + s, row), :]
                block, base = sh.small_at(s)
                place = base + sh.lane_step // 2 + k
                moved = pltpu.roll(columns[sh.at((corner + s) * phases), :], (place - last_u) % LANES, 1)
                small[block] = jnp.where(lane == place, moved, small[block])
        for i, values in enumerate(small):
            messages[step - 1][sh.at(sh.small_rows_at + i * phases), :] = values


def pack_kernel(sh, routes, owner, data, send_plan, *outs):
    raw, (by_level, rims, columns, *messages) = (outs[0], outs[1:]) if sh.deferred else (None, outs)
    lane = lane_ids((sh.phases, LANES))
    fill_send_plan(sh, routes, owner, send_plan)

    def reorder(to_src, unit, carry):
        packed = [jnp.zeros((sh.phases, LANES), F32) for _ in range(sh.rim_parts)]
        column = jnp.zeros((sh.phases, LANES), F32)
        for u in range(sh.wide_two):
            values = data[sh.native(unit, u), :]
            by_level[sh.by_level(unit, u), :] = values
            if to_src:
                raw[sh.by_level(unit, u), :] = values
            column = add_packed(sh, lane, packed, column, u, values)
        for part, values in enumerate(packed):
            rims[sh.rim_at(unit, part), :] = values
        columns[sh.at(unit * sh.phases), :] = column
        return carry

    first = sh.raw_end if sh.deferred else 0
    if sh.deferred:
        lax.fori_loop(0, first, functools.partial(reorder, True), 0)
    lax.fori_loop(first, sh.units, functools.partial(reorder, False), 0)
    write_messages(sh, send_plan, by_level, rims, columns, messages)


def source_scalars(sources, scale, state):
    feed = jnp.float32(0.0)
    outflow = jnp.float32(0.0)
    inflow = []
    for k in range(SOURCES):
        on = lax.rem(lax.shift_right_logical(state, jnp.int32(k)), jnp.int32(2)) == 1
        turn_on, turn_off, arrive = sources[k, 0], sources[k, 1], sources[k, 2]
        feed = feed + jnp.where(on, arrive, 0.0)
        outflow = outflow + jnp.where(on, turn_off, turn_on)
        inflow.append(jnp.where(on, turn_on, turn_off) * scale)
    return feed * scale, outflow * scale, inflow


def prep_kernel(sh, routes, owner, levels_t, service, sources, phase_rates, batch_rates, plan, rates, paired, single,
                exits, turned, wide):
    me = lax.axis_index("level")
    for k in range(sh.slots):
        tile = tile_at(owner, me * sh.slots + k, sh.tiles)
        known = jnp.maximum(tile, 0)
        plan[k, TILE] = tile
        plan[k, LEVEL_ONE] = levels_t[known, 0]
        plan[k, LEVEL_TWO] = levels_t[known, 1]
        for r in range(5):
            found, device, slot = route_of(routes, owner, tile, r, sh.slots)
            kind = jnp.int32(1)
            for step in range(1, sh.levels):
                kind = jnp.where(device == peer(sh, me, step, False), step + 1, kind)
            plan[k, ROUTES + 3 * r] = jnp.where(found, kind, 0)
            plan[k, ROUTES + 3 * r + 1] = slot * sh.states
            plan[k, ROUTES + 3 * r + 2] = jnp.where(slot == 0, 1, 0)

    phases, full = sh.phases, phase_rates.shape[0]
    start = lax.axis_index("phase") * phases
    rows_here = pl.ds(pl.multiple_of(start, phases), phases)
    shape = (full, full)
    moving = phase_rates[...]
    moving = jnp.where(lax.broadcasted_iota(I32, shape, 0) == lax.broadcasted_iota(I32, shape, 1), 0.0, moving)
    total = moving
    for b in range(BATCH):
        total = total + batch_rates[b]
    leaving = jnp.sum(total, axis=1, keepdims=True)
    sources_top = jnp.float32(0.0)
    for k in range(SOURCES):
        sources_top = sources_top + jnp.maximum(sources[k, 2] + sources[k, 1], sources[k, 0])
    uniform = jnp.max(leaving) + (service[0] + service[1] + sources_top)
    inverse = 1.0 / jnp.full((phases, LANES), uniform, F32)
    scale = jnp.max(inverse)
    wide[...] = jnp.broadcast_to(leaving, (full, LANES))
    exits[...] = wide[rows_here, :] * inverse

    base = lax.axis_index("src") * sh.states
    rates[sh.states, 0] = service[0] * scale
    rates[sh.states, 1] = service[1] * scale
    for s in range(sh.states):
        state = base + s
        feed, outflow, inflow = source_scalars(sources, scale, state)
        rates[s, FEED] = feed
        rates[s, STAY] = 1.0 - feed - outflow
        for k in range(SOURCES):
            rates[s, INFLOW + k] = inflow[k]
        if sh.deferred:
            there = lax.bitwise_xor(state, jnp.int32(1 << sh.bits))
            feed_there, outflow_there, inflow_there = source_scalars(sources, scale, there)
            rates[s, FEED_MORE] = feed_there - feed
            rates[s, STAY_MORE] = (feed + outflow) - (feed_there + outflow_there)
            rates[s, SQUARE] = inflow[sh.bits] * inflow_there[sh.bits]

    for b in range(BATCH + 2):
        if b <= BATCH:
            values = (moving if b == 0 else batch_rates[b - 1]) * scale
            turned[0:full, :] = values
            turned[full:2 * full, :] = values
            turned[0:full, :] = turned[pl.ds(pl.multiple_of(start, phases), full), :].T
            values = turned[rows_here, :]
            high = values.astype(BF16)
            low = (values - high.astype(F32)).astype(BF16)
        else:
            high = jnp.zeros((phases, full), BF16)
            low = high
        parts = (high, low, high)
        for i, part in enumerate(parts):
            if 1 <= b <= BATCH:
                single[(b - 1) * phases:b * phases, i * full:(i + 1) * full] = part
            column = (b % 2) * 3 * full + i * full
            paired[(b // 2) * phases:(b // 2 + 1) * phases, column:column + full] = part


def split(values):
    high = values.astype(BF16)
    low = (values - high.astype(F32)).astype(BF16)
    return [high, high, low]


def inner_kernel(sh, first, plan, rates, weights, exits, own, other, *outs):
    phases = sh.phases
    out = outs[0]
    sent = outs[1] if first and sh.deferred else None
    other_at = sh.native if first else sh.by_level
    serve_one, serve_two = rates[sh.states, 0], rates[sh.states, 1]
    lane = lane_ids((phases, LANES))

    def unit_step(sending, unit, carry):
        k = lax.div(unit, jnp.int32(sh.states))
        s = unit - k * sh.states
        a, c = plan[k, LEVEL_ONE], plan[k, LEVEL_TWO]
        feed = rates[s, FEED]
        stay = rates[s, STAY] - exits[...] - jnp.where(jnp.logical_or(lane > 0, a > 0), serve_one, 0.0)
        for pair in range(sh.wide_two // 2):
            columns = []
            for u in (2 * pair, 2 * pair + 1):
                values = jnp.concatenate([own[sh.by_level(unit, u), :], other[other_at(unit, u), :]], axis=0)
                columns.append(jnp.concatenate(split(values) + split(pltpu.roll(values, 1, 1)), axis=0))
            product = jnp.dot(weights[...], jnp.concatenate(columns, axis=1), preferred_element_type=F32)
            for j, u in enumerate((2 * pair, 2 * pair + 1)):
                lanes = slice(j * LANES, (j + 1) * LANES)
                total = product[0:phases, lanes]
                for b in range(1, BATCH // 2 + 1):
                    total = total + pltpu.roll(product[b * phases:(b + 1) * phases, lanes], 2 * b, 1)
                here = own[sh.by_level(unit, u), :]
                two = serve_two if u else jnp.where(c > 0, serve_two, 0.0)
                total = total + (stay - two) * here
                if u:
                    prev = own[sh.by_level(unit, u - 1), :]
                    total = total + serve_one * pltpu.roll(prev, LANES - 1, 1) + feed * prev
                if u + 1 < sh.wide_two:
                    total = total + serve_two * own[sh.by_level(unit, u + 1), :]
                for bit in range(sh.bits):
                    flipped = unit - s + lax.bitwise_xor(s, jnp.int32(1 << bit))
                    total = total + rates[s, INFLOW + bit] * own[sh.by_level(flipped, u), :]
                out[sh.by_level(unit, u), :] = total
                if sending:
                    more = rates[s, STAY_MORE] * here
                    if u:
                        more = more + rates[s, FEED_MORE] * prev
                    sent[sh.by_level(unit - sh.raw_end, u), :] = 2.0 * total + more
        return carry

    if sent is not None:
        lax.fori_loop(sh.raw_end, sh.mid_end, functools.partial(unit_step, True), 0)
        lax.fori_loop(0, sh.raw_end, functools.partial(unit_step, False), 0)
        lax.fori_loop(sh.mid_end, sh.units, functools.partial(unit_step, False), 0)
    else:
        lax.fori_loop(0, sh.units, functools.partial(unit_step, False), 0)


def halo_kernel(sh, first, *refs):
    refs = list(refs)
    n, phases, last_u = sh.levels, sh.phases, sh.wide_two - 1
    plan, rates = refs[:2]
    refs = refs[2:]
    send_plan = refs.pop(0) if first else None
    weights, inner, own, rims_own, rims_other, columns_own, rim_got, rim_other = refs[:8]
    refs = refs[8:]
    edges, refs = refs[:n - 1], refs[n - 1:]
    raw = 0 if sh.deferred else sh.cross
    partners, refs = refs[:raw], refs[raw:]
    raw_got = refs.pop(0) if sh.deferred else None
    start_values = refs.pop(0) if sh.deferred and not first else None
    out = refs.pop(0)
    sent = refs.pop(0) if sh.deferred and first else None
    rims_out, columns_out = (refs.pop(0), refs.pop(0)) if first else (None, None)
    serve_one, serve_two = rates[sh.states, 0], rates[sh.states, 1]
    lane = lane_ids((phases, LANES))
    group_lane = lax.rem(lane, jnp.int32(BATCH))
    zero = jnp.zeros((phases, LANES), F32)
    if sent is not None:
        for start in range(sh.columns_at, sh.late_rows, phases):
            sent[start:start + phases, :] = zero

    def rim_product(halves):
        columns = [jnp.concatenate(split(jnp.concatenate(pair, axis=0)), axis=0) for pair in halves]
        product = jnp.dot(weights[...], jnp.concatenate(columns, axis=1), preferred_element_type=F32)
        sums = []
        for i in range(len(halves)):
            total = zero
            for b in range(1, BATCH + 1):
                block = product[(b - 1) * phases:b * phases, i * LANES:(i + 1) * LANES]
                total = total + jnp.where(group_lane < b, pltpu.roll(block, (b - BATCH) % LANES, 1), 0.0)
            sums.append(total)
        return sums

    def unit_step(group, unit, carry):
        k = lax.div(unit, jnp.int32(sh.states))
        s = unit - k * sh.states

        def kind(which):
            return plan[k, ROUTES + 3 * which]

        def beside(which):
            return plan[k, ROUTES + 3 * which + 1] + s

        def kept(which):
            return jnp.where(plan[k, ROUTES + 3 * which + 2] > 0, 0.0, 1.0).astype(F32)

        def number(flag):
            return jnp.where(flag, 1.0, 0.0).astype(F32)

        def remote(which, rows):
            value = zero
            for step in range(1, n):
                value = jnp.where(kind(which) == step + 1, edges[step - 1][rows, :], value)
            return value

        small_base = lax.rem(s, jnp.int32(sh.per_small)) * sh.lane_step
        small_at = sh.at(sh.small_rows_at + lax.div(s, jnp.int32(sh.per_small)) * phases)
        edge_at = sh.at(sh.state_rim_rows + unit * phases)
        left = jnp.where(kind(LEFT) == 1, own[sh.by_level(beside(LEFT), last_u), :], remote(LEFT, edge_at))
        right = jnp.where(kind(RIGHT) == 1, own[sh.by_level(beside(RIGHT), 0), :], remote(RIGHT, edge_at))
        above = jnp.where(
            kind(ABOVE) == 1,
            columns_own[sh.at(beside(ABOVE) * phases), :],
            pltpu.roll(remote(ABOVE, small_at), LANES - small_base, 1),
        )
        above = jnp.where(lane < sh.wide_two, above, 0.0) * serve_one
        corner = jnp.where(
            kind(CORNER) == 1,
            pltpu.roll(columns_own[sh.at(beside(CORNER) * phases), :], LANES - 1 - last_u, 1),
            pltpu.roll(remote(CORNER, small_at), LANES - 1 - (small_base + sh.lane_step // 2 + k), 1),
        )
        corner = jnp.where(lane == LANES - 1, corner, 0.0) * serve_one
        shifted = jnp.where(lane == LANES - 1, 0.0, pltpu.roll(left, LANES - 1, 1)) * serve_one
        own_column = columns_own[sh.at(unit * phases), :] * serve_one
        below_local, below_remote = number(kind(BELOW) == 1), number(kind(BELOW) > 1)
        under, mine = [], []
        for part in range(sh.rim_parts):
            under.append([
                rims_own[sh.rim_at(beside(BELOW), part), :] * below_local + rim_got[sh.rim_at(s, part), :] * below_remote,
                rims_other[sh.rim_at(beside(BELOW), part), :] * below_local
                + rim_other[sh.rim_at(s, part), :] * below_remote,
            ])
            mine.append([rims_own[sh.rim_at(unit, part), :], rims_other[sh.rim_at(unit, part), :]])
        feed = rates[s, FEED]
        if group is None:
            rims = rim_product([[p - q for p, q in zip(*both)] for both in zip(under, mine)])
        else:
            sums = rim_product(under + mine)
            reach, wrap = sums[:sh.rim_parts], sums[sh.rim_parts:]
            rims = [p - q for p, q in zip(reach, wrap)]
            drop = jnp.float32(0.0 if group == "raw" else 1.0)
            keep_left = kept(LEFT)
            sent_rims = [2.0 * (kept(BELOW) * p - drop * q) for p, q in zip(reach, wrap)]
            sent_column = 2.0 * (kept(ABOVE) * above - drop * own_column)
            sent_first = (2.0 * keep_left) * (shifted + feed * left) + (2.0 * kept(CORNER)) * corner
            sent_first = sent_first + ((2.0 * keep_left - 1.0) * rates[s, FEED_MORE]) * left
            sent_last = (2.0 * kept(RIGHT) * serve_two) * right
            if group != "last":
                sent[sh.at(sh.ends_at + 2 * unit * phases), :] = sent_first
                sent[sh.at(sh.ends_at + (2 * unit + 1) * phases), :] = sent_last
                for part in range(sh.rim_parts):
                    sent[sh.at(sh.rims_at + (unit * sh.rim_parts + part) * phases), :] = sent_rims[part]
                place = sh.at(sh.columns_at + lax.div(unit, jnp.int32(sh.per_column)) * phases)
                base = lax.rem(unit, jnp.int32(sh.per_column)) * sh.wide_two
                sent[place, :] = sent[place, :] + pltpu.roll(sent_column, base, 1)
        column = above - own_column
        packed, packed_column = [zero] * sh.rim_parts, zero
        for u in range(sh.wide_two):
            part, q = u // sh.rim_group, u % sh.rim_group

            def unpacked(rims, column):
                value = jnp.where(lane < BATCH, pltpu.roll(rims[part], LANES - q * BATCH, 1) if q else rims[part], 0.0)
                if u:
                    value = jnp.where(lane == LANES - 1, pltpu.roll(column, LANES - u, 1), value)
                return value

            inside = inner[sh.by_level(unit, u), :]
            total = inside + unpacked(rims, column)
            if u == 0:
                total = total + shifted + corner + feed * left
            if u == last_u:
                total = total + serve_two * right
            for bit, values in enumerate(partners):
                total = total + rates[s, INFLOW + sh.bits + bit] * values[sh.by_level(unit, u), :]
            if group == "raw":
                total = total + (2.0 * rates[s, INFLOW + sh.bits]) * raw_got[sh.by_level(unit, u), :]
            if start_values is not None:
                total = total + rates[s, SQUARE] * start_values[sh.by_level(unit, u), :]
            if raw_got is not None and carry == "raw":
                more = rates[s, STAY_MORE] * raw_got[sh.by_level(unit, u), :]
                if u:
                    more = more + rates[s, FEED_MORE] * raw_got[sh.by_level(unit, u - 1), :]
                total = total + rates[s, INFLOW + sh.bits] * more
            if first:
                packed_column = add_packed(sh, lane, packed, packed_column, u, total)
            if first or sh.deferred:
                out[sh.by_level(unit, u), :] = total
            else:
                out[sh.native(unit, u), :] = jnp.where(plan[k, TILE] >= 0, total, 0.0)
            if group == "last":
                value = 2.0 * inside + unpacked(sent_rims, sent_column) + rates[s, STAY_MORE] * own[sh.by_level(unit, u), :]
                if u:
                    value = value + rates[s, FEED_MORE] * own[sh.by_level(unit, u - 1), :]
                else:
                    value = value + sent_first
                if u == last_u:
                    value = value + sent_last
                sent[sh.by_level(unit - sh.mid_end, u), :] = value
        if first:
            for part in range(sh.rim_parts):
                rims_out[sh.rim_at(unit, part), :] = packed[part]
            columns_out[sh.at(unit * phases), :] = packed_column

    def sweep(start, stop, group, mark=None):
        def step(unit, carry):
            unit_step(group, unit, mark)
            return carry

        lax.fori_loop(start, stop, step, 0)

    if sent is not None:
        sweep(0, sh.raw_end, "raw")
        sweep(sh.raw_end, sh.mid_end, "mid")
        sweep(sh.mid_end, sh.units, "last")
    elif sh.deferred:
        sweep(0, sh.raw_end, None, "raw")
        sweep(sh.raw_end, sh.units, None)
    else:
        sweep(0, sh.units, None)
    if first:
        write_messages(sh, send_plan, out, rims_out, columns_out, refs)


def join_kernel(sh, plan, rates, stepped, got_mid, got_late, out):
    phases, last_u = sh.phases, sh.wide_two - 1
    lane = lane_ids((phases, LANES))
    inflow = rates[0, INFLOW + sh.bits]

    def unit_step(group, unit, carry):
        filled = plan[lax.div(unit, jnp.int32(sh.states)), TILE] >= 0
        if group != "last":
            rims = [
                got_late[sh.at(sh.rims_at + (unit * sh.rim_parts + part) * phases), :] for part in range(sh.rim_parts)
            ]
            column = got_late[sh.at(sh.columns_at + lax.div(unit, jnp.int32(sh.per_column)) * phases), :]
            base = lax.rem(unit, jnp.int32(sh.per_column)) * sh.wide_two
        for u in range(sh.wide_two):
            if group == "last":
                got = got_late[sh.by_level(unit - sh.mid_end, u), :]
            else:
                part, q = u // sh.rim_group, u % sh.rim_group
                got = jnp.where(lane < BATCH, pltpu.roll(rims[part], LANES - q * BATCH, 1) if q else rims[part], 0.0)
                if u:
                    got = jnp.where(lane == LANES - 1, pltpu.roll(column, LANES - (base + u), 1), got)
                if u in (0, last_u):
                    got = got + got_late[sh.at(sh.ends_at + (2 * unit + (1 if u else 0)) * phases), :]
                if group == "mid":
                    got = got + got_mid[sh.by_level(unit - sh.raw_end, u), :]
            total = stepped[sh.by_level(unit, u), :] + inflow * got
            out[sh.native(unit, u), :] = jnp.where(filled, total, 0.0)
        return carry

    lax.fori_loop(0, sh.raw_end, functools.partial(unit_step, "raw"), 0)
    lax.fori_loop(sh.raw_end, sh.mid_end, functools.partial(unit_step, "mid"), 0)
    lax.fori_loop(sh.mid_end, sh.units, functools.partial(unit_step, "last"), 0)


def body(
    state_values,
    phase_rates,
    batch_rates,
    service_rates,
    source_rates,
    tile_levels,
    routes,
    tile_owner,
):
    block = state_values.shape
    sh = Shape(block, tile_owner.shape[0], lax.axis_size("level"))
    n, full = sh.levels, phase_rates.shape[0]
    flat = state_values.reshape(sh.rows, LANES)
    smem, vmem = pl.BlockSpec(memory_space=SM), pl.BlockSpec(memory_space=VM)

    def array(rows):
        return jax.ShapeDtypeStruct((rows, LANES), F32)

    def table(rows, columns, dtype=F32):
        return jax.ShapeDtypeStruct((rows, columns), dtype)

    def call(kernel, scalars, arrays, shapes, micros, scalar_shapes=(), scratch=()):
        return pl.pallas_call(
            kernel,
            out_shape=tuple(scalar_shapes) + tuple(shapes),
            in_specs=[smem] * len(scalars) + [vmem] * len(arrays),
            out_specs=tuple([smem] * len(scalar_shapes) + [vmem] * len(shapes)),
            scratch_shapes=list(scratch),
            cost_estimate=pl.CostEstimate(flops=0, bytes_accessed=int(micros * 3.0e6), transcendentals=0),
            compiler_params=pltpu.CompilerParams(vmem_limit_bytes=GRANT),
        )(*scalars, *arrays)

    packed_shapes = [array(sh.rim_rows), array(sh.edge_rows)] + [array(sh.message_rows)] * (n - 1)

    def along_level(x, step):
        return permute(x, "level", lambda i: sh.sends_to(i, step))

    def exchange(messages, inside):
        got = [along_level(messages[i], i + 1) for i in range(n - 1)]
        got, inside = lax.optimization_barrier((got, inside))
        rim_got = sum(values[:sh.state_rim_rows] for values in got)
        return [rim_got, from_next(rim_got, "phase")] + got, inside

    other = from_next(flat, "phase")
    outs = call(
        functools.partial(pack_kernel, sh),
        [routes, tile_owner],
        [flat],
        ([array(sh.raw_rows)] if sh.deferred else []) + [array(sh.rows)] + packed_shapes,
        3,
        [table(n - 1, PICKS + 2 * sh.slots, I32)],
    )
    send_plan, outs = outs[0], outs[1:]
    if sh.deferred:
        raw_got, outs = from_partner(outs[0], "src", 0), outs[1:]
    start, rims, columns, messages = outs[0], outs[1], outs[2], outs[3:]
    plan, rates, paired, single, exits = call(
        functools.partial(prep_kernel, sh),
        [routes, tile_owner, tile_levels, service_rates, source_rates],
        [phase_rates, batch_rates],
        [
            table((BATCH // 2 + 1) * sh.phases, 6 * full, BF16),
            table(BATCH * sh.phases, 3 * full, BF16),
            array(sh.phases),
        ],
        2,
        [table(sh.slots, ROUTES + 15, I32), table(sh.states + 1, INFLOW + SOURCES)],
        [VM((2 * full, full), F32), VM((full, LANES), F32)],
    )

    def inner(first, values, other):
        shapes = [array(sh.rows)]
        if first and sh.deferred:
            shapes.append(array(sh.mid_rows))
        return call(functools.partial(inner_kernel, sh, first), [plan, rates], [paired, exits, values, other], shapes, 9)

    def halo(first, inside, values, rims, columns, got, extra):
        shapes = [array(sh.rows)]
        if first:
            shapes += ([array(sh.late_rows)] if sh.deferred else []) + packed_shapes
        return call(
            functools.partial(halo_kernel, sh, first),
            [plan, rates] + ([send_plan] if first else []),
            [single, inside, values, rims, from_next(rims, "phase"), columns] + got + extra,
            shapes,
            4,
        )

    if sh.deferred:
        inside, mid = inner(True, start, other)
        got_mid = from_partner(mid, "src", 0)
        got, inside = exchange(messages, inside)
        outs = halo(True, inside, start, rims, columns, got, [raw_got])
        once, late, rims, columns, messages = outs[0], outs[1], outs[2], outs[3], outs[4:]
        got_late = from_partner(late, "src", 0)
        (inside,) = inner(False, once, from_next(once, "phase"))
        got, inside = exchange(messages, inside)
        (twice,) = halo(False, inside, once, rims, columns, got, [raw_got, start])
        (result,) = call(
            functools.partial(join_kernel, sh), [plan, rates], [twice, got_mid, got_late], [array(sh.rows)], 3
        )
    else:
        (inside,) = inner(True, start, other)
        got, inside = exchange(messages, inside)
        extra = [from_partner(start, "src", bit) for bit in range(sh.cross)]
        outs = halo(True, inside, start, rims, columns, got, extra)
        once, rims, columns, messages = outs[0], outs[1], outs[2], outs[3:]
        (inside,) = inner(False, once, from_next(once, "phase"))
        got, inside = exchange(messages, inside)
        extra = [from_partner(once, "src", bit) for bit in range(sh.cross)]
        (result,) = halo(False, inside, once, rims, columns, got, extra)
    return result.reshape(block)


def solution(mesh):
    placed = (
        P(("groups", "level"), "src", "phase", None, None),
        P("groups", None),
        P("groups", None, None),
        P("groups"),
        P("groups", None),
        P("groups", None),
        P("groups", None),
        P("groups"),
    )
    return jax.shard_map(
        body,
        mesh=mesh,
        in_specs=placed,
        out_specs=P(("groups", "level"), "src", "phase", None, None),
        check_vma=False,
    )
```

time: 396 us -> 70 us (0.18); the launches traced: 388 us -> 69.6 us
  blocking collectives: 154 us -> 0 us
  matrix products: 142 us -> 0 us
  local copies, waits for them, and re-layouts: 52.6 us -> 3.52 us
  Pallas kernels: 0 us -> 38.2 us
  other arithmetic: 19 us -> 0.03 us
  between operations: 16.9 us -> 0.17 us
  starting transfers between devices: 3.67 us -> 15.7 us
  waiting for transfers between devices: 0.05 us -> 11.9 us
    all_gather x12 -> x0, blocking collectives: 154 us -> none  [the longest x2 32 us: body(): lax.all_gather(edge_sets[0], 'level', axis=0, tiled=True)]
    dot_general x44 -> x0, matrix products: 142 us -> none  [the longest x34 136 us: body(): jnp.einsum('cspuv,pq->csquv', window, tables_local[offset], precision=PRE...]
    pallas_call x0 -> x7, Pallas kernels: none -> 38.2 us  [call(): pl.pallas_call(kernel, out_shape=tuple(scalar_shapes) + tuple(shapes), in...]
    ppermute x2 -> x15, starting transfers between devices: 3.63 us -> 15.7 us  [permute(): lax.ppermute(x, axis, [(i, pairs_of(i)) for i in range(lax.axis_size(axis...]
    ppermute x2 -> x15, waiting for transfers between devices: 0.01 us -> 11.9 us  [permute(): lax.ppermute(x, axis, [(i, pairs_of(i)) for i in range(lax.axis_size(axis...]
    slice x12 -> x0, local copies, waits for them, and re-layouts: 9.63 us -> none  [the longest x3 2.84 us: edge_parts(): top_part = tile_block[..., tile_block.shape[-1] - rim_depth:]]
    reshape x10 -> x0, local copies, waits for them, and re-layouts: 9.07 us -> none  [the longest x2 4.88 us: body(): top_full = top_full.reshape(full_values.shape[:4] + (BATCH,))]
    select_n x2 -> x0, other arithmetic: 8.73 us -> none  [the longest x1 8.72 us: body(): current = jnp.where(filled[:, None, None, None, None], stepped, 0.0)]
  transfers between devices with their start and end apart: 4 -> 15, of which waited for: 0 -> 5; matrix products, arithmetic and copies ran while one was open for 47% -> 1% of each run, Pallas kernels for 0% -> 40%
where the time goes in v2:
time: 70 us; the launch traced here: 69.6 us
  Pallas kernels  38.2 us (55%)
  starting transfers between devices  15.7 us (22%)
  waiting for transfers between devices  11.9 us (17%)
  local copies, waits for them, and re-layouts  3.52 us (5%)
    pallas_call x7, Pallas kernels, call(): pl.pallas_call(kernel, out_shape=tuple(scalar_shapes) + tuple(shapes), in...  38.2 us
    ppermute x15, starting transfers between devices, permute(): lax.ppermute(x, axis, [(i, pairs_of(i)) for i in range(lax.axis_size(axis...  15.7 us
    ppermute x15, waiting for transfers between devices, permute(): lax.ppermute(x, axis, [(i, pairs_of(i)) for i in range(lax.axis_size(axis...  11.9 us
    unnamed x19, local copies, waits for them, and re-layouts  3.52 us
  transfers between devices with their start and end apart: 15, of which 5 were waited for; matrix products, arithmetic and copies ran while one was open for 1% of the time, Pallas kernels for 40%

profile of v2, /device:TPU:0, one launch (start us, length us, event | category | flops | bytes accessed | tf_op | source)
XLA Modules:
  0.0 69.6 jit_solution(2593120726809461749)
XLA Ops:
  0.0 0.5 collective-permute-start.3
  0.5 1.4 %copy-done = f32[3,4,16,16,128]{4,3,2,1,0:T(8,128)S(1)} copy-done((f32[3,4,16,16,128]{4,3,2,1,0:T(8,128)S(1)}, f32[3,4,16,16,128]{4,3,2,1,0:T(8,128)}, u32[]{:S(2)}) %copy-start) | copy-done | bytes 1572888
  1.9 0.7 copy-done.2
  2.6 0.7 copy-done.6
  3.3 3.4 %shard_map.83 = (s32[3,9]{1,0:T(4,128)S(1)}, f32[1024,128]{1,0:T(8,128)}, f32[3072,128]{1,0:T(8,128)S(1)}, f32[384,128]{1,0:T(8,128)S(1)}, f32[192,128]{1,0:T(8,...) custom-call(s32[8,5]{1,0:T(8,128)S(1)} %copy-done.2, s32[8]{0:T(128)S(1)} %copy-done.6, ...), custom_call_target="tpu_custom_call" | custom-call | bytes 9000000 | tf_op jit(solution)/shard_map/pallas_call | solution.py:582
  6.7 2.6 %collective-permute-start.6 = (f32[1024,128]{1,0:T(8,128)}, f32[1024,128]{1,0:T(8,128)S(1)}, u32[]{:S(2)}, u32[]{:S(2)}) collective-permute-start(f32[1024,128]{1,0:T(8,128)} %get-tuple-element.52), channel_id=1, source_target_pairs={{0,2},{2,0},{1,3},{3,1},{4,6},{6,4},{5,7},{7,5},{8,10},{10,8},{9,1... | collective-permute-start | bytes 1572872 | tf_op jit(solution)/shard_map/ppermute | solution.py:27
  9.2 1.6 %collective-permute-start = (f32[336,128]{1,0:T(8,128)}, f32[336,128]{1,0:T(8,128)S(1)}, u32[]{:S(2)}, u32[]{:S(2)}) collective-permute-start(f32[336,128]{1,0:T(8,128)} %get-tuple-element.39), channel_id=1, source_target_pairs={{0,4},{4,0},{8,12},{12,8},{1,5},{5,1},{9,13},{13,9},{2,6},{6,2},{1... | collective-permute-start | bytes 516104 | tf_op jit(solution)/shard_map/ppermute | solution.py:27
  10.8 2.6 %collective-permute-start.1 = (f32[336,128]{1,0:T(8,128)S(1)}, f32[336,128]{1,0:T(8,128)S(1)}, u32[]{:S(2)}, u32[]{:S(2)}) collective-permute-start(f32[336,128]{1,0:T(8,128)S(1)} %get-tuple-element.40), channel_id=1, source_target_pairs={{0,8},{4,12},{8,0},{12,4},{1,9},{5,13},{9,1},{13,5},{2,10},{6,14},... | collective-permute-start | bytes 516104 | tf_op jit(solution)/shard_map/ppermute | solution.py:27
  13.4 0.2 collective-permute-start.2
  13.6 0.8 %copy.9.levels_t = s32[8,2]{1,0:T(8,128)S(1)} copy(s32[8,2]{0,1:T(2,128)} %param.13) | data formatting | bytes 128 | tf_op args[5]
  14.4 2.6 %shard_map.82 = (s32[3,18]{1,0:T(4,128)S(1)}, f32[5,8]{1,0:T(8,128)S(1)}, bf16[144,192]{1,0:T(8,128)(2,1)S(1)}, bf16[256,96]{1,0:T(8,128)(2,1)S(1)}, f32[16,128]{1,0:T(8,128)S(1)}) custom-call(s32[8,5]{1,0:T(8,128)S(1)} %copy-done.3, s32[8]{0:T(128)S(1)} %copy-done.7, s32[8,2]{1,0:T(8,128)S(1)} %copy.9.levels_t, f32[2]{0:T(128)S(1)} %copy-done.8, ...), custom_call_target="tpu_custom_call" | custom-call | bytes 6000000 | tf_op jit(solution)/shard_map/pallas_call | solution.py:582
  17.0 0.0 collective-permute-done.3.other
  17.0 0.1 collective-permute-start.4
  17.1 8.6 %shard_map.84 = (f32[3072,128]{1,0:T(8,128)S(1)}, f32[1024,128]{1,0:T(8,128)S(1)}) custom-call(s32[3,18]{1,0:T(4,128)S(1)} %get-tuple-element.35.plan.refs_0_, f32[5,8]{1,0:T(8,128)S(1)} %get-tuple-element.36.rates.refs_1_, bf16[144,192]{1,0:T(8,128)(2,1)S(1)} %get-tuple-element.42.weights, f32[16,128]{1,0:T(8,128)S(1)} %get-tuple-element.43.exits, ...), custom_call_target="tpu_custom_call" | custom-call | bytes 27000000 | tf_op jit(solution)/shard_map/pallas_call | solution.py:582
  25.7 0.6 collective-permute-done.1.refs_12_
  26.3 0.1 collective-permute-start.5
  26.4 1.2 %collective-permute-done.5.refs_10_ = f32[128,128]{1,0:T(8,128)S(1)} collective-permute-done((f32[128,128]{1,0:T(8,128)S(1)}, f32[128,128]{1,0:T(8,128)S(1)}, u32[]{:S(2)}, u32[]{:S(2)}) %collective-permute-start.5) | collective-permute-done | bytes 65568 | tf_op jit(solution)/shard_map/ppermute | solution.py:27
  27.7 7.3 %shard_map.85 = (f32[3072,128]{1,0:T(8,128)S(1)}, f32[1552,128]{1,0:T(8,128)S(1)}, f32[384,128]{1,0:T(8,128)S(1)}, f32[192,128]{1,0:T(8,128)S(1)}, f32[336,128]{...) custom-call(s32[3,18]{1,0:T(4,128)S(1)} %get-tuple-element.35.plan.refs_0_, ...), custom_call_target="tpu_custom_call" | custom-call | bytes 12000000 | tf_op jit(solution)/shard_map/pallas_call | solution.py:582
  35.0 0.2 collective-permute-start.10
  35.2 0.5 collective-permute-start.14
  35.8 1.5 %collective-permute-start.13 = (f32[1024,128]{1,0:T(8,128)S(1)}, f32[1024,128]{1,0:T(8,128)S(1)}, u32[]{:S(2)}, u32[]{:S(2)}) collective-permute-start(f32[1024,128]{1,0:T(8,128)S(1)} %get-tuple-element.63), channel_id=1, source_target_pairs={{0,2},{2,0},{1,3},{3,1},{4,6},{6,4},{5,7},{7,5},{8,10},{10,8},{9,1... | collective-permute-start | bytes 1572872 | tf_op jit(solution)/shard_map/ppermute | solution.py:27
  37.3 3.2 %collective-permute-start.7 = (f32[336,128]{1,0:T(8,128)S(1)}, f32[336,128]{1,0:T(8,128)S(1)}, u32[]{:S(2)}, u32[]{:S(2)}) collective-permute-start(f32[336,128]{1,0:T(8,128)S(1)} %get-tuple-element.53), channel_id=1, source_target_pairs={{0,4},{4,0},{8,12},{12,8},{1,5},{5,1},{9,13},{13,9},{2,6},{6,2},{1... | collective-permute-start | bytes 516104 | tf_op jit(solution)/shard_map/ppermute | solution.py:27
  40.5 1.0 %collective-permute-start.8 = (f32[336,128]{1,0:T(8,128)S(1)}, f32[336,128]{1,0:T(8,128)S(1)}, u32[]{:S(2)}, u32[]{:S(2)}) collective-permute-start(f32[336,128]{1,0:T(8,128)S(1)} %get-tuple-element.54), channel_id=1, source_target_pairs={{0,8},{4,12},{8,0},{12,4},{1,9},{5,13},{9,1},{13,5},{2,10},{6,14},... | collective-permute-start | bytes 516104 | tf_op jit(solution)/shard_map/ppermute | solution.py:27
  41.5 1.5 %collective-permute-start.9 = (f32[336,128]{1,0:T(8,128)S(1)}, f32[336,128]{1,0:T(8,128)S(1)}, u32[]{:S(2)}, u32[]{:S(2)}) collective-permute-start(f32[336,128]{1,0:T(8,128)S(1)} %get-tuple-element.55), channel_id=1, source_target_pairs={{0,12},{4,8},{8,4},{12,0},{1,13},{5,9},{9,5},{13,1},{2,14},{6,10},... | collective-permute-start | bytes 516104 | tf_op jit(solution)/shard_map/ppermute | solution.py:27
  43.0 7.9 %shard_map.86.refs_3_ = f32[3072,128]{1,0:T(8,128)S(1)} custom-call(s32[3,18]{1,0:T(4,128)S(1)} %get-tuple-element.35.plan.refs_0_, f32[5,8]{1,0:T(8,128)S(1)} %get-tuple-element.36.rates.refs_1_, bf16[144,192]{1,0:T(8,128)(2,1)S(1)} %get-tuple-element.42.weights, f32[16,128]{1,0:T(8,128)S(1)} %get-tuple-element.43.exits, ...), custom_call_target="tpu_custom_call" | custom-call | bytes 27000000 | tf_op jit(solution)/shard_map/pallas_call | solution.py:582
  50.9 0.1 collective-permute-start.11
  51.0 5.0 %collective-permute-done.8.refs_11_ = f32[336,128]{1,0:T(8,128)S(1)} collective-permute-done((f32[336,128]{1,0:T(8,128)S(1)}, f32[336,128]{1,0:T(8,128)S(1)}, u32[]{:S(2)}, u32[]{:S(2)}) %collective-permute-start.8) | collective-permute-done | bytes 172064 | tf_op jit(solution)/shard_map/ppermute | solution.py:27
  56.1 0.1 collective-permute-start.12
  56.1 1.2 %collective-permute-done.12.refs_9_ = f32[128,128]{1,0:T(8,128)S(1)} collective-permute-done((f32[128,128]{1,0:T(8,128)S(1)}, f32[128,128]{1,0:T(8,128)S(1)}, u32[]{:S(2)}, u32[]{:S(2)}) %collective-permute-start.12) | collective-permute-done | bytes 65568 | tf_op jit(solution)/shard_map/ppermute | solution.py:27
  57.4 5.3 %shard_map.87.stepped = f32[3072,128]{1,0:T(8,128)S(1)} custom-call(s32[3,18]{1,0:T(4,128)S(1)} %get-tuple-element.35.plan.refs_0_, f32[5,8]{1,0:T(8,128)S(1)} %get-tuple-element.36.rates.refs_1_, bf16[256,96]{1,0:T(8,128)(2,1)S(1)} %get-tuple-element.37.refs_3_.refs_2_, f32[3072,128]{1,0:T(8,128)S(1)} %shard_map.86.refs_3_, ...), custom_call_target="tpu_custom_call" | custom-call | bytes 12000000 | tf_op jit(solution)/shard_map/pallas_call | solution.py:582
  62.7 3.8 %collective-permute-done.13.got_mid = f32[1024,128]{1,0:T(8,128)S(1)} collective-permute-done((f32[1024,128]{1,0:T(8,128)S(1)}, f32[1024,128]{1,0:T(8,128)S(1)}, u32[]{:S(2)}, u32[]{:S(2)}) %collective-permute-start.13) | collective-permute-done | bytes 524320 | tf_op jit(solution)/shard_map/ppermute | solution.py:27
  66.5 3.1 %shard_map.88 = f32[3072,128]{1,0:T(8,128)} custom-call(s32[3,18]{1,0:T(4,128)S(1)} %get-tuple-element.35.plan.refs_0_, f32[5,8]{1,0:T(8,128)S(1)} %get-tuple-element.36.rates.refs_1_, f32[3072,128]{1,0:T(8,128)S(1)} %shard_map.87.stepped, f32[1024,128]{1,0:T(8,128)S(1)} %collective-permute-done.13.got_mid, f32[1552,128]{1,0:T(8,128)S(1)} %collective-permute-done.14.got_late), custom_call_target="tpu_custom_call" | custom-call | bytes 9000000 | tf_op jit(solution)/shard_map/pallas_call | solution.py:582
  (26 shorter events, 0.1 us)
Async XLA Ops:
  0.0 14.4 %copy-start.7 = (s32[8]{0:T(128)S(1)}, s32[8]{0:T(128)}, u32[]{:S(2)}) copy-start(s32[8]{0:T(128)} %owner.3) | copy-start | bytes 100
  0.0 14.4 %copy-start.8 = (f32[2]{0:T(128)S(1)}, f32[2]{0:T(128)}, u32[]{:S(2)}) copy-start(f32[2]{0:T(128)} %service.1) | copy-start | bytes 28
  0.0 17.0 %collective-permute-start.3 = (f32[3072,128]{1,0:T(8,128)}, f32[3072,128]{1,0:T(8,128)}, u32[]{:S(2)}, u32[]{:S(2)}) collective-permute-start(f32[3072,128]{1,0:T(8,128)} %bitcast.2), channel_id=1, source_target_pairs={{0,1},{1,0},{2,3},{3,2},{4,5},{5,4},{6,7},{7,6},{8,9},{9,8},{10,11... | collective-permute-start | bytes 4718600 | tf_op jit(solution)/shard_map/ppermute | solution.py:27
  0.5 1.4 %copy-start = (f32[3,4,16,16,128]{4,3,2,1,0:T(8,128)S(1)}, f32[3,4,16,16,128]{4,3,2,1,0:T(8,128)}, u32[]{:S(2)}) copy-start(f32[3,4,16,16,128]{4,3,2,1,0:T(8,128)} %param.8) | copy-start | bytes 4718596
  1.9 0.7 copy-start.2
  2.6 0.7 copy-start.6
  3.2 11.1 %copy-start.1 = (f32[16,32,32]{2,1,0:T(8,128)S(1)}, f32[16,32,32]{2,1,0:T(8,128)}, u32[]{:S(2)}) copy-start(f32[16,32,32]{2,1,0:T(8,128)} %batch_rates.1) | copy-start | bytes 196612
  3.3 11.1 %copy-start.3 = (s32[8,5]{1,0:T(8,128)S(1)}, s32[8,5]{1,0:T(8,128)}, u32[]{:S(2)}) copy-start(s32[8,5]{1,0:T(8,128)} %routes.3) | copy-start | bytes 484
  3.3 11.1 %copy-start.4 = (f32[32,32]{1,0:T(8,128)S(1)}, f32[32,32]{1,0:T(8,128)}, u32[]{:S(2)}) copy-start(f32[32,32]{1,0:T(8,128)} %phase_rates.1) | copy-start | bytes 12292
  3.3 11.1 %copy-start.5 = (f32[3,3]{1,0:T(4,128)S(1)}, f32[3,3]{1,0:T(4,128)}, u32[]{:S(2)}) copy-start(f32[3,3]{1,0:T(4,128)} %sources.1) | copy-start | bytes 112
  6.7 19.8 %collective-permute-start.6 = (f32[1024,128]{1,0:T(8,128)}, f32[1024,128]{1,0:T(8,128)S(1)}, u32[]{:S(2)}, u32[]{:S(2)}) collective-permute-start(f32[1024,128]{1,0:T(8,128)} %get-tuple-element.52), channel_id=1, source_target_pairs={{0,2},{2,0},{1,3},{3,1},{4,6},{6,4},{5,7},{7,5},{8,10},{10,8},{9,1... | collective-permute-start | bytes 1572872 | tf_op jit(solution)/shard_map/ppermute | solution.py:27
  9.2 16.5 %collective-permute-start = (f32[336,128]{1,0:T(8,128)}, f32[336,128]{1,0:T(8,128)S(1)}, u32[]{:S(2)}, u32[]{:S(2)}) collective-permute-start(f32[336,128]{1,0:T(8,128)} %get-tuple-element.39), channel_id=1, source_target_pairs={{0,4},{4,0},{8,12},{12,8},{1,5},{5,1},{9,13},{13,9},{2,6},{6,2},{1... | collective-permute-start | bytes 516104 | tf_op jit(solution)/shard_map/ppermute | solution.py:27
  10.8 15.5 %collective-permute-start.1 = (f32[336,128]{1,0:T(8,128)S(1)}, f32[336,128]{1,0:T(8,128)S(1)}, u32[]{:S(2)}, u32[]{:S(2)}) collective-permute-start(f32[336,128]{1,0:T(8,128)S(1)} %get-tuple-element.40), channel_id=1, source_target_pairs={{0,8},{4,12},{8,0},{12,4},{1,9},{5,13},{9,1},{13,5},{2,10},{6,14},... | collective-permute-start | bytes 516104 | tf_op jit(solution)/shard_map/ppermute | solution.py:27
  13.4 12.9 %collective-permute-start.2 = (f32[336,128]{1,0:T(8,128)S(1)}, f32[336,128]{1,0:T(8,128)S(1)}, u32[]{:S(2)}, u32[]{:S(2)}) collective-permute-start(f32[336,128]{1,0:T(8,128)S(1)} %get-tuple-element.41), channel_id=1, source_target_pairs={{0,12},{4,8},{8,4},{12,0},{1,13},{5,9},{9,5},{13,1},{2,14},{6,10},... | collective-permute-start | bytes 516104 | tf_op jit(solution)/shard_map/ppermute | solution.py:27
  17.0 9.4 %collective-permute-start.4 = (f32[384,128]{1,0:T(8,128)S(1)}, f32[384,128]{1,0:T(8,128)S(1)}, u32[]{:S(2)}, u32[]{:S(2)}) collective-permute-start(f32[384,128]{1,0:T(8,128)S(1)} %get-tuple-element.47.refs_6_), channel_id=1, source_target_pairs={{0,1},{1,0},{2,3},{3,2},{4,5},{5,4},{6,7},{7,6},{8,9},{9,8},{10,11... | collective-permute-start | bytes 589832 | tf_op jit(solution)/shard_map/ppermute | solution.py:27
  26.3 1.3 %collective-permute-start.5 = (f32[128,128]{1,0:T(8,128)S(1)}, f32[128,128]{1,0:T(8,128)S(1)}, u32[]{:S(2)}, u32[]{:S(2)}) collective-permute-start(f32[128,128]{1,0:T(8,128)S(1)} %slice_add_fusion.1.refs_9_), channel_id=1, source_target_pairs={{0,1},{1,0},{2,3},{3,2},{4,5},{5,4},{6,7},{7,6},{8,9},{9,8},{10,11... | collective-permute-start | bytes 196616 | tf_op jit(solution)/shard_map/ppermute | solution.py:27
  35.0 6.5 %collective-permute-start.10 = (f32[3072,128]{1,0:T(8,128)S(1)}, f32[3072,128]{1,0:T(8,128)S(1)}, u32[]{:S(2)}, u32[]{:S(2)}) collective-permute-start(f32[3072,128]{1,0:T(8,128)S(1)} %get-tuple-element.56.own.refs_4_), channel_id=1, source_target_pairs={{0,1},{1,0},{2,3},{3,2},{4,5},{5,4},{6,7},{7,6},{8,9},{9,8},{10,11... | collective-permute-start | bytes 4718600 | tf_op jit(solution)/shard_map/ppermute | solution.py:27
  35.2 31.2 %collective-permute-start.14 = (f32[1552,128]{1,0:T(8,128)S(1)}, f32[1552,128]{1,0:T(8,128)S(1)}, u32[]{:S(2)}, u32[]{:S(2)}) collective-permute-start(f32[1552,128]{1,0:T(8,128)S(1)} %get-tuple-element.64), channel_id=1, source_target_pairs={{0,2},{2,0},{1,3},{3,1},{4,6},{6,4},{5,7},{7,5},{8,10},{10,8},{9,1... | collective-permute-start | bytes 2383880 | tf_op jit(solution)/shard_map/ppermute | solution.py:27
  35.8 30.7 %collective-permute-start.13 = (f32[1024,128]{1,0:T(8,128)S(1)}, f32[1024,128]{1,0:T(8,128)S(1)}, u32[]{:S(2)}, u32[]{:S(2)}) collective-permute-start(f32[1024,128]{1,0:T(8,128)S(1)} %get-tuple-element.63), channel_id=1, source_target_pairs={{0,2},{2,0},{1,3},{3,1},{4,6},{6,4},{5,7},{7,5},{8,10},{10,8},{9,1... | collective-permute-start | bytes 1572872 | tf_op jit(solution)/shard_map/ppermute | solution.py:27
  37.3 13.6 %collective-permute-start.7 = (f32[336,128]{1,0:T(8,128)S(1)}, f32[336,128]{1,0:T(8,128)S(1)}, u32[]{:S(2)}, u32[]{:S(2)}) collective-permute-start(f32[336,128]{1,0:T(8,128)S(1)} %get-tuple-element.53), channel_id=1, source_target_pairs={{0,4},{4,0},{8,12},{12,8},{1,5},{5,1},{9,13},{13,9},{2,6},{6,2},{1... | collective-permute-start | bytes 516104 | tf_op jit(solution)/shard_map/ppermute | solution.py:27
  40.5 15.5 %collective-permute-start.8 = (f32[336,128]{1,0:T(8,128)S(1)}, f32[336,128]{1,0:T(8,128)S(1)}, u32[]{:S(2)}, u32[]{:S(2)}) collective-permute-start(f32[336,128]{1,0:T(8,128)S(1)} %get-tuple-element.54), channel_id=1, source_target_pairs={{0,8},{4,12},{8,0},{12,4},{1,9},{5,13},{9,1},{13,5},{2,10},{6,14},... | collective-permute-start | bytes 516104 | tf_op jit(solution)/shard_map/ppermute | solution.py:27
  41.5 14.5 %collective-permute-start.9 = (f32[336,128]{1,0:T(8,128)S(1)}, f32[336,128]{1,0:T(8,128)S(1)}, u32[]{:S(2)}, u32[]{:S(2)}) collective-permute-start(f32[336,128]{1,0:T(8,128)S(1)} %get-tuple-element.55), channel_id=1, source_target_pairs={{0,12},{4,8},{8,4},{12,0},{1,13},{5,9},{9,5},{13,1},{2,14},{6,10},... | collective-permute-start | bytes 516104 | tf_op jit(solution)/shard_map/ppermute | solution.py:27
  50.9 5.2 %collective-permute-start.11 = (f32[384,128]{1,0:T(8,128)S(1)}, f32[384,128]{1,0:T(8,128)S(1)}, u32[]{:S(2)}, u32[]{:S(2)}) collective-permute-start(f32[384,128]{1,0:T(8,128)S(1)} %get-tuple-element.58.refs_5_), channel_id=1, source_target_pairs={{0,1},{1,0},{2,3},{3,2},{4,5},{5,4},{6,7},{7,6},{8,9},{9,8},{10,11... | collective-permute-start | bytes 589832 | tf_op jit(solution)/shard_map/ppermute | solution.py:27
  56.1 1.3 %collective-permute-start.12 = (f32[128,128]{1,0:T(8,128)S(1)}, f32[128,128]{1,0:T(8,128)S(1)}, u32[]{:S(2)}, u32[]{:S(2)}) collective-permute-start(f32[128,128]{1,0:T(8,128)S(1)} %slice_add_fusion.refs_8_), channel_id=1, source_target_pairs={{0,1},{1,0},{2,3},{3,2},{4,5},{5,4},{6,7},{7,6},{8,9},{9,8},{10,11... | collective-permute-start | bytes 196616 | tf_op jit(solution)/shard_map/ppermute | solution.py:27

commit v3 on v2

--- a/solution.py
+++ b/solution.py
@@ -6,6 +6,7 @@
 from jax.experimental import pallas as pl
 from jax.experimental.pallas import tpu as pltpu
 from jax.sharding import PartitionSpec as P
+
 
 BATCH = 16
 SOURCES = 3
@@ -214,7 +215,7 @@
     return feed * scale, outflow * scale, inflow
 
 
-def prep_kernel(sh, routes, owner, levels_t, service, sources, phase_rates, batch_rates, plan, rates, paired, single,
+def prep_kernel(sh, routes, owner, levels_t, service, sources, phase_rates, batch_rates, plan, rates, paired, rim_paired,
                 exits, turned, wide):
     me = lax.axis_index("level")
     for k in range(sh.slots):
@@ -283,7 +284,8 @@
         parts = (high, low, high)
         for i, part in enumerate(parts):
             if 1 <= b <= BATCH:
-                single[(b - 1) * phases:b * phases, i * full:(i + 1) * full] = part
+                column = ((b - 1) % 2) * 3 * full + i * full
+                rim_paired[((b - 1) // 2) * phases:((b - 1) // 2 + 1) * phases, column:column + full] = part
             column = (b % 2) * 3 * full + i * full
             paired[(b // 2) * phases:(b // 2 + 1) * phases, column:column + full] = part
 
@@ -301,6 +303,8 @@
     other_at = sh.native if first else sh.by_level
     serve_one, serve_two = rates[sh.states, 0], rates[sh.states, 1]
     lane = lane_ids((phases, LANES))
+    inner_one = jnp.where(lane == LANES - 1, 0.0, serve_one)
+    later = lane_ids((weights.shape[1] // 6, LANES)) > 0
 
     def unit_step(sending, unit, carry):
         k = lax.div(unit, jnp.int32(sh.states))
@@ -312,19 +316,20 @@
             columns = []
             for u in (2 * pair, 2 * pair + 1):
                 values = jnp.concatenate([own[sh.by_level(unit, u), :], other[other_at(unit, u), :]], axis=0)
-                columns.append(jnp.concatenate(split(values) + split(pltpu.roll(values, 1, 1)), axis=0))
+                columns.append(jnp.concatenate(split(values) + split(jnp.where(later, pltpu.roll(values, 1, 1), 0.0)), axis=0))
             product = jnp.dot(weights[...], jnp.concatenate(columns, axis=1), preferred_element_type=F32)
             for j, u in enumerate((2 * pair, 2 * pair + 1)):
                 lanes = slice(j * LANES, (j + 1) * LANES)
                 total = product[0:phases, lanes]
                 for b in range(1, BATCH // 2 + 1):
-                    total = total + pltpu.roll(product[b * phases:(b + 1) * phases, lanes], 2 * b, 1)
+                    moved = pltpu.roll(product[b * phases:(b + 1) * phases, lanes], 2 * b, 1)
+                    total = total + jnp.where(lane >= 2 * b, moved, 0.0)
                 here = own[sh.by_level(unit, u), :]
                 two = serve_two if u else jnp.where(c > 0, serve_two, 0.0)
                 total = total + (stay - two) * here
                 if u:
                     prev = own[sh.by_level(unit, u - 1), :]
-                    total = total + serve_one * pltpu.roll(prev, LANES - 1, 1) + feed * prev
+                    total = total + inner_one * pltpu.roll(prev, LANES - 1, 1) + feed * prev
                 if u + 1 < sh.wide_two:
                     total = total + serve_two * own[sh.by_level(unit, u + 1), :]
                 for bit in range(sh.bits):
@@ -371,14 +376,20 @@
             sent[start:start + phases, :] = zero
 
     def rim_product(halves):
-        columns = [jnp.concatenate(split(jnp.concatenate(pair, axis=0)), axis=0) for pair in halves]
+        columns = []
+        for pair in halves:
+            values = jnp.concatenate(pair, axis=0)
+            ends = lax.rem(lane_ids(values.shape), jnp.int32(BATCH)) == BATCH - 1
+            moved = jnp.where(ends, 0.0, pltpu.roll(values, LANES - 1, 1))
+            columns.append(jnp.concatenate(split(moved) + split(values), axis=0))
         product = jnp.dot(weights[...], jnp.concatenate(columns, axis=1), preferred_element_type=F32)
         sums = []
         for i in range(len(halves)):
-            total = zero
-            for b in range(1, BATCH + 1):
-                block = product[(b - 1) * phases:b * phases, i * LANES:(i + 1) * LANES]
-                total = total + jnp.where(group_lane < b, pltpu.roll(block, (b - BATCH) % LANES, 1), 0.0)
+            total = product[(BATCH // 2 - 1) * phases:(BATCH // 2) * phases, i * LANES:(i + 1) * LANES]
+            for j in range(BATCH // 2 - 1):
+                block = product[j * phases:(j + 1) * phases, i * LANES:(i + 1) * LANES]
+                moved = pltpu.roll(block, (2 * j + 2 - BATCH) % LANES, 1)
+                total = total + jnp.where(group_lane <= 2 * j + 1, moved, 0.0)
             sums.append(total)
         return sums
 
@@ -422,27 +433,19 @@
         )
         corner = jnp.where(lane == LANES - 1, corner, 0.0) * serve_one
         shifted = jnp.where(lane == LANES - 1, 0.0, pltpu.roll(left, LANES - 1, 1)) * serve_one
-        own_column = columns_own[sh.at(unit * phases), :] * serve_one
         below_local, below_remote = number(kind(BELOW) == 1), number(kind(BELOW) > 1)
-        under, mine = [], []
+        under = []
         for part in range(sh.rim_parts):
             under.append([
                 rims_own[sh.rim_at(beside(BELOW), part), :] * below_local + rim_got[sh.rim_at(s, part), :] * below_remote,
                 rims_other[sh.rim_at(beside(BELOW), part), :] * below_local
                 + rim_other[sh.rim_at(s, part), :] * below_remote,
             ])
-            mine.append([rims_own[sh.rim_at(unit, part), :], rims_other[sh.rim_at(unit, part), :]])
         feed = rates[s, FEED]
-        if group is None:
-            rims = rim_product([[p - q for p, q in zip(*both)] for both in zip(under, mine)])
-        else:
-            sums = rim_product(under + mine)
-            reach, wrap = sums[:sh.rim_parts], sums[sh.rim_parts:]
-            rims = [p - q for p, q in zip(reach, wrap)]
-            drop = jnp.float32(0.0 if group == "raw" else 1.0)
+        rims = rim_product(under)
+        if group is not None:
             keep_left = kept(LEFT)
-            sent_rims = [2.0 * (kept(BELOW) * p - drop * q) for p, q in zip(reach, wrap)]
-            sent_column = 2.0 * (kept(ABOVE) * above - drop * own_column)
+            rim_scale, column_scale = 2.0 * kept(BELOW), 2.0 * kept(ABOVE)
             sent_first = (2.0 * keep_left) * (shifted + feed * left) + (2.0 * kept(CORNER)) * corner
             sent_first = sent_first + ((2.0 * keep_left - 1.0) * rates[s, FEED_MORE]) * left
             sent_last = (2.0 * kept(RIGHT) * serve_two) * right
@@ -450,23 +453,18 @@
                 sent[sh.at(sh.ends_at + 2 * unit * phases), :] = sent_first
                 sent[sh.at(sh.ends_at + (2 * unit + 1) * phases), :] = sent_last
                 for part in range(sh.rim_parts):
-                    sent[sh.at(sh.rims_at + (unit * sh.rim_parts + part) * phases), :] = sent_rims[part]
+                    sent[sh.at(sh.rims_at + (unit * sh.rim_parts + part) * phases), :] = rim_scale * rims[part]
                 place = sh.at(sh.columns_at + lax.div(unit, jnp.int32(sh.per_column)) * phases)
                 base = lax.rem(unit, jnp.int32(sh.per_column)) * sh.wide_two
-                sent[place, :] = sent[place, :] + pltpu.roll(sent_column, base, 1)
-        column = above - own_column
+                sent[place, :] = sent[place, :] + column_scale * pltpu.roll(above, base, 1)
         packed, packed_column = [zero] * sh.rim_parts, zero
         for u in range(sh.wide_two):
             part, q = u // sh.rim_group, u % sh.rim_group
 
-            def unpacked(rims, column):
-                value = jnp.where(lane < BATCH, pltpu.roll(rims[part], LANES - q * BATCH, 1) if q else rims[part], 0.0)
-                if u:
-                    value = jnp.where(lane == LANES - 1, pltpu.roll(column, LANES - u, 1), value)
-                return value
-
             inside = inner[sh.by_level(unit, u), :]
-            total = inside + unpacked(rims, column)
+            rim = jnp.where(lane < BATCH, pltpu.roll(rims[part], LANES - q * BATCH, 1) if q else rims[part], 0.0)
+            edge = jnp.where(lane == LANES - 1, pltpu.roll(above, LANES - u, 1), 0.0) if u else zero
+            total = inside + rim + edge
             if u == 0:
                 total = total + shifted + corner + feed * left
             if u == last_u:
@@ -489,7 +487,8 @@
             else:
                 out[sh.native(unit, u), :] = jnp.where(plan[k, TILE] >= 0, total, 0.0)
             if group == "last":
-                value = 2.0 * inside + unpacked(sent_rims, sent_column) + rates[s, STAY_MORE] * own[sh.by_level(unit, u), :]
+                value = 2.0 * inside + rim_scale * rim + column_scale * edge
+                value = value + rates[s, STAY_MORE] * own[sh.by_level(unit, u), :]
                 if u:
                     value = value + rates[s, FEED_MORE] * own[sh.by_level(unit, u - 1), :]
                 else:
@@ -503,11 +502,15 @@
             columns_out[sh.at(unit * phases), :] = packed_column
 
     def sweep(start, stop, group, mark=None):
-        def step(unit, carry):
-            unit_step(group, unit, mark)
+        wished = 2 if first else 4
+        many = wished if (stop - start) % wished == 0 else 1
+
+        def step(index, carry):
+            for j in range(many):
+                unit_step(group, start + index * many + j, mark)
             return carry
 
-        lax.fori_loop(start, stop, step, 0)
+        lax.fori_loop(0, (stop - start) // many, step, 0)
 
     if sent is not None:
         sweep(0, sh.raw_end, "raw")
@@ -613,13 +616,13 @@
     if sh.deferred:
         raw_got, outs = from_partner(outs[0], "src", 0), outs[1:]
     start, rims, columns, messages = outs[0], outs[1], outs[2], outs[3:]
-    plan, rates, paired, single, exits = call(
+    plan, rates, paired, rim_paired, exits = call(
         functools.partial(prep_kernel, sh),
         [routes, tile_owner, tile_levels, service_rates, source_rates],
         [phase_rates, batch_rates],
         [
             table((BATCH // 2 + 1) * sh.phases, 6 * full, BF16),
-            table(BATCH * sh.phases, 3 * full, BF16),
+            table((BATCH // 2) * sh.phases, 6 * full, BF16),
             array(sh.phases),
         ],
         2,
@@ -637,10 +640,11 @@
         shapes = [array(sh.rows)]
         if first:
             shapes += ([array(sh.late_rows)] if sh.deferred else []) + packed_shapes
+        rims_other = from_next(rims, "phase")
         return call(
             functools.partial(halo_kernel, sh, first),
             [plan, rates] + ([send_plan] if first else []),
-            [single, inside, values, rims, from_next(rims, "phase"), columns] + got + extra,
+            [rim_paired, inside, values, rims, rims_other, columns] + got + extra,
             shapes,
             4,
         )
@@ -652,7 +656,8 @@
         outs = halo(True, inside, start, rims, columns, got, [raw_got])
         once, late, rims, columns, messages = outs[0], outs[1], outs[2], outs[3], outs[4:]
         got_late = from_partner(late, "src", 0)
-        (inside,) = inner(False, once, from_next(once, "phase"))
+        other = from_next(once, "phase")
+        (inside,) = inner(False, once, other)
         got, inside = exchange(messages, inside)
         (twice,) = halo(False, inside, once, rims, columns, got, [raw_got, start])
         (result,) = call(
@@ -682,6 +687,7 @@
         P("groups", None),
         P("groups"),
     )
+
     return jax.shard_map(
         body,
         mesh=mesh,

time: 70 us -> 67.3 us (0.961)
  Pallas kernels: 38.2 us -> 33.5 us
  waiting for transfers between devices: 11.9 us -> 13.9 us
    pallas_call x7, Pallas kernels: 38.2 us -> 33.5 us  [call(): pl.pallas_call(kernel, out_shape=tuple(scalar_shapes) + tuple(shapes), in...]
    ppermute x15, waiting for transfers between devices: 11.9 us -> 13.9 us  [permute(): lax.ppermute(x, axis, [(i, pairs_of(i)) for i in range(lax.axis_size(axis...]
  transfers between devices with their start and end apart: 15 -> 15, of which waited for: 5 -> 5; matrix products, arithmetic and copies ran while one was open for 1% -> 1% of each run, Pallas kernels for 40% -> 38%
where the time goes in v3:
time: 67.3 us; the launch traced here: 66.9 us
  Pallas kernels  33.5 us (50%)
  starting transfers between devices  15.8 us (23%)
  waiting for transfers between devices  13.9 us (21%)
  local copies, waits for them, and re-layouts  3.52 us (5%)
    pallas_call x7, Pallas kernels, call(): pl.pallas_call(kernel, out_shape=tuple(scalar_shapes) + tuple(shapes), in...  33.5 us
    ppermute x15, starting transfers between devices, permute(): lax.ppermute(x, axis, [(i, pairs_of(i)) for i in range(lax.axis_size(axis...  15.8 us
    ppermute x15, waiting for transfers between devices, permute(): lax.ppermute(x, axis, [(i, pairs_of(i)) for i in range(lax.axis_size(axis...  13.9 us
    unnamed x19, local copies, waits for them, and re-layouts  3.52 us
  transfers between devices with their start and end apart: 15, of which 5 were waited for; matrix products, arithmetic and copies ran while one was open for 1% of the time, Pallas kernels for 38%

profile of v3, /device:TPU:0, one launch (start us, length us, event | category | flops | bytes accessed | tf_op | source)
XLA Modules:
  0.0 66.9 jit_solution(17238619489147991620)
XLA Ops:
  0.0 0.5 collective-permute-start.3
  0.5 1.4 %copy-done = f32[3,4,16,16,128]{4,3,2,1,0:T(8,128)S(1)} copy-done((f32[3,4,16,16,128]{4,3,2,1,0:T(8,128)S(1)}, f32[3,4,16,16,128]{4,3,2,1,0:T(8,128)}, u32[]{:S(2)}) %copy-start) | copy-done | bytes 1572888
  1.9 0.7 %copy-done.2 = s32[8,5]{1,0:T(8,128)S(1)} copy-done((s32[8,5]{1,0:T(8,128)S(1)}, s32[8,5]{1,0:T(8,128)}, u32[]{:S(2)}) %copy-start.2) | copy-done | bytes 184
  2.6 0.7 copy-done.6
  3.3 3.4 %shard_map.83 = (s32[3,9]{1,0:T(4,128)S(1)}, f32[1024,128]{1,0:T(8,128)}, f32[3072,128]{1,0:T(8,128)S(1)}, f32[384,128]{1,0:T(8,128)S(1)}, f32[192,128]{1,0:T(8,...) custom-call(s32[8,5]{1,0:T(8,128)S(1)} %copy-done.2, s32[8]{0:T(128)S(1)} %copy-done.6, ...), custom_call_target="tpu_custom_call" | custom-call | bytes 9000000 | tf_op jit(solution)/shard_map/pallas_call | solution.py:585
  6.7 2.6 %collective-permute-start.6 = (f32[1024,128]{1,0:T(8,128)}, f32[1024,128]{1,0:T(8,128)S(1)}, u32[]{:S(2)}, u32[]{:S(2)}) collective-permute-start(f32[1024,128]{1,0:T(8,128)} %get-tuple-element.52), channel_id=1, source_target_pairs={{0,2},{2,0},{1,3},{3,1},{4,6},{6,4},{5,7},{7,5},{8,10},{10,8},{9,1... | collective-permute-start | bytes 1572872 | tf_op jit(solution)/shard_map/ppermute | solution.py:28
  9.2 1.6 %collective-permute-start = (f32[336,128]{1,0:T(8,128)}, f32[336,128]{1,0:T(8,128)S(1)}, u32[]{:S(2)}, u32[]{:S(2)}) collective-permute-start(f32[336,128]{1,0:T(8,128)} %get-tuple-element.39), channel_id=1, source_target_pairs={{0,4},{4,0},{8,12},{12,8},{1,5},{5,1},{9,13},{13,9},{2,6},{6,2},{1... | collective-permute-start | bytes 516104 | tf_op jit(solution)/shard_map/ppermute | solution.py:28
  10.8 2.6 %collective-permute-start.1 = (f32[336,128]{1,0:T(8,128)S(1)}, f32[336,128]{1,0:T(8,128)S(1)}, u32[]{:S(2)}, u32[]{:S(2)}) collective-permute-start(f32[336,128]{1,0:T(8,128)S(1)} %get-tuple-element.40), channel_id=1, source_target_pairs={{0,8},{4,12},{8,0},{12,4},{1,9},{5,13},{9,1},{13,5},{2,10},{6,14},... | collective-permute-start | bytes 516104 | tf_op jit(solution)/shard_map/ppermute | solution.py:28
  13.4 0.2 collective-permute-start.2
  13.6 0.8 %copy.9.levels_t = s32[8,2]{1,0:T(8,128)S(1)} copy(s32[8,2]{0,1:T(2,128)} %param.13) | data formatting | bytes 128 | tf_op args[5]
  14.4 2.6 %shard_map.82 = (s32[3,18]{1,0:T(4,128)S(1)}, f32[5,8]{1,0:T(8,128)S(1)}, bf16[144,192]{1,0:T(8,128)(2,1)S(1)}, bf16[128,192]{1,0:T(8,128)(2,1)S(1)}, f32[16,128]{1,0:T(8,128)S(1)}) custom-call(s32[8,5]{1,0:T(8,128)S(1)} %copy-done.3, s32[8]{0:T(128)S(1)} %copy-done.7, s32[8,2]{1,0:T(8,128)S(1)} %copy.9.levels_t, f32[2]{0:T(128)S(1)} %copy-done.8, ...), custom_call_target="tpu_custom_call" | custom-call | bytes 6000000 | tf_op jit(solution)/shard_map/pallas_call | solution.py:585
  17.1 0.1 collective-permute-start.4
  17.1 8.7 %shard_map.84 = (f32[3072,128]{1,0:T(8,128)S(1)}, f32[1024,128]{1,0:T(8,128)S(1)}) custom-call(s32[3,18]{1,0:T(4,128)S(1)} %get-tuple-element.35.plan.refs_0_, f32[5,8]{1,0:T(8,128)S(1)} %get-tuple-element.36.rates.refs_1_, bf16[144,192]{1,0:T(8,128)(2,1)S(1)} %get-tuple-element.42.weights, f32[16,128]{1,0:T(8,128)S(1)} %get-tuple-element.43.exits, ...), custom_call_target="tpu_custom_call" | custom-call | bytes 27000000 | tf_op jit(solution)/shard_map/pallas_call | solution.py:585
  25.9 0.0 collective-permute-done.refs_11_
  25.9 0.5 collective-permute-done.1.refs_12_
  26.3 0.1 collective-permute-start.5
  26.5 1.2 %collective-permute-done.5.refs_10_ = f32[128,128]{1,0:T(8,128)S(1)} collective-permute-done((f32[128,128]{1,0:T(8,128)S(1)}, f32[128,128]{1,0:T(8,128)S(1)}, u32[]{:S(2)}, u32[]{:S(2)}) %collective-permute-start.5) | collective-permute-done | bytes 65568 | tf_op jit(solution)/shard_map/ppermute | solution.py:28
  27.7 4.7 %shard_map.85 = (f32[3072,128]{1,0:T(8,128)S(1)}, f32[1552,128]{1,0:T(8,128)S(1)}, f32[384,128]{1,0:T(8,128)S(1)}, f32[192,128]{1,0:T(8,128)S(1)}, f32[336,128]{...) custom-call(s32[3,18]{1,0:T(4,128)S(1)} %get-tuple-element.35.plan.refs_0_, ...), custom_call_target="tpu_custom_call" | custom-call | bytes 12000000 | tf_op jit(solution)/shard_map/pallas_call | solution.py:585
  32.4 0.2 collective-permute-start.10
  32.6 0.5 collective-permute-start.14
  33.1 1.5 %collective-permute-start.13 = (f32[1024,128]{1,0:T(8,128)S(1)}, f32[1024,128]{1,0:T(8,128)S(1)}, u32[]{:S(2)}, u32[]{:S(2)}) collective-permute-start(f32[1024,128]{1,0:T(8,128)S(1)} %get-tuple-element.63), channel_id=1, source_target_pairs={{0,2},{2,0},{1,3},{3,1},{4,6},{6,4},{5,7},{7,5},{8,10},{10,8},{9,1... | collective-permute-start | bytes 1572872 | tf_op jit(solution)/shard_map/ppermute | solution.py:28
  34.6 3.2 %collective-permute-start.7 = (f32[336,128]{1,0:T(8,128)S(1)}, f32[336,128]{1,0:T(8,128)S(1)}, u32[]{:S(2)}, u32[]{:S(2)}) collective-permute-start(f32[336,128]{1,0:T(8,128)S(1)} %get-tuple-element.53), channel_id=1, source_target_pairs={{0,4},{4,0},{8,12},{12,8},{1,5},{5,1},{9,13},{13,9},{2,6},{6,2},{1... | collective-permute-start | bytes 516104 | tf_op jit(solution)/shard_map/ppermute | solution.py:28
  37.9 1.0 %collective-permute-start.8 = (f32[336,128]{1,0:T(8,128)S(1)}, f32[336,128]{1,0:T(8,128)S(1)}, u32[]{:S(2)}, u32[]{:S(2)}) collective-permute-start(f32[336,128]{1,0:T(8,128)S(1)} %get-tuple-element.54), channel_id=1, source_target_pairs={{0,8},{4,12},{8,0},{12,4},{1,9},{5,13},{9,1},{13,5},{2,10},{6,14},... | collective-permute-start | bytes 516104 | tf_op jit(solution)/shard_map/ppermute | solution.py:28
  38.9 1.5 %collective-permute-start.9 = (f32[336,128]{1,0:T(8,128)S(1)}, f32[336,128]{1,0:T(8,128)S(1)}, u32[]{:S(2)}, u32[]{:S(2)}) collective-permute-start(f32[336,128]{1,0:T(8,128)S(1)} %get-tuple-element.55), channel_id=1, source_target_pairs={{0,12},{4,8},{8,4},{12,0},{1,13},{5,9},{9,5},{13,1},{2,14},{6,10},... | collective-permute-start | bytes 516104 | tf_op jit(solution)/shard_map/ppermute | solution.py:28
  40.4 8.1 %shard_map.86.refs_3_ = f32[3072,128]{1,0:T(8,128)S(1)} custom-call(s32[3,18]{1,0:T(4,128)S(1)} %get-tuple-element.35.plan.refs_0_, f32[5,8]{1,0:T(8,128)S(1)} %get-tuple-element.36.rates.refs_1_, bf16[144,192]{1,0:T(8,128)(2,1)S(1)} %get-tuple-element.42.weights, f32[16,128]{1,0:T(8,128)S(1)} %get-tuple-element.43.exits, ...), custom_call_target="tpu_custom_call" | custom-call | bytes 27000000 | tf_op jit(solution)/shard_map/pallas_call | solution.py:585
  48.5 0.1 collective-permute-start.11
  48.6 4.8 %collective-permute-done.8.refs_11_ = f32[336,128]{1,0:T(8,128)S(1)} collective-permute-done((f32[336,128]{1,0:T(8,128)S(1)}, f32[336,128]{1,0:T(8,128)S(1)}, u32[]{:S(2)}, u32[]{:S(2)}) %collective-permute-start.8) | collective-permute-done | bytes 172064 | tf_op jit(solution)/shard_map/ppermute | solution.py:28
  53.4 0.1 collective-permute-start.12
  53.5 1.2 %collective-permute-done.12.refs_9_ = f32[128,128]{1,0:T(8,128)S(1)} collective-permute-done((f32[128,128]{1,0:T(8,128)S(1)}, f32[128,128]{1,0:T(8,128)S(1)}, u32[]{:S(2)}, u32[]{:S(2)}) %collective-permute-start.12) | collective-permute-done | bytes 65568 | tf_op jit(solution)/shard_map/ppermute | solution.py:28
  54.7 2.9 %shard_map.87.stepped = f32[3072,128]{1,0:T(8,128)S(1)} custom-call(s32[3,18]{1,0:T(4,128)S(1)} %get-tuple-element.35.plan.refs_0_, f32[5,8]{1,0:T(8,128)S(1)} %get-tuple-element.36.rates.refs_1_, bf16[128,192]{1,0:T(8,128)(2,1)S(1)} %get-tuple-element.37.refs_3_.refs_2_, f32[3072,128]{1,0:T(8,128)S(1)} %shard_map.86.refs_3_, ...), custom_call_target="tpu_custom_call" | custom-call | bytes 12000000 | tf_op jit(solution)/shard_map/pallas_call | solution.py:585
  57.6 6.2 %collective-permute-done.13.got_mid = f32[1024,128]{1,0:T(8,128)S(1)} collective-permute-done((f32[1024,128]{1,0:T(8,128)S(1)}, f32[1024,128]{1,0:T(8,128)S(1)}, u32[]{:S(2)}, u32[]{:S(2)}) %collective-permute-start.13) | collective-permute-done | bytes 524320 | tf_op jit(solution)/shard_map/ppermute | solution.py:28
  63.8 3.1 %shard_map.88 = f32[3072,128]{1,0:T(8,128)} custom-call(s32[3,18]{1,0:T(4,128)S(1)} %get-tuple-element.35.plan.refs_0_, f32[5,8]{1,0:T(8,128)S(1)} %get-tuple-element.36.rates.refs_1_, f32[3072,128]{1,0:T(8,128)S(1)} %shard_map.87.stepped, f32[1024,128]{1,0:T(8,128)S(1)} %collective-permute-done.13.got_mid, f32[1552,128]{1,0:T(8,128)S(1)} %collective-permute-done.14.got_late), custom_call_target="tpu_custom_call" | custom-call | bytes 9000000 | tf_op jit(solution)/shard_map/pallas_call | solution.py:585
  (26 shorter events, 0.1 us)
Async XLA Ops:
  0.0 14.4 %copy-start.7 = (s32[8]{0:T(128)S(1)}, s32[8]{0:T(128)}, u32[]{:S(2)}) copy-start(s32[8]{0:T(128)} %owner.3) | copy-start | bytes 100
  0.0 14.4 %copy-start.8 = (f32[2]{0:T(128)S(1)}, f32[2]{0:T(128)}, u32[]{:S(2)}) copy-start(f32[2]{0:T(128)} %service.1) | copy-start | bytes 28
  0.0 17.1 %collective-permute-start.3 = (f32[3072,128]{1,0:T(8,128)}, f32[3072,128]{1,0:T(8,128)}, u32[]{:S(2)}, u32[]{:S(2)}) collective-permute-start(f32[3072,128]{1,0:T(8,128)} %bitcast.2), channel_id=1, source_target_pairs={{0,1},{1,0},{2,3},{3,2},{4,5},{5,4},{6,7},{7,6},{8,9},{9,8},{10,11... | collective-permute-start | bytes 4718600 | tf_op jit(solution)/shard_map/ppermute | solution.py:28
  0.5 1.4 %copy-start = (f32[3,4,16,16,128]{4,3,2,1,0:T(8,128)S(1)}, f32[3,4,16,16,128]{4,3,2,1,0:T(8,128)}, u32[]{:S(2)}) copy-start(f32[3,4,16,16,128]{4,3,2,1,0:T(8,128)} %param.8) | copy-start | bytes 4718596
  1.9 0.7 %copy-start.2 = (s32[8,5]{1,0:T(8,128)S(1)}, s32[8,5]{1,0:T(8,128)}, u32[]{:S(2)}) copy-start(s32[8,5]{1,0:T(8,128)} %routes.3) | copy-start | bytes 484
  2.6 0.7 copy-start.6
  3.2 11.1 %copy-start.1 = (f32[16,32,32]{2,1,0:T(8,128)S(1)}, f32[16,32,32]{2,1,0:T(8,128)}, u32[]{:S(2)}) copy-start(f32[16,32,32]{2,1,0:T(8,128)} %batch_rates.1) | copy-start | bytes 196612
  3.3 11.1 %copy-start.3 = (s32[8,5]{1,0:T(8,128)S(1)}, s32[8,5]{1,0:T(8,128)}, u32[]{:S(2)}) copy-start(s32[8,5]{1,0:T(8,128)} %routes.3) | copy-start | bytes 484
  3.3 11.1 %copy-start.4 = (f32[32,32]{1,0:T(8,128)S(1)}, f32[32,32]{1,0:T(8,128)}, u32[]{:S(2)}) copy-start(f32[32,32]{1,0:T(8,128)} %phase_rates.1) | copy-start | bytes 12292
  3.3 11.1 %copy-start.5 = (f32[3,3]{1,0:T(4,128)S(1)}, f32[3,3]{1,0:T(4,128)}, u32[]{:S(2)}) copy-start(f32[3,3]{1,0:T(4,128)} %sources.1) | copy-start | bytes 112
  6.7 19.8 %collective-permute-start.6 = (f32[1024,128]{1,0:T(8,128)}, f32[1024,128]{1,0:T(8,128)S(1)}, u32[]{:S(2)}, u32[]{:S(2)}) collective-permute-start(f32[1024,128]{1,0:T(8,128)} %get-tuple-element.52), channel_id=1, source_target_pairs={{0,2},{2,0},{1,3},{3,1},{4,6},{6,4},{5,7},{7,5},{8,10},{10,8},{9,1... | collective-permute-start | bytes 1572872 | tf_op jit(solution)/shard_map/ppermute | solution.py:28
  9.2 16.6 %collective-permute-start = (f32[336,128]{1,0:T(8,128)}, f32[336,128]{1,0:T(8,128)S(1)}, u32[]{:S(2)}, u32[]{:S(2)}) collective-permute-start(f32[336,128]{1,0:T(8,128)} %get-tuple-element.39), channel_id=1, source_target_pairs={{0,4},{4,0},{8,12},{12,8},{1,5},{5,1},{9,13},{13,9},{2,6},{6,2},{1... | collective-permute-start | bytes 516104 | tf_op jit(solution)/shard_map/ppermute | solution.py:28
  10.8 15.5 %collective-permute-start.1 = (f32[336,128]{1,0:T(8,128)S(1)}, f32[336,128]{1,0:T(8,128)S(1)}, u32[]{:S(2)}, u32[]{:S(2)}) collective-permute-start(f32[336,128]{1,0:T(8,128)S(1)} %get-tuple-element.40), channel_id=1, source_target_pairs={{0,8},{4,12},{8,0},{12,4},{1,9},{5,13},{9,1},{13,5},{2,10},{6,14},... | collective-permute-start | bytes 516104 | tf_op jit(solution)/shard_map/ppermute | solution.py:28
  13.4 12.9 %collective-permute-start.2 = (f32[336,128]{1,0:T(8,128)S(1)}, f32[336,128]{1,0:T(8,128)S(1)}, u32[]{:S(2)}, u32[]{:S(2)}) collective-permute-start(f32[336,128]{1,0:T(8,128)S(1)} %get-tuple-element.41), channel_id=1, source_target_pairs={{0,12},{4,8},{8,4},{12,0},{1,13},{5,9},{9,5},{13,1},{2,14},{6,10},... | collective-permute-start | bytes 516104 | tf_op jit(solution)/shard_map/ppermute | solution.py:28
  17.1 9.4 %collective-permute-start.4 = (f32[384,128]{1,0:T(8,128)S(1)}, f32[384,128]{1,0:T(8,128)S(1)}, u32[]{:S(2)}, u32[]{:S(2)}) collective-permute-start(f32[384,128]{1,0:T(8,128)S(1)} %get-tuple-element.47.refs_6_), channel_id=1, source_target_pairs={{0,1},{1,0},{2,3},{3,2},{4,5},{5,4},{6,7},{7,6},{8,9},{9,8},{10,11... | collective-permute-start | bytes 589832 | tf_op jit(solution)/shard_map/ppermute | solution.py:28
  26.3 1.3 %collective-permute-start.5 = (f32[128,128]{1,0:T(8,128)S(1)}, f32[128,128]{1,0:T(8,128)S(1)}, u32[]{:S(2)}, u32[]{:S(2)}) collective-permute-start(f32[128,128]{1,0:T(8,128)S(1)} %slice_add_fusion.1.refs_9_), channel_id=1, source_target_pairs={{0,1},{1,0},{2,3},{3,2},{4,5},{5,4},{6,7},{7,6},{8,9},{9,8},{10,11... | collective-permute-start | bytes 196616 | tf_op jit(solution)/shard_map/ppermute | solution.py:28
  32.4 6.5 %collective-permute-start.10 = (f32[3072,128]{1,0:T(8,128)S(1)}, f32[3072,128]{1,0:T(8,128)S(1)}, u32[]{:S(2)}, u32[]{:S(2)}) collective-permute-start(f32[3072,128]{1,0:T(8,128)S(1)} %get-tuple-element.56.own.refs_4_), channel_id=1, source_target_pairs={{0,1},{1,0},{2,3},{3,2},{4,5},{5,4},{6,7},{7,6},{8,9},{9,8},{10,11... | collective-permute-start | bytes 4718600 | tf_op jit(solution)/shard_map/ppermute | solution.py:28
  32.6 31.2 %collective-permute-start.14 = (f32[1552,128]{1,0:T(8,128)S(1)}, f32[1552,128]{1,0:T(8,128)S(1)}, u32[]{:S(2)}, u32[]{:S(2)}) collective-permute-start(f32[1552,128]{1,0:T(8,128)S(1)} %get-tuple-element.64), channel_id=1, source_target_pairs={{0,2},{2,0},{1,3},{3,1},{4,6},{6,4},{5,7},{7,5},{8,10},{10,8},{9,1... | collective-permute-start | bytes 2383880 | tf_op jit(solution)/shard_map/ppermute | solution.py:28
  33.1 30.7 %collective-permute-start.13 = (f32[1024,128]{1,0:T(8,128)S(1)}, f32[1024,128]{1,0:T(8,128)S(1)}, u32[]{:S(2)}, u32[]{:S(2)}) collective-permute-start(f32[1024,128]{1,0:T(8,128)S(1)} %get-tuple-element.63), channel_id=1, source_target_pairs={{0,2},{2,0},{1,3},{3,1},{4,6},{6,4},{5,7},{7,5},{8,10},{10,8},{9,1... | collective-permute-start | bytes 1572872 | tf_op jit(solution)/shard_map/ppermute | solution.py:28
  34.6 13.8 %collective-permute-start.7 = (f32[336,128]{1,0:T(8,128)S(1)}, f32[336,128]{1,0:T(8,128)S(1)}, u32[]{:S(2)}, u32[]{:S(2)}) collective-permute-start(f32[336,128]{1,0:T(8,128)S(1)} %get-tuple-element.53), channel_id=1, source_target_pairs={{0,4},{4,0},{8,12},{12,8},{1,5},{5,1},{9,13},{13,9},{2,6},{6,2},{1... | collective-permute-start | bytes 516104 | tf_op jit(solution)/shard_map/ppermute | solution.py:28
  37.9 15.5 %collective-permute-start.8 = (f32[336,128]{1,0:T(8,128)S(1)}, f32[336,128]{1,0:T(8,128)S(1)}, u32[]{:S(2)}, u32[]{:S(2)}) collective-permute-start(f32[336,128]{1,0:T(8,128)S(1)} %get-tuple-element.54), channel_id=1, source_target_pairs={{0,8},{4,12},{8,0},{12,4},{1,9},{5,13},{9,1},{13,5},{2,10},{6,14},... | collective-permute-start | bytes 516104 | tf_op jit(solution)/shard_map/ppermute | solution.py:28
  38.9 14.5 %collective-permute-start.9 = (f32[336,128]{1,0:T(8,128)S(1)}, f32[336,128]{1,0:T(8,128)S(1)}, u32[]{:S(2)}, u32[]{:S(2)}) collective-permute-start(f32[336,128]{1,0:T(8,128)S(1)} %get-tuple-element.55), channel_id=1, source_target_pairs={{0,12},{4,8},{8,4},{12,0},{1,13},{5,9},{9,5},{13,1},{2,14},{6,10},... | collective-permute-start | bytes 516104 | tf_op jit(solution)/shard_map/ppermute | solution.py:28
  48.5 5.0 %collective-permute-start.11 = (f32[384,128]{1,0:T(8,128)S(1)}, f32[384,128]{1,0:T(8,128)S(1)}, u32[]{:S(2)}, u32[]{:S(2)}) collective-permute-start(f32[384,128]{1,0:T(8,128)S(1)} %get-tuple-element.58.refs_5_), channel_id=1, source_target_pairs={{0,1},{1,0},{2,3},{3,2},{4,5},{5,4},{6,7},{7,6},{8,9},{9,8},{10,11... | collective-permute-start | bytes 589832 | tf_op jit(solution)/shard_map/ppermute | solution.py:28
  53.4 1.3 %collective-permute-start.12 = (f32[128,128]{1,0:T(8,128)S(1)}, f32[128,128]{1,0:T(8,128)S(1)}, u32[]{:S(2)}, u32[]{:S(2)}) collective-permute-start(f32[128,128]{1,0:T(8,128)S(1)} %slice_add_fusion.refs_8_), channel_id=1, source_target_pairs={{0,1},{1,0},{2,3},{3,2},{4,5},{5,4},{6,7},{7,6},{8,9},{9,8},{10,11... | collective-permute-start | bytes 196616 | tf_op jit(solution)/shard_map/ppermute | solution.py:28

commit v4 on v3

--- a/solution.py
+++ b/solution.py
@@ -17,6 +17,7 @@
 VM = pltpu.VMEM
 SM = pltpu.SMEM
 GRANT = 24 << 20
+PACK_TURN, JOIN_TURN = 4, 4
 
 FEED, STAY, FEED_MORE, STAY_MORE, SQUARE, INFLOW = 0, 1, 2, 3, 4, 5
 TILE, LEVEL_ONE, LEVEL_TWO, ROUTES = 0, 1, 2, 3
@@ -92,6 +93,17 @@
         return me ^ step if self.power else (me + self.levels - step) % self.levels
 
 
+def sweep(start, stop, wished, visit):
+    many = wished if (stop - start) % wished == 0 else 1
+
+    def turn(index, carry):
+        for j in range(many):
+            visit(start + index * many + j)
+        return carry
+
+    lax.fori_loop(0, (stop - start) // many, turn, 0)
+
+
 def lane_ids(shape):
     return lax.broadcasted_iota(I32, shape, len(shape) - 1)
 
@@ -176,12 +188,20 @@
             messages[step - 1][sh.at(sh.small_rows_at + i * phases), :] = values
 
 
-def pack_kernel(sh, routes, owner, data, send_plan, *outs):
+def pack_kernel(sh, routes, owner, data_hbm, send_plan, *outs):
+    outs, (data, arrived) = outs[:-2], outs[-2:]
     raw, (by_level, rims, columns, *messages) = (outs[0], outs[1:]) if sh.deferred else (None, outs)
     lane = lane_ids((sh.phases, LANES))
+    size = sh.rows // sh.slots
+    copies = [
+        pltpu.make_async_copy(data_hbm.at[pl.ds(k * size, size)], data.at[pl.ds(k * size, size)], arrived.at[k])
+        for k in range(sh.slots)
+    ]
+    for copy in copies:
+        copy.start()
     fill_send_plan(sh, routes, owner, send_plan)
 
-    def reorder(to_src, unit, carry):
+    def reorder(to_src, unit):
         packed = [jnp.zeros((sh.phases, LANES), F32) for _ in range(sh.rim_parts)]
         column = jnp.zeros((sh.phases, LANES), F32)
         for u in range(sh.wide_two):
@@ -193,12 +213,10 @@
         for part, values in enumerate(packed):
             rims[sh.rim_at(unit, part), :] = values
         columns[sh.at(unit * sh.phases), :] = column
-        return carry
-
-    first = sh.raw_end if sh.deferred else 0
-    if sh.deferred:
-        lax.fori_loop(0, first, functools.partial(reorder, True), 0)
-    lax.fori_loop(first, sh.units, functools.partial(reorder, False), 0)
+
+    for k, copy in enumerate(copies):
+        copy.wait()
+        sweep(k * sh.states, (k + 1) * sh.states, PACK_TURN, functools.partial(reorder, sh.deferred and k == 0))
     write_messages(sh, send_plan, by_level, rims, columns, messages)
 
 
@@ -222,8 +240,8 @@
         tile = tile_at(owner, me * sh.slots + k, sh.tiles)
         known = jnp.maximum(tile, 0)
         plan[k, TILE] = tile
-        plan[k, LEVEL_ONE] = levels_t[known, 0]
-        plan[k, LEVEL_TWO] = levels_t[known, 1]
+        plan[k, LEVEL_ONE] = levels_t[0, known]
+        plan[k, LEVEL_TWO] = levels_t[1, known]
         for r in range(5):
             found, device, slot = route_of(routes, owner, tile, r, sh.slots)
             kind = jnp.int32(1)
@@ -296,17 +314,17 @@
     return [high, high, low]
 
 
-def inner_kernel(sh, first, plan, rates, weights, exits, own, other, *outs):
+def inner_kernel(sh, first, spans, plan, rates, weights, exits, own, other, *refs):
     phases = sh.phases
-    out = outs[0]
-    sent = outs[1] if first and sh.deferred else None
+    start_values, raw_got, got_mid = refs[:3] if sh.deferred and not first else (None, None, None)
+    out, sent = refs[-2:] if spans[0][0] == "sent" else (refs[-1], None)
     other_at = sh.native if first else sh.by_level
     serve_one, serve_two = rates[sh.states, 0], rates[sh.states, 1]
     lane = lane_ids((phases, LANES))
     inner_one = jnp.where(lane == LANES - 1, 0.0, serve_one)
     later = lane_ids((weights.shape[1] // 6, LANES)) > 0
 
-    def unit_step(sending, unit, carry):
+    def unit_step(group, unit):
         k = lax.div(unit, jnp.int32(sh.states))
         s = unit - k * sh.states
         a, c = plan[k, LEVEL_ONE], plan[k, LEVEL_TWO]
@@ -335,20 +353,24 @@
                 for bit in range(sh.bits):
                     flipped = unit - s + lax.bitwise_xor(s, jnp.int32(1 << bit))
                     total = total + rates[s, INFLOW + bit] * own[sh.by_level(flipped, u), :]
+                if start_values is not None:
+                    total = total + rates[s, SQUARE] * start_values[sh.by_level(unit, u), :]
+                    if group == "raw":
+                        more = rates[s, STAY_MORE] * raw_got[sh.by_level(unit, u), :]
+                        if u:
+                            more = more + rates[s, FEED_MORE] * raw_got[sh.by_level(unit, u - 1), :]
+                        total = total + rates[s, INFLOW + sh.bits] * more
+                    if group == "mid":
+                        total = total + rates[s, INFLOW + sh.bits] * got_mid[sh.by_level(unit - sh.raw_end, u), :]
                 out[sh.by_level(unit, u), :] = total
-                if sending:
+                if group == "sent":
                     more = rates[s, STAY_MORE] * here
                     if u:
                         more = more + rates[s, FEED_MORE] * prev
                     sent[sh.by_level(unit - sh.raw_end, u), :] = 2.0 * total + more
-        return carry
-
-    if sent is not None:
-        lax.fori_loop(sh.raw_end, sh.mid_end, functools.partial(unit_step, True), 0)
-        lax.fori_loop(0, sh.raw_end, functools.partial(unit_step, False), 0)
-        lax.fori_loop(sh.mid_end, sh.units, functools.partial(unit_step, False), 0)
-    else:
-        lax.fori_loop(0, sh.units, functools.partial(unit_step, False), 0)
+
+    for group, start, stop in spans:
+        sweep(start, stop, 1, functools.partial(unit_step, group))
 
 
 def halo_kernel(sh, first, *refs):
@@ -362,8 +384,7 @@
     edges, refs = refs[:n - 1], refs[n - 1:]
     raw = 0 if sh.deferred else sh.cross
     partners, refs = refs[:raw], refs[raw:]
-    raw_got = refs.pop(0) if sh.deferred else None
-    start_values = refs.pop(0) if sh.deferred and not first else None
+    raw_got = refs.pop(0) if sh.deferred and first else None
     out = refs.pop(0)
     sent = refs.pop(0) if sh.deferred and first else None
     rims_out, columns_out = (refs.pop(0), refs.pop(0)) if first else (None, None)
@@ -393,7 +414,7 @@
             sums.append(total)
         return sums
 
-    def unit_step(group, unit, carry):
+    def unit_step(group, unit):
         k = lax.div(unit, jnp.int32(sh.states))
         s = unit - k * sh.states
 
@@ -473,13 +494,6 @@
                 total = total + rates[s, INFLOW + sh.bits + bit] * values[sh.by_level(unit, u), :]
             if group == "raw":
                 total = total + (2.0 * rates[s, INFLOW + sh.bits]) * raw_got[sh.by_level(unit, u), :]
-            if start_values is not None:
-                total = total + rates[s, SQUARE] * start_values[sh.by_level(unit, u), :]
-            if raw_got is not None and carry == "raw":
-                more = rates[s, STAY_MORE] * raw_got[sh.by_level(unit, u), :]
-                if u:
-                    more = more + rates[s, FEED_MORE] * raw_got[sh.by_level(unit, u - 1), :]
-                total = total + rates[s, INFLOW + sh.bits] * more
             if first:
                 packed_column = add_packed(sh, lane, packed, packed_column, u, total)
             if first or sh.deferred:
@@ -501,36 +515,24 @@
                 rims_out[sh.rim_at(unit, part), :] = packed[part]
             columns_out[sh.at(unit * phases), :] = packed_column
 
-    def sweep(start, stop, group, mark=None):
-        wished = 2 if first else 4
-        many = wished if (stop - start) % wished == 0 else 1
-
-        def step(index, carry):
-            for j in range(many):
-                unit_step(group, start + index * many + j, mark)
-            return carry
-
-        lax.fori_loop(0, (stop - start) // many, step, 0)
+    turn = 2 if first else 4
 
     if sent is not None:
-        sweep(0, sh.raw_end, "raw")
-        sweep(sh.raw_end, sh.mid_end, "mid")
-        sweep(sh.mid_end, sh.units, "last")
-    elif sh.deferred:
-        sweep(0, sh.raw_end, None, "raw")
-        sweep(sh.raw_end, sh.units, None)
+        sweep(0, sh.raw_end, turn, functools.partial(unit_step, "raw"))
+        sweep(sh.raw_end, sh.mid_end, turn, functools.partial(unit_step, "mid"))
+        sweep(sh.mid_end, sh.units, turn, functools.partial(unit_step, "last"))
     else:
-        sweep(0, sh.units, None)
+        sweep(0, sh.units, turn, functools.partial(unit_step, None))
     if first:
         write_messages(sh, send_plan, out, rims_out, columns_out, refs)
 
 
-def join_kernel(sh, plan, rates, stepped, got_mid, got_late, out):
+def join_kernel(sh, plan, rates, stepped, got_late, out):
     phases, last_u = sh.phases, sh.wide_two - 1
     lane = lane_ids((phases, LANES))
     inflow = rates[0, INFLOW + sh.bits]
 
-    def unit_step(group, unit, carry):
+    def unit_step(group, unit):
         filled = plan[lax.div(unit, jnp.int32(sh.states)), TILE] >= 0
         if group != "last":
             rims = [
@@ -548,15 +550,11 @@
                     got = jnp.where(lane == LANES - 1, pltpu.roll(column, LANES - (base + u), 1), got)
                 if u in (0, last_u):
                     got = got + got_late[sh.at(sh.ends_at + (2 * unit + (1 if u else 0)) * phases), :]
-                if group == "mid":
-                    got = got + got_mid[sh.by_level(unit - sh.raw_end, u), :]
             total = stepped[sh.by_level(unit, u), :] + inflow * got
             out[sh.native(unit, u), :] = jnp.where(filled, total, 0.0)
-        return carry
-
-    lax.fori_loop(0, sh.raw_end, functools.partial(unit_step, "raw"), 0)
-    lax.fori_loop(sh.raw_end, sh.mid_end, functools.partial(unit_step, "mid"), 0)
-    lax.fori_loop(sh.mid_end, sh.units, functools.partial(unit_step, "last"), 0)
+
+    sweep(0, sh.mid_end, JOIN_TURN, functools.partial(unit_step, None))
+    sweep(sh.mid_end, sh.units, JOIN_TURN, functools.partial(unit_step, "last"))
 
 
 def body(
@@ -581,13 +579,14 @@
     def table(rows, columns, dtype=F32):
         return jax.ShapeDtypeStruct((rows, columns), dtype)
 
-    def call(kernel, scalars, arrays, shapes, micros, scalar_shapes=(), scratch=()):
+    def call(kernel, scalars, arrays, shapes, micros, scalar_shapes=(), scratch=(), space=VM, aliases=None):
         return pl.pallas_call(
             kernel,
             out_shape=tuple(scalar_shapes) + tuple(shapes),
-            in_specs=[smem] * len(scalars) + [vmem] * len(arrays),
+            in_specs=[smem] * len(scalars) + [pl.BlockSpec(memory_space=space)] * len(arrays),
             out_specs=tuple([smem] * len(scalar_shapes) + [vmem] * len(shapes)),
             scratch_shapes=list(scratch),
+            input_output_aliases=aliases or {},
             cost_estimate=pl.CostEstimate(flops=0, bytes_accessed=int(micros * 3.0e6), transcendentals=0),
             compiler_params=pltpu.CompilerParams(vmem_limit_bytes=GRANT),
         )(*scalars, *arrays)
@@ -598,28 +597,36 @@
         return permute(x, "level", lambda i: sh.sends_to(i, step))
 
     def exchange(messages, inside):
-        got = [along_level(messages[i], i + 1) for i in range(n - 1)]
+        got = []
+        for i in range(n - 1):
+            got.append(along_level(messages[i], i + 1))
         got, inside = lax.optimization_barrier((got, inside))
         rim_got = sum(values[:sh.state_rim_rows] for values in got)
         return [rim_got, from_next(rim_got, "phase")] + got, inside
 
     other = from_next(flat, "phase")
-    outs = call(
+
+    def in_hbm(values):
+        return [pltpu.with_memory_space_constraint(v, pltpu.HBM) for v in values]
+
+    routes, tile_owner, flat = in_hbm([routes, tile_owner, flat])
+    send_plan, *outs = call(
         functools.partial(pack_kernel, sh),
         [routes, tile_owner],
         [flat],
         ([array(sh.raw_rows)] if sh.deferred else []) + [array(sh.rows)] + packed_shapes,
         3,
         [table(n - 1, PICKS + 2 * sh.slots, I32)],
+        [VM((sh.rows, LANES), F32), pltpu.SemaphoreType.DMA((sh.slots,))],
+        pltpu.HBM,
     )
-    send_plan, outs = outs[0], outs[1:]
     if sh.deferred:
         raw_got, outs = from_partner(outs[0], "src", 0), outs[1:]
     start, rims, columns, messages = outs[0], outs[1], outs[2], outs[3:]
     plan, rates, paired, rim_paired, exits = call(
         functools.partial(prep_kernel, sh),
-        [routes, tile_owner, tile_levels, service_rates, source_rates],
-        [phase_rates, batch_rates],
+        [routes, tile_owner, *in_hbm([tile_levels.T, service_rates, source_rates])],
+        in_hbm([phase_rates, batch_rates]),
         [
             table((BATCH // 2 + 1) * sh.phases, 6 * full, BF16),
             table((BATCH // 2) * sh.phases, 6 * full, BF16),
@@ -630,11 +637,14 @@
         [VM((2 * full, full), F32), VM((full, LANES), F32)],
     )
 
-    def inner(first, values, other):
+    def inner(first, values, other, spans, extra=(), aliases=None):
         shapes = [array(sh.rows)]
-        if first and sh.deferred:
+        if spans[0][0] == "sent":
             shapes.append(array(sh.mid_rows))
-        return call(functools.partial(inner_kernel, sh, first), [plan, rates], [paired, exits, values, other], shapes, 9)
+        operands = [paired, exits, values, other, *extra]
+        micros = 9 * sum(stop - start for _, start, stop in spans) / sh.units
+        kernel = functools.partial(inner_kernel, sh, first, spans)
+        return call(kernel, [plan, rates], operands, shapes, micros, aliases=aliases)
 
     def halo(first, inside, values, rims, columns, got, extra):
         shapes = [array(sh.rows)]
@@ -650,26 +660,34 @@
         )
 
     if sh.deferred:
-        inside, mid = inner(True, start, other)
+        inside, mid = inner(True, start, other, [("sent", sh.raw_end, sh.mid_end)])
         got_mid = from_partner(mid, "src", 0)
+        spans = [(None, 0, sh.raw_end), (None, sh.mid_end, sh.units)]
+        (inside,) = inner(True, start, other, spans, [inside], {6: 0})
         got, inside = exchange(messages, inside)
         outs = halo(True, inside, start, rims, columns, got, [raw_got])
         once, late, rims, columns, messages = outs[0], outs[1], outs[2], outs[3], outs[4:]
         got_late = from_partner(late, "src", 0)
         other = from_next(once, "phase")
-        (inside,) = inner(False, once, other)
+        (inside,) = inner(
+            False,
+            once,
+            other,
+            [("raw", 0, sh.raw_end), ("mid", sh.raw_end, sh.mid_end), (None, sh.mid_end, sh.units)],
+            [start, raw_got, got_mid],
+        )
         got, inside = exchange(messages, inside)
-        (twice,) = halo(False, inside, once, rims, columns, got, [raw_got, start])
+        (twice,) = halo(False, inside, once, rims, columns, got, [])
         (result,) = call(
-            functools.partial(join_kernel, sh), [plan, rates], [twice, got_mid, got_late], [array(sh.rows)], 3
+            functools.partial(join_kernel, sh), [plan, rates], [twice, got_late], [array(sh.rows)], 3
         )
     else:
-        (inside,) = inner(True, start, other)
+        (inside,) = inner(True, start, other, [(None, 0, sh.units)])
         got, inside = exchange(messages, inside)
         extra = [from_partner(start, "src", bit) for bit in range(sh.cross)]
         outs = halo(True, inside, start, rims, columns, got, extra)
         once, rims, columns, messages = outs[0], outs[1], outs[2], outs[3:]
-        (inside,) = inner(False, once, from_next(once, "phase"))
+        (inside,) = inner(False, once, from_next(once, "phase"), [(None, 0, sh.units)])
         got, inside = exchange(messages, inside)
         extra = [from_partner(once, "src", bit) for bit in range(sh.cross)]
         (result,) = halo(False, inside, once, rims, columns, got, extra)

time: 67.3 us -> 64.2 us (0.954)
  local copies, waits for them, and re-layouts: 3.52 us -> 0 us
  starting transfers between devices: 15.8 us -> 17.6 us
  waiting for transfers between devices: 13.9 us -> 12.6 us
    unnamed x19 -> x0, local copies, waits for them, and re-layouts: 3.52 us -> none
    ppermute x15, starting transfers between devices: 15.8 us -> 17.6 us  [permute(): lax.ppermute(x, axis, [(i, pairs_of(i)) for i in range(lax.axis_size(axis...]
    ppermute x15, waiting for transfers between devices: 13.9 us -> 12.6 us  [permute(): lax.ppermute(x, axis, [(i, pairs_of(i)) for i in range(lax.axis_size(axis...]
    pallas_call x7 -> x8, Pallas kernels: 33.5 us -> 33.4 us  [call(): pl.pallas_call(kernel, out_shape=tuple(scalar_shapes) + tuple(shapes), in...]
  transfers between devices with their start and end apart: 15 -> 15, of which waited for: 5 -> 5; matrix products, arithmetic and copies ran while one was open for 1% -> 0% of each run, Pallas kernels for 38% -> 41%
where the time goes in v4:
time: 64.2 us; the launch traced here: 63.8 us
  Pallas kernels  33.4 us (52%)
  starting transfers between devices  17.6 us (27%)
  waiting for transfers between devices  12.6 us (20%)
    pallas_call x8, Pallas kernels, call(): pl.pallas_call(kernel, out_shape=tuple(scalar_shapes) + tuple(shapes), in...  33.4 us
    ppermute x15, starting transfers between devices, permute(): lax.ppermute(x, axis, [(i, pairs_of(i)) for i in range(lax.axis_size(axis...  17.6 us
    ppermute x15, waiting for transfers between devices, permute(): lax.ppermute(x, axis, [(i, pairs_of(i)) for i in range(lax.axis_size(axis...  12.6 us
  transfers between devices with their start and end apart: 15, of which 5 were waited for; matrix products, arithmetic and copies ran while one was open for 0% of the time, Pallas kernels for 41%

profile of v4, /device:TPU:0, one launch (start us, length us, event | category | flops | bytes accessed | tf_op | source)
XLA Modules:
  0.0 63.8 jit_solution(9989844596006245893)
XLA Ops:
  0.0 0.5 collective-permute-start.3
  0.5 3.5 %shard_map.83 = (s32[3,9]{1,0:T(4,128)S(1)}, f32[1024,128]{1,0:T(8,128)S(1)}, f32[3072,128]{1,0:T(8,128)S(1)}, f32[384,128]{1,0:T(8,128)S(1)}, f32[192,128]{1,0:...) custom-call(s32[8,5]{1,0:T(8,128)} %routes.3, s32[8]{0:T(128)} %owner.3, ...), custom_call_target="tpu_custom_call" | custom-call | bytes 9000000 | tf_op jit(solution)/shard_map/pallas_call | solution.py:583
  4.0 2.5 %collective-permute-start.6 = (f32[1024,128]{1,0:T(8,128)S(1)}, f32[1024,128]{1,0:T(8,128)S(1)}, u32[]{:S(2)}, u32[]{:S(2)}) collective-permute-start(f32[1024,128]{1,0:T(8,128)S(1)} %get-tuple-element.52), channel_id=1, source_target_pairs={{0,2},{2,0},{1,3},{3,1},{4,6},{6,4},{5,7},{7,5},{8,10},{10,8},{9,1... | collective-permute-start | bytes 1572872 | tf_op jit(solution)/shard_map/ppermute | solution.py:29
  6.6 1.6 %collective-permute-start = (f32[336,128]{1,0:T(8,128)S(1)}, f32[336,128]{1,0:T(8,128)S(1)}, u32[]{:S(2)}, u32[]{:S(2)}) collective-permute-start(f32[336,128]{1,0:T(8,128)S(1)} %get-tuple-element.39), channel_id=1, source_target_pairs={{0,4},{4,0},{8,12},{12,8},{1,5},{5,1},{9,13},{13,9},{2,6},{6,2},{1... | collective-permute-start | bytes 516104 | tf_op jit(solution)/shard_map/ppermute | solution.py:29
  8.1 2.6 %collective-permute-start.1 = (f32[336,128]{1,0:T(8,128)S(1)}, f32[336,128]{1,0:T(8,128)S(1)}, u32[]{:S(2)}, u32[]{:S(2)}) collective-permute-start(f32[336,128]{1,0:T(8,128)S(1)} %get-tuple-element.40), channel_id=1, source_target_pairs={{0,8},{4,12},{8,0},{12,4},{1,9},{5,13},{9,1},{13,5},{2,10},{6,14},... | collective-permute-start | bytes 516104 | tf_op jit(solution)/shard_map/ppermute | solution.py:29
  10.7 0.2 collective-permute-start.2
  11.0 2.9 %shard_map.82 = (s32[3,18]{1,0:T(4,128)S(1)}, f32[5,8]{1,0:T(8,128)S(1)}, bf16[144,192]{1,0:T(8,128)(2,1)S(1)}, bf16[128,192]{1,0:T(8,128)(2,1)S(1)}, f32[16,128]{1,0:T(8,128)S(1)}) custom-call(s32[8,5]{1,0:T(8,128)} %routes.3, s32[8]{0:T(128)} %owner.3, s32[2,8]{1,0:T(2,128)} %bitcast.5, f32[2]{0:T(128)} %service.1, f32[3,3]{1,0:T(4,128)} %sources.1, ...), custom_call_target="tpu_custom_call" | custom-call | bytes 6000000 | tf_op jit(solution)/shard_map/pallas_call | solution.py:583
  13.9 0.0 collective-permute-done.3.other
  13.9 0.1 collective-permute-start.4
  13.9 3.1 %shard_map.84 = (f32[3072,128]{1,0:T(8,128)S(1)}, f32[1024,128]{1,0:T(8,128)S(1)}) custom-call(s32[3,18]{1,0:T(4,128)S(1)} %get-tuple-element.35.plan.refs_0_, f32[5,8]{1,0:T(8,128)S(1)} %get-tuple-element.36.rates.refs_1_, bf16[144,192]{1,0:T(8,128)(2,1)S(1)} %get-tuple-element.42.weights, f32[16,128]{1,0:T(8,128)S(1)} %get-tuple-element.43.exits, ...), custom_call_target="tpu_custom_call" | custom-call | bytes 9000000 | tf_op jit(solution)/shard_map/pallas_call | solution.py:583
  17.1 5.6 %shard_map.85.refs_4_ = f32[3072,128]{1,0:T(8,128)S(1)} custom-call(s32[3,18]{1,0:T(4,128)S(1)} %get-tuple-element.35.plan.refs_0_, f32[5,8]{1,0:T(8,128)S(1)} %get-tuple-element.36.rates.refs_1_, bf16[144,192]{1,0:T(8,128)(2,1)S(1)} %get-tuple-element.42.weights, f32[16,128]{1,0:T(8,128)S(1)} %get-tuple-element.43.exits, ...), custom_call_target="tpu_custom_call", output_to_operand_aliasing={{}: (6, {})} | custom-call | bytes 18000000 | tf_op jit(solution)/shard_map/pallas_call | solution.py:583
  22.7 0.0 collective-permute-done.refs_11_
  22.7 1.0 %collective-permute-done.1.refs_12_ = f32[336,128]{1,0:T(8,128)S(1)} collective-permute-done((f32[336,128]{1,0:T(8,128)S(1)}, f32[336,128]{1,0:T(8,128)S(1)}, u32[]{:S(2)}, u32[]{:S(2)}) %collective-permute-start.1) | collective-permute-done | bytes 172064 | tf_op jit(solution)/shard_map/ppermute | solution.py:29
  23.7 0.1 collective-permute-start.5
  23.8 0.0 collective-permute-done.4.refs_7_
  23.8 1.2 %collective-permute-done.5.refs_10_ = f32[128,128]{1,0:T(8,128)S(1)} collective-permute-done((f32[128,128]{1,0:T(8,128)S(1)}, f32[128,128]{1,0:T(8,128)S(1)}, u32[]{:S(2)}, u32[]{:S(2)}) %collective-permute-start.5) | collective-permute-done | bytes 65568 | tf_op jit(solution)/shard_map/ppermute | solution.py:29
  25.0 4.7 %shard_map.86 = (f32[3072,128]{1,0:T(8,128)S(1)}, f32[1552,128]{1,0:T(8,128)S(1)}, f32[384,128]{1,0:T(8,128)S(1)}, f32[192,128]{1,0:T(8,128)S(1)}, f32[336,128]{...) custom-call(s32[3,18]{1,0:T(4,128)S(1)} %get-tuple-element.35.plan.refs_0_, ...), custom_call_target="tpu_custom_call" | custom-call | bytes 12000000 | tf_op jit(solution)/shard_map/pallas_call | solution.py:583
  29.7 0.2 collective-permute-start.10
  29.9 0.5 collective-permute-start.11
  30.5 1.5 %collective-permute-start.14 = (f32[1552,128]{1,0:T(8,128)S(1)}, f32[1552,128]{1,0:T(8,128)S(1)}, u32[]{:S(2)}, u32[]{:S(2)}) collective-permute-start(f32[1552,128]{1,0:T(8,128)S(1)} %get-tuple-element.64), channel_id=1, source_target_pairs={{0,2},{2,0},{1,3},{3,1},{4,6},{6,4},{5,7},{7,5},{8,10},{10,8},{9,1... | collective-permute-start | bytes 2383880 | tf_op jit(solution)/shard_map/ppermute | solution.py:29
  32.0 3.3 %collective-permute-start.7 = (f32[336,128]{1,0:T(8,128)S(1)}, f32[336,128]{1,0:T(8,128)S(1)}, u32[]{:S(2)}, u32[]{:S(2)}) collective-permute-start(f32[336,128]{1,0:T(8,128)S(1)} %get-tuple-element.53), channel_id=1, source_target_pairs={{0,4},{4,0},{8,12},{12,8},{1,5},{5,1},{9,13},{13,9},{2,6},{6,2},{1... | collective-permute-start | bytes 516104 | tf_op jit(solution)/shard_map/ppermute | solution.py:29
  35.2 1.0 %collective-permute-start.8 = (f32[336,128]{1,0:T(8,128)S(1)}, f32[336,128]{1,0:T(8,128)S(1)}, u32[]{:S(2)}, u32[]{:S(2)}) collective-permute-start(f32[336,128]{1,0:T(8,128)S(1)} %get-tuple-element.54), channel_id=1, source_target_pairs={{0,8},{4,12},{8,0},{12,4},{1,9},{5,13},{9,1},{13,5},{2,10},{6,14},... | collective-permute-start | bytes 516104 | tf_op jit(solution)/shard_map/ppermute | solution.py:29
  36.3 8.5 %collective-permute-done.11.refs_2_ = f32[1024,128]{1,0:T(8,128)S(1)} collective-permute-done((f32[1024,128]{1,0:T(8,128)S(1)}, f32[1024,128]{1,0:T(8,128)S(1)}, u32[]{:S(2)}, u32[]{:S(2)}) %collective-permute-start.11) | collective-permute-done | bytes 524320 | tf_op jit(solution)/shard_map/ppermute | solution.py:29
  44.7 3.0 %collective-permute-start.9 = (f32[336,128]{1,0:T(8,128)S(1)}, f32[336,128]{1,0:T(8,128)S(1)}, u32[]{:S(2)}, u32[]{:S(2)}) collective-permute-start(f32[336,128]{1,0:T(8,128)S(1)} %get-tuple-element.55), channel_id=1, source_target_pairs={{0,12},{4,8},{8,4},{12,0},{1,13},{5,9},{9,5},{13,1},{2,14},{6,10},... | collective-permute-start | bytes 516104 | tf_op jit(solution)/shard_map/ppermute | solution.py:29
  47.7 8.1 %shard_map.87.refs_3_ = f32[3072,128]{1,0:T(8,128)S(1)} custom-call(s32[3,18]{1,0:T(4,128)S(1)} %get-tuple-element.35.plan.refs_0_, f32[5,8]{1,0:T(8,128)S(1)} %get-tuple-element.36.rates.refs_1_, bf16[144,192]{1,0:T(8,128)(2,1)S(1)} %get-tuple-element.42.weights, f32[16,128]{1,0:T(8,128)S(1)} %get-tuple-element.43.exits, ...), custom_call_target="tpu_custom_call" | custom-call | bytes 27000000 | tf_op jit(solution)/shard_map/pallas_call | solution.py:583
  55.9 0.0 collective-permute-done.7.refs_10_
  55.9 0.0 collective-permute-done.8.refs_11_
  55.9 0.6 collective-permute-start.13
  56.5 0.9 %collective-permute-done.13.refs_9_ = f32[128,128]{1,0:T(8,128)S(1)} collective-permute-done((f32[128,128]{1,0:T(8,128)S(1)}, f32[128,128]{1,0:T(8,128)S(1)}, u32[]{:S(2)}, u32[]{:S(2)}) %collective-permute-start.13) | collective-permute-done | bytes 65568 | tf_op jit(solution)/shard_map/ppermute | solution.py:29
  57.4 2.8 %shard_map.88.stepped = f32[3072,128]{1,0:T(8,128)S(1)} custom-call(s32[3,18]{1,0:T(4,128)S(1)} %get-tuple-element.35.plan.refs_0_, f32[5,8]{1,0:T(8,128)S(1)} %get-tuple-element.36.rates.refs_1_, bf16[128,192]{1,0:T(8,128)(2,1)S(1)} %get-tuple-element.37.refs_3_.refs_2_, f32[3072,128]{1,0:T(8,128)S(1)} %shard_map.87.refs_3_, ...), custom_call_target="tpu_custom_call" | custom-call | bytes 12000000 | tf_op jit(solution)/shard_map/pallas_call | solution.py:583
  60.2 0.9 %collective-permute-done.14.got_late = f32[1552,128]{1,0:T(8,128)S(1)} collective-permute-done((f32[1552,128]{1,0:T(8,128)S(1)}, f32[1552,128]{1,0:T(8,128)S(1)}, u32[]{:S(2)}, u32[]{:S(2)}) %collective-permute-start.14) | collective-permute-done | bytes 794656 | tf_op jit(solution)/shard_map/ppermute | solution.py:29
  61.2 2.6 %shard_map.89 = f32[3072,128]{1,0:T(8,128)} custom-call(s32[3,18]{1,0:T(4,128)S(1)} %get-tuple-element.35.plan.refs_0_, f32[5,8]{1,0:T(8,128)S(1)} %get-tuple-element.36.rates.refs_1_, f32[3072,128]{1,0:T(8,128)S(1)} %shard_map.88.stepped, f32[1552,128]{1,0:T(8,128)S(1)} %collective-permute-done.14.got_late), custom_call_target="tpu_custom_call" | custom-call | bytes 9000000 | tf_op jit(solution)/shard_map/pallas_call | solution.py:583
  (8 shorter events, 0.0 us)
Async XLA Ops:
  0.0 13.9 %collective-permute-start.3 = (f32[3072,128]{1,0:T(8,128)}, f32[3072,128]{1,0:T(8,128)S(1)}, u32[]{:S(2)}, u32[]{:S(2)}) collective-permute-start(f32[3072,128]{1,0:T(8,128)} %bitcast.3), channel_id=1, source_target_pairs={{0,1},{1,0},{2,3},{3,2},{4,5},{5,4},{6,7},{7,6},{8,9},{9,8},{10,11... | collective-permute-start | bytes 4718600 | tf_op jit(solution)/shard_map/ppermute | solution.py:29
  4.0 19.8 %collective-permute-start.6 = (f32[1024,128]{1,0:T(8,128)S(1)}, f32[1024,128]{1,0:T(8,128)S(1)}, u32[]{:S(2)}, u32[]{:S(2)}) collective-permute-start(f32[1024,128]{1,0:T(8,128)S(1)} %get-tuple-element.52), channel_id=1, source_target_pairs={{0,2},{2,0},{1,3},{3,1},{4,6},{6,4},{5,7},{7,5},{8,10},{10,8},{9,1... | collective-permute-start | bytes 1572872 | tf_op jit(solution)/shard_map/ppermute | solution.py:29
  6.6 16.1 %collective-permute-start = (f32[336,128]{1,0:T(8,128)S(1)}, f32[336,128]{1,0:T(8,128)S(1)}, u32[]{:S(2)}, u32[]{:S(2)}) collective-permute-start(f32[336,128]{1,0:T(8,128)S(1)} %get-tuple-element.39), channel_id=1, source_target_pairs={{0,4},{4,0},{8,12},{12,8},{1,5},{5,1},{9,13},{13,9},{2,6},{6,2},{1... | collective-permute-start | bytes 516104 | tf_op jit(solution)/shard_map/ppermute | solution.py:29
  8.1 15.5 %collective-permute-start.1 = (f32[336,128]{1,0:T(8,128)S(1)}, f32[336,128]{1,0:T(8,128)S(1)}, u32[]{:S(2)}, u32[]{:S(2)}) collective-permute-start(f32[336,128]{1,0:T(8,128)S(1)} %get-tuple-element.40), channel_id=1, source_target_pairs={{0,8},{4,12},{8,0},{12,4},{1,9},{5,13},{9,1},{13,5},{2,10},{6,14},... | collective-permute-start | bytes 516104 | tf_op jit(solution)/shard_map/ppermute | solution.py:29
  10.7 12.9 %collective-permute-start.2 = (f32[336,128]{1,0:T(8,128)S(1)}, f32[336,128]{1,0:T(8,128)S(1)}, u32[]{:S(2)}, u32[]{:S(2)}) collective-permute-start(f32[336,128]{1,0:T(8,128)S(1)} %get-tuple-element.41), channel_id=1, source_target_pairs={{0,12},{4,8},{8,4},{12,0},{1,13},{5,9},{9,5},{13,1},{2,14},{6,10},... | collective-permute-start | bytes 516104 | tf_op jit(solution)/shard_map/ppermute | solution.py:29
  13.9 9.9 %collective-permute-start.4 = (f32[384,128]{1,0:T(8,128)S(1)}, f32[384,128]{1,0:T(8,128)S(1)}, u32[]{:S(2)}, u32[]{:S(2)}) collective-permute-start(f32[384,128]{1,0:T(8,128)S(1)} %get-tuple-element.47.refs_6_), channel_id=1, source_target_pairs={{0,1},{1,0},{2,3},{3,2},{4,5},{5,4},{6,7},{7,6},{8,9},{9,8},{10,11... | collective-permute-start | bytes 589832 | tf_op jit(solution)/shard_map/ppermute | solution.py:29
  23.7 1.3 %collective-permute-start.5 = (f32[128,128]{1,0:T(8,128)S(1)}, f32[128,128]{1,0:T(8,128)S(1)}, u32[]{:S(2)}, u32[]{:S(2)}) collective-permute-start(f32[128,128]{1,0:T(8,128)S(1)} %slice_add_fusion.1.refs_9_), channel_id=1, source_target_pairs={{0,1},{1,0},{2,3},{3,2},{4,5},{5,4},{6,7},{7,6},{8,9},{9,8},{10,11... | collective-permute-start | bytes 196616 | tf_op jit(solution)/shard_map/ppermute | solution.py:29
  29.7 18.0 %collective-permute-start.10 = (f32[3072,128]{1,0:T(8,128)S(1)}, f32[3072,128]{1,0:T(8,128)S(1)}, u32[]{:S(2)}, u32[]{:S(2)}) collective-permute-start(f32[3072,128]{1,0:T(8,128)S(1)} %get-tuple-element.56.own.refs_4_), channel_id=1, source_target_pairs={{0,1},{1,0},{2,3},{3,2},{4,5},{5,4},{6,7},{7,6},{8,9},{9,8},{10,11... | collective-permute-start | bytes 4718600 | tf_op jit(solution)/shard_map/ppermute | solution.py:29
  29.9 14.8 %collective-permute-start.11 = (f32[1024,128]{1,0:T(8,128)S(1)}, f32[1024,128]{1,0:T(8,128)S(1)}, u32[]{:S(2)}, u32[]{:S(2)}) collective-permute-start(f32[1024,128]{1,0:T(8,128)S(1)} %get-tuple-element.57), channel_id=1, source_target_pairs={{0,2},{2,0},{1,3},{3,1},{4,6},{6,4},{5,7},{7,5},{8,10},{10,8},{9,1... | collective-permute-start | bytes 1572872 | tf_op jit(solution)/shard_map/ppermute | solution.py:29
  30.5 30.7 %collective-permute-start.14 = (f32[1552,128]{1,0:T(8,128)S(1)}, f32[1552,128]{1,0:T(8,128)S(1)}, u32[]{:S(2)}, u32[]{:S(2)}) collective-permute-start(f32[1552,128]{1,0:T(8,128)S(1)} %get-tuple-element.64), channel_id=1, source_target_pairs={{0,2},{2,0},{1,3},{3,1},{4,6},{6,4},{5,7},{7,5},{8,10},{10,8},{9,1... | collective-permute-start | bytes 2383880 | tf_op jit(solution)/shard_map/ppermute | solution.py:29
  32.0 23.9 %collective-permute-start.7 = (f32[336,128]{1,0:T(8,128)S(1)}, f32[336,128]{1,0:T(8,128)S(1)}, u32[]{:S(2)}, u32[]{:S(2)}) collective-permute-start(f32[336,128]{1,0:T(8,128)S(1)} %get-tuple-element.53), channel_id=1, source_target_pairs={{0,4},{4,0},{8,12},{12,8},{1,5},{5,1},{9,13},{13,9},{2,6},{6,2},{1... | collective-permute-start | bytes 516104 | tf_op jit(solution)/shard_map/ppermute | solution.py:29
  35.2 20.6 %collective-permute-start.8 = (f32[336,128]{1,0:T(8,128)S(1)}, f32[336,128]{1,0:T(8,128)S(1)}, u32[]{:S(2)}, u32[]{:S(2)}) collective-permute-start(f32[336,128]{1,0:T(8,128)S(1)} %get-tuple-element.54), channel_id=1, source_target_pairs={{0,8},{4,12},{8,0},{12,4},{1,9},{5,13},{9,1},{13,5},{2,10},{6,14},... | collective-permute-start | bytes 516104 | tf_op jit(solution)/shard_map/ppermute | solution.py:29
  44.7 11.1 %collective-permute-start.9 = (f32[336,128]{1,0:T(8,128)S(1)}, f32[336,128]{1,0:T(8,128)S(1)}, u32[]{:S(2)}, u32[]{:S(2)}) collective-permute-start(f32[336,128]{1,0:T(8,128)S(1)} %get-tuple-element.55), channel_id=1, source_target_pairs={{0,12},{4,8},{8,4},{12,0},{1,13},{5,9},{9,5},{13,1},{2,14},{6,10},... | collective-permute-start | bytes 516104 | tf_op jit(solution)/shard_map/ppermute | solution.py:29
  47.7 8.8 %collective-permute-start.12 = (f32[384,128]{1,0:T(8,128)S(1)}, f32[384,128]{1,0:T(8,128)S(1)}, u32[]{:S(2)}, u32[]{:S(2)}) collective-permute-start(f32[384,128]{1,0:T(8,128)S(1)} %get-tuple-element.59.refs_5_), channel_id=1, source_target_pairs={{0,1},{1,0},{2,3},{3,2},{4,5},{5,4},{6,7},{7,6},{8,9},{9,8},{10,11... | collective-permute-start | bytes 589832 | tf_op jit(solution)/shard_map/ppermute | solution.py:29
  55.9 1.5 %collective-permute-start.13 = (f32[128,128]{1,0:T(8,128)S(1)}, f32[128,128]{1,0:T(8,128)S(1)}, u32[]{:S(2)}, u32[]{:S(2)}) collective-permute-start(f32[128,128]{1,0:T(8,128)S(1)} %slice_add_fusion.refs_8_), channel_id=1, source_target_pairs={{0,1},{1,0},{2,3},{3,2},{4,5},{5,4},{6,7},{7,6},{8,9},{9,8},{10,11... | collective-permute-start | bytes 196616 | tf_op jit(solution)/shard_map/ppermute | solution.py:29

commit v5 on v4

--- a/solution.py
+++ b/solution.py
@@ -17,7 +17,7 @@
 VM = pltpu.VMEM
 SM = pltpu.SMEM
 GRANT = 24 << 20
-PACK_TURN, JOIN_TURN = 4, 4
+PACK_TURN = 4
 
 FEED, STAY, FEED_MORE, STAY_MORE, SQUARE, INFLOW = 0, 1, 2, 3, 4, 5
 TILE, LEVEL_ONE, LEVEL_TWO, ROUTES = 0, 1, 2, 3
@@ -64,7 +64,8 @@
         self.mid_rows = (self.mid_end - self.raw_end) * self.wide_two * self.phases
         self.ends_at = self.states * self.wide_two * self.phases
         self.rims_at = self.ends_at + self.mid_end * 2 * self.phases
-        self.columns_at = self.rims_at + self.mid_end * self.rim_parts * self.phases
+        self.rim_units = max(self.mid_end - self.states, self.raw_end)
+        self.columns_at = self.rims_at + self.rim_units * self.rim_parts * self.phases
         self.per_column = LANES // self.wide_two
         self.late_rows = self.columns_at + -(-self.mid_end // self.per_column) * self.phases
         self.power = levels & (levels - 1) == 0
@@ -82,6 +83,10 @@
 
     def rim_at(self, unit, part):
         return self.at((unit * self.rim_parts + part) * self.phases)
+
+    def sent_rim_at(self, unit, part):
+        index = unit if isinstance(unit, int) else jnp.where(unit < self.raw_end, unit, unit - self.states)
+        return self.at(self.rims_at + (index * self.rim_parts + part) * self.phases)
 
     def small_at(self, state):
         return state // self.per_small, (state % self.per_small) * self.lane_step
@@ -473,8 +478,9 @@
             if group != "last":
                 sent[sh.at(sh.ends_at + 2 * unit * phases), :] = sent_first
                 sent[sh.at(sh.ends_at + (2 * unit + 1) * phases), :] = sent_last
-                for part in range(sh.rim_parts):
-                    sent[sh.at(sh.rims_at + (unit * sh.rim_parts + part) * phases), :] = rim_scale * rims[part]
+                if group != "second":
+                    for part in range(sh.rim_parts):
+                        sent[sh.sent_rim_at(unit, part), :] = rim_scale * rims[part]
                 place = sh.at(sh.columns_at + lax.div(unit, jnp.int32(sh.per_column)) * phases)
                 base = lax.rem(unit, jnp.int32(sh.per_column)) * sh.wide_two
                 sent[place, :] = sent[place, :] + column_scale * pltpu.roll(above, base, 1)
@@ -519,7 +525,10 @@
 
     if sent is not None:
         sweep(0, sh.raw_end, turn, functools.partial(unit_step, "raw"))
-        sweep(sh.raw_end, sh.mid_end, turn, functools.partial(unit_step, "mid"))
+        second_end = min(2 * sh.states, sh.mid_end)
+        sweep(sh.raw_end, second_end, turn, functools.partial(unit_step, "second"))
+        if sh.mid_end > second_end:
+            sweep(second_end, sh.mid_end, turn, functools.partial(unit_step, "mid"))
         sweep(sh.mid_end, sh.units, turn, functools.partial(unit_step, "last"))
     else:
         sweep(0, sh.units, turn, functools.partial(unit_step, None))
@@ -531,30 +540,39 @@
     phases, last_u = sh.phases, sh.wide_two - 1
     lane = lane_ids((phases, LANES))
     inflow = rates[0, INFLOW + sh.bits]
-
-    def unit_step(group, unit):
-        filled = plan[lax.div(unit, jnp.int32(sh.states)), TILE] >= 0
+    slot = pl.program_id(0)
+    filled = plan[slot, TILE] >= 0
+
+    def unit_step(group, state):
+        unit = slot * sh.states + state
         if group != "last":
-            rims = [
-                got_late[sh.at(sh.rims_at + (unit * sh.rim_parts + part) * phases), :] for part in range(sh.rim_parts)
-            ]
             column = got_late[sh.at(sh.columns_at + lax.div(unit, jnp.int32(sh.per_column)) * phases), :]
             base = lax.rem(unit, jnp.int32(sh.per_column)) * sh.wide_two
+        if group == "rims":
+            rims = [got_late[sh.sent_rim_at(unit, part), :] for part in range(sh.rim_parts)]
         for u in range(sh.wide_two):
             if group == "last":
                 got = got_late[sh.by_level(unit - sh.mid_end, u), :]
             else:
-                part, q = u // sh.rim_group, u % sh.rim_group
-                got = jnp.where(lane < BATCH, pltpu.roll(rims[part], LANES - q * BATCH, 1) if q else rims[part], 0.0)
+                got = jnp.zeros((phases, LANES), F32)
+                if group == "rims":
+                    part, q = u // sh.rim_group, u % sh.rim_group
+                    got = jnp.where(lane < BATCH, pltpu.roll(rims[part], LANES - q * BATCH, 1) if q else rims[part], 0.0)
                 if u:
                     got = jnp.where(lane == LANES - 1, pltpu.roll(column, LANES - (base + u), 1), got)
                 if u in (0, last_u):
                     got = got + got_late[sh.at(sh.ends_at + (2 * unit + (1 if u else 0)) * phases), :]
             total = stepped[sh.by_level(unit, u), :] + inflow * got
-            out[sh.native(unit, u), :] = jnp.where(filled, total, 0.0)
-
-    sweep(0, sh.mid_end, JOIN_TURN, functools.partial(unit_step, None))
-    sweep(sh.mid_end, sh.units, JOIN_TURN, functools.partial(unit_step, "last"))
+            out[sh.native(state, u), :] = jnp.where(filled, total, 0.0)
+
+    def slot_step(group):
+        sweep(0, sh.states, 4, functools.partial(unit_step, group))
+
+    last = slot == sh.slots - 1
+    second = jnp.logical_and(slot == 1, jnp.logical_not(last))
+    pl.when(last)(functools.partial(slot_step, "last"))
+    pl.when(second)(functools.partial(slot_step, "second"))
+    pl.when(jnp.logical_not(jnp.logical_or(last, second)))(functools.partial(slot_step, "rims"))
 
 
 def body(
@@ -609,11 +627,10 @@
     def in_hbm(values):
         return [pltpu.with_memory_space_constraint(v, pltpu.HBM) for v in values]
 
-    routes, tile_owner, flat = in_hbm([routes, tile_owner, flat])
     send_plan, *outs = call(
         functools.partial(pack_kernel, sh),
-        [routes, tile_owner],
-        [flat],
+        in_hbm([routes, tile_owner]),
+        in_hbm([flat]),
         ([array(sh.raw_rows)] if sh.deferred else []) + [array(sh.rows)] + packed_shapes,
         3,
         [table(n - 1, PICKS + 2 * sh.slots, I32)],
@@ -625,8 +642,8 @@
     start, rims, columns, messages = outs[0], outs[1], outs[2], outs[3:]
     plan, rates, paired, rim_paired, exits = call(
         functools.partial(prep_kernel, sh),
-        [routes, tile_owner, *in_hbm([tile_levels.T, service_rates, source_rates])],
-        in_hbm([phase_rates, batch_rates]),
+        [routes, tile_owner, tile_levels.T, service_rates, source_rates],
+        [phase_rates, batch_rates],
         [
             table((BATCH // 2 + 1) * sh.phases, 6 * full, BF16),
             table((BATCH // 2) * sh.phases, 6 * full, BF16),
@@ -678,9 +695,14 @@
         )
         got, inside = exchange(messages, inside)
         (twice,) = halo(False, inside, once, rims, columns, got, [])
-        (result,) = call(
-            functools.partial(join_kernel, sh), [plan, rates], [twice, got_late], [array(sh.rows)], 3
-        )
+        result = pl.pallas_call(
+            functools.partial(join_kernel, sh),
+            grid=(sh.slots,),
+            out_shape=array(sh.rows),
+            in_specs=[smem] * 2 + [vmem] * 2,
+            out_specs=pl.BlockSpec((sh.rows // sh.slots, LANES), lambda k: (k, 0)),
+            compiler_params=pltpu.CompilerParams(vmem_limit_bytes=GRANT),
+        )(plan, rates, twice, got_late)
     else:
         (inside,) = inner(True, start, other, [(None, 0, sh.units)])
         got, inside = exchange(messages, inside)

time: 64.2 us -> 63.2 us (0.984)
    pallas_call x8 -> x7, Pallas kernels: 33.4 us -> 30.5 us  [call(): pl.pallas_call(kernel, out_shape=tuple(scalar_shapes) + tuple(shapes), in...]
    pallas_call x0 -> x1, Pallas kernels: none -> 2.8 us  [body(): pl.pallas_call(functools.partial(join_kernel, sh), grid=(sh.slots,), out_...]
  transfers between devices with their start and end apart: 15 -> 15, of which waited for: 5 -> 4; matrix products, arithmetic and copies ran while one was open for 0% -> 0% of each run, Pallas kernels for 41% -> 41%
where the time goes in v5:
time: 63.2 us; the launch traced here: 63 us
  Pallas kernels  33.3 us (53%)
  starting transfers between devices  17.5 us (28%)
  waiting for transfers between devices  12 us (19%)
    pallas_call x7, Pallas kernels, call(): pl.pallas_call(kernel, out_shape=tuple(scalar_shapes) + tuple(shapes), in...  30.5 us
    ppermute x15, starting transfers between devices, permute(): lax.ppermute(x, axis, [(i, pairs_of(i)) for i in range(lax.axis_size(axis...  17.5 us
    ppermute x15, waiting for transfers between devices, permute(): lax.ppermute(x, axis, [(i, pairs_of(i)) for i in range(lax.axis_size(axis...  12 us
    pallas_call x1, Pallas kernels, body(): pl.pallas_call(functools.partial(join_kernel, sh), grid=(sh.slots,), out_...  2.8 us
  transfers between devices with their start and end apart: 15, of which 4 were waited for; matrix products, arithmetic and copies ran while one was open for 0% of the time, Pallas kernels for 41%

profile of v5, /device:TPU:0, one launch (start us, length us, event | category | flops | bytes accessed | tf_op | source)
XLA Modules:
  0.0 63.0 jit_solution(1216705739021636526)
XLA Ops:
  0.0 0.6 collective-permute-start.3
  0.6 3.5 %shard_map.83 = (s32[3,9]{1,0:T(4,128)S(1)}, f32[1024,128]{1,0:T(8,128)S(1)}, f32[3072,128]{1,0:T(8,128)S(1)}, f32[384,128]{1,0:T(8,128)S(1)}, f32[192,128]{1,0:...) custom-call(s32[8,5]{1,0:T(8,128)} %routes.3, s32[8]{0:T(128)} %owner.3, ...), custom_call_target="tpu_custom_call" | custom-call | bytes 9000000 | tf_op jit(solution)/shard_map/pallas_call | solution.py:601
  4.1 2.7 %collective-permute-start.6 = (f32[1024,128]{1,0:T(8,128)S(1)}, f32[1024,128]{1,0:T(8,128)S(1)}, u32[]{:S(2)}, u32[]{:S(2)}) collective-permute-start(f32[1024,128]{1,0:T(8,128)S(1)} %get-tuple-element.52), channel_id=1, source_target_pairs={{0,2},{2,0},{1,3},{3,1},{4,6},{6,4},{5,7},{7,5},{8,10},{10,8},{9,1... | collective-permute-start | bytes 1572872 | tf_op jit(solution)/shard_map/ppermute | solution.py:29
  6.8 1.6 %collective-permute-start = (f32[336,128]{1,0:T(8,128)S(1)}, f32[336,128]{1,0:T(8,128)S(1)}, u32[]{:S(2)}, u32[]{:S(2)}) collective-permute-start(f32[336,128]{1,0:T(8,128)S(1)} %get-tuple-element.39), channel_id=1, source_target_pairs={{0,4},{4,0},{8,12},{12,8},{1,5},{5,1},{9,13},{13,9},{2,6},{6,2},{1... | collective-permute-start | bytes 516104 | tf_op jit(solution)/shard_map/ppermute | solution.py:29
  8.4 2.6 %collective-permute-start.1 = (f32[336,128]{1,0:T(8,128)S(1)}, f32[336,128]{1,0:T(8,128)S(1)}, u32[]{:S(2)}, u32[]{:S(2)}) collective-permute-start(f32[336,128]{1,0:T(8,128)S(1)} %get-tuple-element.40), channel_id=1, source_target_pairs={{0,8},{4,12},{8,0},{12,4},{1,9},{5,13},{9,1},{13,5},{2,10},{6,14},... | collective-permute-start | bytes 516104 | tf_op jit(solution)/shard_map/ppermute | solution.py:29
  11.0 0.2 collective-permute-start.2
  11.3 2.6 %shard_map.82 = (s32[3,18]{1,0:T(4,128)S(1)}, f32[5,8]{1,0:T(8,128)S(1)}, bf16[144,192]{1,0:T(8,128)(2,1)S(1)}, bf16[128,192]{1,0:T(8,128)(2,1)S(1)}, f32[16,128]{1,0:T(8,128)S(1)}) custom-call(s32[8,5]{1,0:T(8,128)S(1)} %copy-done.1, s32[8]{0:T(128)S(1)} %copy-done.4, s32[2,8]{1,0:T(2,128)S(1)} %bitcast.3, f32[2]{0:T(128)S(1)} %copy-done.6, ...), custom_call_target="tpu_custom_call" | custom-call | bytes 6000000 | tf_op jit(solution)/shard_map/pallas_call | solution.py:601
  13.9 0.1 collective-permute-start.4
  13.9 3.1 %shard_map.84 = (f32[3072,128]{1,0:T(8,128)S(1)}, f32[1024,128]{1,0:T(8,128)S(1)}) custom-call(s32[3,18]{1,0:T(4,128)S(1)} %get-tuple-element.35.plan.refs_0_, f32[5,8]{1,0:T(8,128)S(1)} %get-tuple-element.36.rates.refs_1_, bf16[144,192]{1,0:T(8,128)(2,1)S(1)} %get-tuple-element.42.weights, f32[16,128]{1,0:T(8,128)S(1)} %get-tuple-element.43.exits, ...), custom_call_target="tpu_custom_call" | custom-call | bytes 9000000 | tf_op jit(solution)/shard_map/pallas_call | solution.py:601
  17.1 5.6 %shard_map.85.refs_4_ = f32[3072,128]{1,0:T(8,128)S(1)} custom-call(s32[3,18]{1,0:T(4,128)S(1)} %get-tuple-element.35.plan.refs_0_, f32[5,8]{1,0:T(8,128)S(1)} %get-tuple-element.36.rates.refs_1_, bf16[144,192]{1,0:T(8,128)(2,1)S(1)} %get-tuple-element.42.weights, f32[16,128]{1,0:T(8,128)S(1)} %get-tuple-element.43.exits, ...), custom_call_target="tpu_custom_call", output_to_operand_aliasing={{}: (6, {})} | custom-call | bytes 18000000 | tf_op jit(solution)/shard_map/pallas_call | solution.py:601
  22.7 0.0 collective-permute-done.refs_11_
  22.7 1.2 %collective-permute-done.1.refs_12_ = f32[336,128]{1,0:T(8,128)S(1)} collective-permute-done((f32[336,128]{1,0:T(8,128)S(1)}, f32[336,128]{1,0:T(8,128)S(1)}, u32[]{:S(2)}, u32[]{:S(2)}) %collective-permute-start.1) | collective-permute-done | bytes 172064 | tf_op jit(solution)/shard_map/ppermute | solution.py:29
  23.9 0.0 collective-permute-done.2.refs_13_
  24.0 0.1 collective-permute-start.5
  24.0 0.0 collective-permute-done.4.refs_7_
  24.1 1.2 %collective-permute-done.5.refs_10_ = f32[128,128]{1,0:T(8,128)S(1)} collective-permute-done((f32[128,128]{1,0:T(8,128)S(1)}, f32[128,128]{1,0:T(8,128)S(1)}, u32[]{:S(2)}, u32[]{:S(2)}) %collective-permute-start.5) | collective-permute-done | bytes 65568 | tf_op jit(solution)/shard_map/ppermute | solution.py:29
  25.3 4.7 %shard_map.86 = (f32[3072,128]{1,0:T(8,128)S(1)}, f32[1424,128]{1,0:T(8,128)S(1)}, f32[384,128]{1,0:T(8,128)S(1)}, f32[192,128]{1,0:T(8,128)S(1)}, f32[336,128]{...) custom-call(s32[3,18]{1,0:T(4,128)S(1)} %get-tuple-element.35.plan.refs_0_, ...), custom_call_target="tpu_custom_call" | custom-call | bytes 12000000 | tf_op jit(solution)/shard_map/pallas_call | solution.py:601
  30.0 0.2 collective-permute-start.10
  30.2 0.5 collective-permute-start.11
  30.8 1.5 %collective-permute-start.14 = (f32[1424,128]{1,0:T(8,128)S(1)}, f32[1424,128]{1,0:T(8,128)S(1)}, u32[]{:S(2)}, u32[]{:S(2)}) collective-permute-start(f32[1424,128]{1,0:T(8,128)S(1)} %get-tuple-element.64), channel_id=1, source_target_pairs={{0,2},{2,0},{1,3},{3,1},{4,6},{6,4},{5,7},{7,5},{8,10},{10,8},{9,1... | collective-permute-start | bytes 2187272 | tf_op jit(solution)/shard_map/ppermute | solution.py:29
  32.2 3.1 %collective-permute-start.7 = (f32[336,128]{1,0:T(8,128)S(1)}, f32[336,128]{1,0:T(8,128)S(1)}, u32[]{:S(2)}, u32[]{:S(2)}) collective-permute-start(f32[336,128]{1,0:T(8,128)S(1)} %get-tuple-element.53), channel_id=1, source_target_pairs={{0,4},{4,0},{8,12},{12,8},{1,5},{5,1},{9,13},{13,9},{2,6},{6,2},{1... | collective-permute-start | bytes 516104 | tf_op jit(solution)/shard_map/ppermute | solution.py:29
  35.4 1.0 %collective-permute-start.8 = (f32[336,128]{1,0:T(8,128)S(1)}, f32[336,128]{1,0:T(8,128)S(1)}, u32[]{:S(2)}, u32[]{:S(2)}) collective-permute-start(f32[336,128]{1,0:T(8,128)S(1)} %get-tuple-element.54), channel_id=1, source_target_pairs={{0,8},{4,12},{8,0},{12,4},{1,9},{5,13},{9,1},{13,5},{2,10},{6,14},... | collective-permute-start | bytes 516104 | tf_op jit(solution)/shard_map/ppermute | solution.py:29
  36.4 8.6 %collective-permute-done.11.refs_2_ = f32[1024,128]{1,0:T(8,128)S(1)} collective-permute-done((f32[1024,128]{1,0:T(8,128)S(1)}, f32[1024,128]{1,0:T(8,128)S(1)}, u32[]{:S(2)}, u32[]{:S(2)}) %collective-permute-start.11) | collective-permute-done | bytes 524320 | tf_op jit(solution)/shard_map/ppermute | solution.py:29
  45.0 2.7 %collective-permute-start.9 = (f32[336,128]{1,0:T(8,128)S(1)}, f32[336,128]{1,0:T(8,128)S(1)}, u32[]{:S(2)}, u32[]{:S(2)}) collective-permute-start(f32[336,128]{1,0:T(8,128)S(1)} %get-tuple-element.55), channel_id=1, source_target_pairs={{0,12},{4,8},{8,4},{12,0},{1,13},{5,9},{9,5},{13,1},{2,14},{6,10},... | collective-permute-start | bytes 516104 | tf_op jit(solution)/shard_map/ppermute | solution.py:29
  47.7 0.0 collective-permute-done.10.other
  47.7 8.1 %shard_map.87.refs_3_ = f32[3072,128]{1,0:T(8,128)S(1)} custom-call(s32[3,18]{1,0:T(4,128)S(1)} %get-tuple-element.35.plan.refs_0_, f32[5,8]{1,0:T(8,128)S(1)} %get-tuple-element.36.rates.refs_1_, bf16[144,192]{1,0:T(8,128)(2,1)S(1)} %get-tuple-element.42.weights, f32[16,128]{1,0:T(8,128)S(1)} %get-tuple-element.43.exits, ...), custom_call_target="tpu_custom_call" | custom-call | bytes 27000000 | tf_op jit(solution)/shard_map/pallas_call | solution.py:601
  55.9 0.0 collective-permute-done.9.refs_12_
  55.9 0.6 collective-permute-start.13
  56.5 0.9 %collective-permute-done.13.refs_9_ = f32[128,128]{1,0:T(8,128)S(1)} collective-permute-done((f32[128,128]{1,0:T(8,128)S(1)}, f32[128,128]{1,0:T(8,128)S(1)}, u32[]{:S(2)}, u32[]{:S(2)}) %collective-permute-start.13) | collective-permute-done | bytes 65568 | tf_op jit(solution)/shard_map/ppermute | solution.py:29
  57.4 2.8 %shard_map.88.stepped = f32[3072,128]{1,0:T(8,128)S(1)} custom-call(s32[3,18]{1,0:T(4,128)S(1)} %get-tuple-element.35.plan.refs_0_, f32[5,8]{1,0:T(8,128)S(1)} %get-tuple-element.36.rates.refs_1_, bf16[128,192]{1,0:T(8,128)(2,1)S(1)} %get-tuple-element.37.refs_3_.refs_2_, f32[3072,128]{1,0:T(8,128)S(1)} %shard_map.87.refs_3_, ...), custom_call_target="tpu_custom_call" | custom-call | bytes 12000000 | tf_op jit(solution)/shard_map/pallas_call | solution.py:601
  60.2 0.0 collective-permute-done.14.got_late
  60.2 2.8 %shard_map.89 = f32[3072,128]{1,0:T(8,128)} custom-call(s32[3,18]{1,0:T(4,128)S(1)} %get-tuple-element.35.plan.refs_0_, f32[5,8]{1,0:T(8,128)S(1)} %get-tuple-element.36.rates.refs_1_, f32[3072,128]{1,0:T(8,128)S(1)} %shard_map.88.stepped, f32[1424,128]{1,0:T(8,128)S(1)} %collective-permute-done.14.got_late), custom_call_target="tpu_custom_call" | custom-call | tf_op jit(solution)/shard_map/pallas_call | solution.py:698
  (22 shorter events, 0.1 us)
Async XLA Ops:
  0.0 11.2 %copy-start.1 = (s32[8,5]{1,0:T(8,128)S(1)}, s32[8,5]{1,0:T(8,128)}, u32[]{:S(2)}) copy-start(s32[8,5]{1,0:T(8,128)} %routes.3) | copy-start | bytes 484
  0.0 11.2 %copy-start.4 = (s32[8]{0:T(128)S(1)}, s32[8]{0:T(128)}, u32[]{:S(2)}) copy-start(s32[8]{0:T(128)} %owner.3) | copy-start | bytes 100
  0.0 11.2 %copy-start.5 = (s32[8,2]{0,1:T(2,128)S(1)}, s32[8,2]{0,1:T(2,128)}, u32[]{:S(2)}) copy-start(s32[8,2]{0,1:T(2,128)} %param.13) | copy-start | bytes 196
  0.0 11.2 %copy-start = (f32[16,32,32]{2,1,0:T(8,128)S(1)}, f32[16,32,32]{2,1,0:T(8,128)}, u32[]{:S(2)}) copy-start(f32[16,32,32]{2,1,0:T(8,128)} %batch_rates.1) | copy-start | bytes 196612
  0.0 11.2 %copy-start.6 = (f32[2]{0:T(128)S(1)}, f32[2]{0:T(128)}, u32[]{:S(2)}) copy-start(f32[2]{0:T(128)} %service.1) | copy-start | bytes 28
  0.0 11.2 %copy-start.3 = (f32[3,3]{1,0:T(4,128)S(1)}, f32[3,3]{1,0:T(4,128)}, u32[]{:S(2)}) copy-start(f32[3,3]{1,0:T(4,128)} %sources.1) | copy-start | bytes 112
  0.0 11.2 %copy-start.2 = (f32[32,32]{1,0:T(8,128)S(1)}, f32[32,32]{1,0:T(8,128)}, u32[]{:S(2)}) copy-start(f32[32,32]{1,0:T(8,128)} %phase_rates.1) | copy-start | bytes 12292
  0.0 13.8 %collective-permute-start.3 = (f32[3072,128]{1,0:T(8,128)}, f32[3072,128]{1,0:T(8,128)S(1)}, u32[]{:S(2)}, u32[]{:S(2)}) collective-permute-start(f32[3072,128]{1,0:T(8,128)} %bitcast.4), channel_id=1, source_target_pairs={{0,1},{1,0},{2,3},{3,2},{4,5},{5,4},{6,7},{7,6},{8,9},{9,8},{10,11... | collective-permute-start | bytes 4718600 | tf_op jit(solution)/shard_map/ppermute | solution.py:29
  4.1 19.9 %collective-permute-start.6 = (f32[1024,128]{1,0:T(8,128)S(1)}, f32[1024,128]{1,0:T(8,128)S(1)}, u32[]{:S(2)}, u32[]{:S(2)}) collective-permute-start(f32[1024,128]{1,0:T(8,128)S(1)} %get-tuple-element.52), channel_id=1, source_target_pairs={{0,2},{2,0},{1,3},{3,1},{4,6},{6,4},{5,7},{7,5},{8,10},{10,8},{9,1... | collective-permute-start | bytes 1572872 | tf_op jit(solution)/shard_map/ppermute | solution.py:29
  6.8 15.8 %collective-permute-start = (f32[336,128]{1,0:T(8,128)S(1)}, f32[336,128]{1,0:T(8,128)S(1)}, u32[]{:S(2)}, u32[]{:S(2)}) collective-permute-start(f32[336,128]{1,0:T(8,128)S(1)} %get-tuple-element.39), channel_id=1, source_target_pairs={{0,4},{4,0},{8,12},{12,8},{1,5},{5,1},{9,13},{13,9},{2,6},{6,2},{1... | collective-permute-start | bytes 516104 | tf_op jit(solution)/shard_map/ppermute | solution.py:29
  8.4 15.5 %collective-permute-start.1 = (f32[336,128]{1,0:T(8,128)S(1)}, f32[336,128]{1,0:T(8,128)S(1)}, u32[]{:S(2)}, u32[]{:S(2)}) collective-permute-start(f32[336,128]{1,0:T(8,128)S(1)} %get-tuple-element.40), channel_id=1, source_target_pairs={{0,8},{4,12},{8,0},{12,4},{1,9},{5,13},{9,1},{13,5},{2,10},{6,14},... | collective-permute-start | bytes 516104 | tf_op jit(solution)/shard_map/ppermute | solution.py:29
  11.0 12.9 %collective-permute-start.2 = (f32[336,128]{1,0:T(8,128)S(1)}, f32[336,128]{1,0:T(8,128)S(1)}, u32[]{:S(2)}, u32[]{:S(2)}) collective-permute-start(f32[336,128]{1,0:T(8,128)S(1)} %get-tuple-element.41), channel_id=1, source_target_pairs={{0,12},{4,8},{8,4},{12,0},{1,13},{5,9},{9,5},{13,1},{2,14},{6,10},... | collective-permute-start | bytes 516104 | tf_op jit(solution)/shard_map/ppermute | solution.py:29
  13.9 10.2 %collective-permute-start.4 = (f32[384,128]{1,0:T(8,128)S(1)}, f32[384,128]{1,0:T(8,128)S(1)}, u32[]{:S(2)}, u32[]{:S(2)}) collective-permute-start(f32[384,128]{1,0:T(8,128)S(1)} %get-tuple-element.47.refs_6_), channel_id=1, source_target_pairs={{0,1},{1,0},{2,3},{3,2},{4,5},{5,4},{6,7},{7,6},{8,9},{9,8},{10,11... | collective-permute-start | bytes 589832 | tf_op jit(solution)/shard_map/ppermute | solution.py:29
  24.0 1.3 %collective-permute-start.5 = (f32[128,128]{1,0:T(8,128)S(1)}, f32[128,128]{1,0:T(8,128)S(1)}, u32[]{:S(2)}, u32[]{:S(2)}) collective-permute-start(f32[128,128]{1,0:T(8,128)S(1)} %slice_add_fusion.1.refs_9_), channel_id=1, source_target_pairs={{0,1},{1,0},{2,3},{3,2},{4,5},{5,4},{6,7},{7,6},{8,9},{9,8},{10,11... | collective-permute-start | bytes 196616 | tf_op jit(solution)/shard_map/ppermute | solution.py:29
  30.0 17.7 %collective-permute-start.10 = (f32[3072,128]{1,0:T(8,128)S(1)}, f32[3072,128]{1,0:T(8,128)S(1)}, u32[]{:S(2)}, u32[]{:S(2)}) collective-permute-start(f32[3072,128]{1,0:T(8,128)S(1)} %get-tuple-element.56.own.refs_4_), channel_id=1, source_target_pairs={{0,1},{1,0},{2,3},{3,2},{4,5},{5,4},{6,7},{7,6},{8,9},{9,8},{10,11... | collective-permute-start | bytes 4718600 | tf_op jit(solution)/shard_map/ppermute | solution.py:29
  30.2 14.8 %collective-permute-start.11 = (f32[1024,128]{1,0:T(8,128)S(1)}, f32[1024,128]{1,0:T(8,128)S(1)}, u32[]{:S(2)}, u32[]{:S(2)}) collective-permute-start(f32[1024,128]{1,0:T(8,128)S(1)} %get-tuple-element.57), channel_id=1, source_target_pairs={{0,2},{2,0},{1,3},{3,1},{4,6},{6,4},{5,7},{7,5},{8,10},{10,8},{9,1... | collective-permute-start | bytes 1572872 | tf_op jit(solution)/shard_map/ppermute | solution.py:29
  30.8 29.5 %collective-permute-start.14 = (f32[1424,128]{1,0:T(8,128)S(1)}, f32[1424,128]{1,0:T(8,128)S(1)}, u32[]{:S(2)}, u32[]{:S(2)}) collective-permute-start(f32[1424,128]{1,0:T(8,128)S(1)} %get-tuple-element.64), channel_id=1, source_target_pairs={{0,2},{2,0},{1,3},{3,1},{4,6},{6,4},{5,7},{7,5},{8,10},{10,8},{9,1... | collective-permute-start | bytes 2187272 | tf_op jit(solution)/shard_map/ppermute | solution.py:29
  32.2 23.6 %collective-permute-start.7 = (f32[336,128]{1,0:T(8,128)S(1)}, f32[336,128]{1,0:T(8,128)S(1)}, u32[]{:S(2)}, u32[]{:S(2)}) collective-permute-start(f32[336,128]{1,0:T(8,128)S(1)} %get-tuple-element.53), channel_id=1, source_target_pairs={{0,4},{4,0},{8,12},{12,8},{1,5},{5,1},{9,13},{13,9},{2,6},{6,2},{1... | collective-permute-start | bytes 516104 | tf_op jit(solution)/shard_map/ppermute | solution.py:29
  35.4 20.5 %collective-permute-start.8 = (f32[336,128]{1,0:T(8,128)S(1)}, f32[336,128]{1,0:T(8,128)S(1)}, u32[]{:S(2)}, u32[]{:S(2)}) collective-permute-start(f32[336,128]{1,0:T(8,128)S(1)} %get-tuple-element.54), channel_id=1, source_target_pairs={{0,8},{4,12},{8,0},{12,4},{1,9},{5,13},{9,1},{13,5},{2,10},{6,14},... | collective-permute-start | bytes 516104 | tf_op jit(solution)/shard_map/ppermute | solution.py:29
  45.0 10.9 %collective-permute-start.9 = (f32[336,128]{1,0:T(8,128)S(1)}, f32[336,128]{1,0:T(8,128)S(1)}, u32[]{:S(2)}, u32[]{:S(2)}) collective-permute-start(f32[336,128]{1,0:T(8,128)S(1)} %get-tuple-element.55), channel_id=1, source_target_pairs={{0,12},{4,8},{8,4},{12,0},{1,13},{5,9},{9,5},{13,1},{2,14},{6,10},... | collective-permute-start | bytes 516104 | tf_op jit(solution)/shard_map/ppermute | solution.py:29
  47.7 8.8 %collective-permute-start.12 = (f32[384,128]{1,0:T(8,128)S(1)}, f32[384,128]{1,0:T(8,128)S(1)}, u32[]{:S(2)}, u32[]{:S(2)}) collective-permute-start(f32[384,128]{1,0:T(8,128)S(1)} %get-tuple-element.59.refs_5_), channel_id=1, source_target_pairs={{0,1},{1,0},{2,3},{3,2},{4,5},{5,4},{6,7},{7,6},{8,9},{9,8},{10,11... | collective-permute-start | bytes 589832 | tf_op jit(solution)/shard_map/ppermute | solution.py:29
  55.9 1.5 %collective-permute-start.13 = (f32[128,128]{1,0:T(8,128)S(1)}, f32[128,128]{1,0:T(8,128)S(1)}, u32[]{:S(2)}, u32[]{:S(2)}) collective-permute-start(f32[128,128]{1,0:T(8,128)S(1)} %slice_add_fusion.refs_8_), channel_id=1, source_target_pairs={{0,1},{1,0},{2,3},{3,2},{4,5},{5,4},{6,7},{7,6},{8,9},{9,8},{10,11... | collective-permute-start | bytes 196616 | tf_op jit(solution)/shard_map/ppermute | solution.py:29

commit v6 on v5

--- a/solution.py
+++ b/solution.py
@@ -18,6 +18,8 @@
 SM = pltpu.SMEM
 GRANT = 24 << 20
 PACK_TURN = 4
+GROUP = 3
+GROUPS = -(-(BATCH + 1) // GROUP)
 
 FEED, STAY, FEED_MORE, STAY_MORE, SQUARE, INFLOW = 0, 1, 2, 3, 4, 5
 TILE, LEVEL_ONE, LEVEL_TWO, ROUTES = 0, 1, 2, 3
@@ -292,7 +294,7 @@
             rates[s, STAY_MORE] = (feed + outflow) - (feed_there + outflow_there)
             rates[s, SQUARE] = inflow[sh.bits] * inflow_there[sh.bits]
 
-    for b in range(BATCH + 2):
+    for b in range(GROUP * GROUPS):
         if b <= BATCH:
             values = (moving if b == 0 else batch_rates[b - 1]) * scale
             turned[0:full, :] = values
@@ -309,8 +311,8 @@
             if 1 <= b <= BATCH:
                 column = ((b - 1) % 2) * 3 * full + i * full
                 rim_paired[((b - 1) // 2) * phases:((b - 1) // 2 + 1) * phases, column:column + full] = part
-            column = (b % 2) * 3 * full + i * full
-            paired[(b // 2) * phases:(b // 2 + 1) * phases, column:column + full] = part
+            column = (b % GROUP) * 3 * full + i * full
+            paired[(b // GROUP) * phases:(b // GROUP + 1) * phases, column:column + full] = part
 
 
 def split(values):
@@ -327,7 +329,7 @@
     serve_one, serve_two = rates[sh.states, 0], rates[sh.states, 1]
     lane = lane_ids((phases, LANES))
     inner_one = jnp.where(lane == LANES - 1, 0.0, serve_one)
-    later = lane_ids((weights.shape[1] // 6, LANES)) > 0
+    level = lane_ids((weights.shape[1] // (3 * GROUP), LANES))
 
     def unit_step(group, unit):
         k = lax.div(unit, jnp.int32(sh.states))
@@ -339,14 +341,17 @@
             columns = []
             for u in (2 * pair, 2 * pair + 1):
                 values = jnp.concatenate([own[sh.by_level(unit, u), :], other[other_at(unit, u), :]], axis=0)
-                columns.append(jnp.concatenate(split(values) + split(jnp.where(later, pltpu.roll(values, 1, 1), 0.0)), axis=0))
+                parts = split(values)
+                for e in range(1, GROUP):
+                    parts += split(jnp.where(level >= e, pltpu.roll(values, e, 1), 0.0))
+                columns.append(jnp.concatenate(parts, axis=0))
             product = jnp.dot(weights[...], jnp.concatenate(columns, axis=1), preferred_element_type=F32)
             for j, u in enumerate((2 * pair, 2 * pair + 1)):
                 lanes = slice(j * LANES, (j + 1) * LANES)
                 total = product[0:phases, lanes]
-                for b in range(1, BATCH // 2 + 1):
-                    moved = pltpu.roll(product[b * phases:(b + 1) * phases, lanes], 2 * b, 1)
-                    total = total + jnp.where(lane >= 2 * b, moved, 0.0)
+                for b in range(1, GROUPS):
+                    moved = pltpu.roll(product[b * phases:(b + 1) * phases, lanes], GROUP * b, 1)
+                    total = total + jnp.where(lane >= GROUP * b, moved, 0.0)
                 here = own[sh.by_level(unit, u), :]
                 two = serve_two if u else jnp.where(c > 0, serve_two, 0.0)
                 total = total + (stay - two) * here
@@ -375,7 +380,7 @@
                     sent[sh.by_level(unit - sh.raw_end, u), :] = 2.0 * total + more
 
     for group, start, stop in spans:
-        sweep(start, stop, 1, functools.partial(unit_step, group))
+        sweep(start, stop, 2, functools.partial(unit_step, group))
 
 
 def halo_kernel(sh, first, *refs):
@@ -645,7 +650,7 @@
         [routes, tile_owner, tile_levels.T, service_rates, source_rates],
         [phase_rates, batch_rates],
         [
-            table((BATCH // 2 + 1) * sh.phases, 6 * full, BF16),
+            table(GROUPS * sh.phases, 3 * GROUP * full, BF16),
             table((BATCH // 2) * sh.phases, 6 * full, BF16),
             array(sh.phases),
         ],

time: 63.2 us -> 63 us (level)
  waiting for transfers between devices: 12 us -> 15.3 us
  Pallas kernels: 33.3 us -> 30 us
    ppermute x15, waiting for transfers between devices: 12 us -> 15.3 us  [permute(): lax.ppermute(x, axis, [(i, pairs_of(i)) for i in range(lax.axis_size(axis...]
    pallas_call x7, Pallas kernels: 30.5 us -> 27.3 us  [call(): pl.pallas_call(kernel, out_shape=tuple(scalar_shapes) + tuple(shapes), in...]
  transfers between devices with their start and end apart: 15 -> 15, of which waited for: 4 -> 5; matrix products, arithmetic and copies ran while one was open for 0% -> 0% of each run, Pallas kernels for 41% -> 36%
where the time goes in v6:
time: 63 us; the launch traced here: 62.8 us
  Pallas kernels  30 us (48%)
  starting transfers between devices  17.2 us (27%)
  waiting for transfers between devices  15.3 us (24%)
    pallas_call x7, Pallas kernels, call(): pl.pallas_call(kernel, out_shape=tuple(scalar_shapes) + tuple(shapes), in...  27.3 us
    ppermute x15, starting transfers between devices, permute(): lax.ppermute(x, axis, [(i, pairs_of(i)) for i in range(lax.axis_size(axis...  17.2 us
    ppermute x15, waiting for transfers between devices, permute(): lax.ppermute(x, axis, [(i, pairs_of(i)) for i in range(lax.axis_size(axis...  15.3 us
    pallas_call x1, Pallas kernels, body(): pl.pallas_call(functools.partial(join_kernel, sh), grid=(sh.slots,), out_...  2.76 us
  transfers between devices with their start and end apart: 15, of which 5 were waited for; matrix products, arithmetic and copies ran while one was open for 0% of the time, Pallas kernels for 36%

profile of v6, /device:TPU:0, one launch (start us, length us, event | category | flops | bytes accessed | tf_op | source)
XLA Modules:
  0.0 62.8 jit_solution(763522929309988435)
XLA Ops:
  0.0 0.6 collective-permute-start.3
  0.6 3.5 %shard_map.83 = (s32[3,9]{1,0:T(4,128)S(1)}, f32[1024,128]{1,0:T(8,128)S(1)}, f32[3072,128]{1,0:T(8,128)S(1)}, f32[384,128]{1,0:T(8,128)S(1)}, f32[192,128]{1,0:...) custom-call(s32[8,5]{1,0:T(8,128)} %routes.3, s32[8]{0:T(128)} %owner.3, ...), custom_call_target="tpu_custom_call" | custom-call | bytes 9000000 | tf_op jit(solution)/shard_map/pallas_call | solution.py:606
  4.1 2.7 %collective-permute-start.6 = (f32[1024,128]{1,0:T(8,128)S(1)}, f32[1024,128]{1,0:T(8,128)S(1)}, u32[]{:S(2)}, u32[]{:S(2)}) collective-permute-start(f32[1024,128]{1,0:T(8,128)S(1)} %get-tuple-element.52), channel_id=1, source_target_pairs={{0,2},{2,0},{1,3},{3,1},{4,6},{6,4},{5,7},{7,5},{8,10},{10,8},{9,1... | collective-permute-start | bytes 1572872 | tf_op jit(solution)/shard_map/ppermute | solution.py:31
  6.8 1.6 %collective-permute-start = (f32[336,128]{1,0:T(8,128)S(1)}, f32[336,128]{1,0:T(8,128)S(1)}, u32[]{:S(2)}, u32[]{:S(2)}) collective-permute-start(f32[336,128]{1,0:T(8,128)S(1)} %get-tuple-element.39), channel_id=1, source_target_pairs={{0,4},{4,0},{8,12},{12,8},{1,5},{5,1},{9,13},{13,9},{2,6},{6,2},{1... | collective-permute-start | bytes 516104 | tf_op jit(solution)/shard_map/ppermute | solution.py:31
  8.4 2.6 %collective-permute-start.1 = (f32[336,128]{1,0:T(8,128)S(1)}, f32[336,128]{1,0:T(8,128)S(1)}, u32[]{:S(2)}, u32[]{:S(2)}) collective-permute-start(f32[336,128]{1,0:T(8,128)S(1)} %get-tuple-element.40), channel_id=1, source_target_pairs={{0,8},{4,12},{8,0},{12,4},{1,9},{5,13},{9,1},{13,5},{2,10},{6,14},... | collective-permute-start | bytes 516104 | tf_op jit(solution)/shard_map/ppermute | solution.py:31
  11.0 0.2 collective-permute-start.2
  11.3 2.5 %shard_map.82 = (s32[3,18]{1,0:T(4,128)S(1)}, f32[5,8]{1,0:T(8,128)S(1)}, bf16[96,288]{1,0:T(8,128)(2,1)S(1)}, bf16[128,192]{1,0:T(8,128)(2,1)S(1)}, f32[16,128]{1,0:T(8,128)S(1)}) custom-call(s32[8,5]{1,0:T(8,128)S(1)} %copy-done.1, s32[8]{0:T(128)S(1)} %copy-done.4, s32[2,8]{1,0:T(2,128)S(1)} %bitcast.3, f32[2]{0:T(128)S(1)} %copy-done.6, ...), custom_call_target="tpu_custom_call" | custom-call | bytes 6000000 | tf_op jit(solution)/shard_map/pallas_call | solution.py:606
  13.8 0.0 collective-permute-done.3.other
  13.8 0.1 collective-permute-start.4
  13.9 2.6 %shard_map.84 = (f32[3072,128]{1,0:T(8,128)S(1)}, f32[1024,128]{1,0:T(8,128)S(1)}) custom-call(s32[3,18]{1,0:T(4,128)S(1)} %get-tuple-element.35.plan.refs_0_, f32[5,8]{1,0:T(8,128)S(1)} %get-tuple-element.36.rates.refs_1_, bf16[96,288]{1,0:T(8,128)(2,1)S(1)} %get-tuple-element.42.weights, f32[16,128]{1,0:T(8,128)S(1)} %get-tuple-element.43.exits, ...), custom_call_target="tpu_custom_call" | custom-call | bytes 9000000 | tf_op jit(solution)/shard_map/pallas_call | solution.py:606
  16.5 4.5 %shard_map.85.refs_4_ = f32[3072,128]{1,0:T(8,128)S(1)} custom-call(s32[3,18]{1,0:T(4,128)S(1)} %get-tuple-element.35.plan.refs_0_, f32[5,8]{1,0:T(8,128)S(1)} %get-tuple-element.36.rates.refs_1_, bf16[96,288]{1,0:T(8,128)(2,1)S(1)} %get-tuple-element.42.weights, f32[16,128]{1,0:T(8,128)S(1)} %get-tuple-element.43.exits, ...), custom_call_target="tpu_custom_call", output_to_operand_aliasing={{}: (6, {})} | custom-call | bytes 18000000 | tf_op jit(solution)/shard_map/pallas_call | solution.py:606
  21.0 0.0 collective-permute-done.refs_11_
  21.0 2.9 %collective-permute-done.1.refs_12_ = f32[336,128]{1,0:T(8,128)S(1)} collective-permute-done((f32[336,128]{1,0:T(8,128)S(1)}, f32[336,128]{1,0:T(8,128)S(1)}, u32[]{:S(2)}, u32[]{:S(2)}) %collective-permute-start.1) | collective-permute-done | bytes 172064 | tf_op jit(solution)/shard_map/ppermute | solution.py:31
  23.9 0.0 collective-permute-done.2.refs_13_
  24.0 0.1 collective-permute-start.5
  24.0 0.0 collective-permute-done.4.refs_7_
  24.1 1.2 %collective-permute-done.5.refs_10_ = f32[128,128]{1,0:T(8,128)S(1)} collective-permute-done((f32[128,128]{1,0:T(8,128)S(1)}, f32[128,128]{1,0:T(8,128)S(1)}, u32[]{:S(2)}, u32[]{:S(2)}) %collective-permute-start.5) | collective-permute-done | bytes 65568 | tf_op jit(solution)/shard_map/ppermute | solution.py:31
  25.3 4.7 %shard_map.86 = (f32[3072,128]{1,0:T(8,128)S(1)}, f32[1424,128]{1,0:T(8,128)S(1)}, f32[384,128]{1,0:T(8,128)S(1)}, f32[192,128]{1,0:T(8,128)S(1)}, f32[336,128]{...) custom-call(s32[3,18]{1,0:T(4,128)S(1)} %get-tuple-element.35.plan.refs_0_, ...), custom_call_target="tpu_custom_call" | custom-call | bytes 12000000 | tf_op jit(solution)/shard_map/pallas_call | solution.py:606
  30.0 0.2 collective-permute-start.10
  30.2 0.5 collective-permute-start.11
  30.8 1.5 %collective-permute-start.14 = (f32[1424,128]{1,0:T(8,128)S(1)}, f32[1424,128]{1,0:T(8,128)S(1)}, u32[]{:S(2)}, u32[]{:S(2)}) collective-permute-start(f32[1424,128]{1,0:T(8,128)S(1)} %get-tuple-element.64), channel_id=1, source_target_pairs={{0,2},{2,0},{1,3},{3,1},{4,6},{6,4},{5,7},{7,5},{8,10},{10,8},{9,1... | collective-permute-start | bytes 2187272 | tf_op jit(solution)/shard_map/ppermute | solution.py:31
  32.2 3.1 %collective-permute-start.7 = (f32[336,128]{1,0:T(8,128)S(1)}, f32[336,128]{1,0:T(8,128)S(1)}, u32[]{:S(2)}, u32[]{:S(2)}) collective-permute-start(f32[336,128]{1,0:T(8,128)S(1)} %get-tuple-element.53), channel_id=1, source_target_pairs={{0,4},{4,0},{8,12},{12,8},{1,5},{5,1},{9,13},{13,9},{2,6},{6,2},{1... | collective-permute-start | bytes 516104 | tf_op jit(solution)/shard_map/ppermute | solution.py:31
  35.4 1.0 %collective-permute-start.8 = (f32[336,128]{1,0:T(8,128)S(1)}, f32[336,128]{1,0:T(8,128)S(1)}, u32[]{:S(2)}, u32[]{:S(2)}) collective-permute-start(f32[336,128]{1,0:T(8,128)S(1)} %get-tuple-element.54), channel_id=1, source_target_pairs={{0,8},{4,12},{8,0},{12,4},{1,9},{5,13},{9,1},{13,5},{2,10},{6,14},... | collective-permute-start | bytes 516104 | tf_op jit(solution)/shard_map/ppermute | solution.py:31
  36.4 8.6 %collective-permute-done.11.refs_2_ = f32[1024,128]{1,0:T(8,128)S(1)} collective-permute-done((f32[1024,128]{1,0:T(8,128)S(1)}, f32[1024,128]{1,0:T(8,128)S(1)}, u32[]{:S(2)}, u32[]{:S(2)}) %collective-permute-start.11) | collective-permute-done | bytes 524320 | tf_op jit(solution)/shard_map/ppermute | solution.py:31
  45.0 2.5 %collective-permute-start.9 = (f32[336,128]{1,0:T(8,128)S(1)}, f32[336,128]{1,0:T(8,128)S(1)}, u32[]{:S(2)}, u32[]{:S(2)}) collective-permute-start(f32[336,128]{1,0:T(8,128)S(1)} %get-tuple-element.55), channel_id=1, source_target_pairs={{0,12},{4,8},{8,4},{12,0},{1,13},{5,9},{9,5},{13,1},{2,14},{6,10},... | collective-permute-start | bytes 516104 | tf_op jit(solution)/shard_map/ppermute | solution.py:31
  47.5 6.6 %shard_map.87.refs_3_ = f32[3072,128]{1,0:T(8,128)S(1)} custom-call(s32[3,18]{1,0:T(4,128)S(1)} %get-tuple-element.35.plan.refs_0_, f32[5,8]{1,0:T(8,128)S(1)} %get-tuple-element.36.rates.refs_1_, bf16[96,288]{1,0:T(8,128)(2,1)S(1)} %get-tuple-element.42.weights, f32[16,128]{1,0:T(8,128)S(1)} %get-tuple-element.43.exits, ...), custom_call_target="tpu_custom_call" | custom-call | bytes 27000000 | tf_op jit(solution)/shard_map/pallas_call | solution.py:606
  54.1 0.0 collective-permute-done.9.refs_12_
  54.1 0.6 collective-permute-start.13
  54.7 0.9 %collective-permute-done.13.refs_9_ = f32[128,128]{1,0:T(8,128)S(1)} collective-permute-done((f32[128,128]{1,0:T(8,128)S(1)}, f32[128,128]{1,0:T(8,128)S(1)}, u32[]{:S(2)}, u32[]{:S(2)}) %collective-permute-start.13) | collective-permute-done | bytes 65568 | tf_op jit(solution)/shard_map/ppermute | solution.py:31
  55.6 2.8 %shard_map.88.stepped = f32[3072,128]{1,0:T(8,128)S(1)} custom-call(s32[3,18]{1,0:T(4,128)S(1)} %get-tuple-element.35.plan.refs_0_, f32[5,8]{1,0:T(8,128)S(1)} %get-tuple-element.36.rates.refs_1_, bf16[128,192]{1,0:T(8,128)(2,1)S(1)} %get-tuple-element.37.refs_3_.refs_2_, f32[3072,128]{1,0:T(8,128)S(1)} %shard_map.87.refs_3_, ...), custom_call_target="tpu_custom_call" | custom-call | bytes 12000000 | tf_op jit(solution)/shard_map/pallas_call | solution.py:606
  58.4 1.6 %collective-permute-done.14.got_late = f32[1424,128]{1,0:T(8,128)S(1)} collective-permute-done((f32[1424,128]{1,0:T(8,128)S(1)}, f32[1424,128]{1,0:T(8,128)S(1)}, u32[]{:S(2)}, u32[]{:S(2)}) %collective-permute-start.14) | collective-permute-done | bytes 729120 | tf_op jit(solution)/shard_map/ppermute | solution.py:31
  60.0 2.8 %shard_map.89 = f32[3072,128]{1,0:T(8,128)} custom-call(s32[3,18]{1,0:T(4,128)S(1)} %get-tuple-element.35.plan.refs_0_, f32[5,8]{1,0:T(8,128)S(1)} %get-tuple-element.36.rates.refs_1_, f32[3072,128]{1,0:T(8,128)S(1)} %shard_map.88.stepped, f32[1424,128]{1,0:T(8,128)S(1)} %collective-permute-done.14.got_late), custom_call_target="tpu_custom_call" | custom-call | tf_op jit(solution)/shard_map/pallas_call | solution.py:703
  (22 shorter events, 0.1 us)
Async XLA Ops:
  0.0 11.2 %copy-start.1 = (s32[8,5]{1,0:T(8,128)S(1)}, s32[8,5]{1,0:T(8,128)}, u32[]{:S(2)}) copy-start(s32[8,5]{1,0:T(8,128)} %routes.3) | copy-start | bytes 484
  0.0 11.2 %copy-start.4 = (s32[8]{0:T(128)S(1)}, s32[8]{0:T(128)}, u32[]{:S(2)}) copy-start(s32[8]{0:T(128)} %owner.3) | copy-start | bytes 100
  0.0 11.2 %copy-start.5 = (s32[8,2]{0,1:T(2,128)S(1)}, s32[8,2]{0,1:T(2,128)}, u32[]{:S(2)}) copy-start(s32[8,2]{0,1:T(2,128)} %param.13) | copy-start | bytes 196
  0.0 11.2 %copy-start = (f32[16,32,32]{2,1,0:T(8,128)S(1)}, f32[16,32,32]{2,1,0:T(8,128)}, u32[]{:S(2)}) copy-start(f32[16,32,32]{2,1,0:T(8,128)} %batch_rates.1) | copy-start | bytes 196612
  0.0 11.2 %copy-start.6 = (f32[2]{0:T(128)S(1)}, f32[2]{0:T(128)}, u32[]{:S(2)}) copy-start(f32[2]{0:T(128)} %service.1) | copy-start | bytes 28
  0.0 11.2 %copy-start.3 = (f32[3,3]{1,0:T(4,128)S(1)}, f32[3,3]{1,0:T(4,128)}, u32[]{:S(2)}) copy-start(f32[3,3]{1,0:T(4,128)} %sources.1) | copy-start | bytes 112
  0.0 11.2 %copy-start.2 = (f32[32,32]{1,0:T(8,128)S(1)}, f32[32,32]{1,0:T(8,128)}, u32[]{:S(2)}) copy-start(f32[32,32]{1,0:T(8,128)} %phase_rates.1) | copy-start | bytes 12292
  0.0 13.7 %collective-permute-start.3 = (f32[3072,128]{1,0:T(8,128)}, f32[3072,128]{1,0:T(8,128)S(1)}, u32[]{:S(2)}, u32[]{:S(2)}) collective-permute-start(f32[3072,128]{1,0:T(8,128)} %bitcast.4), channel_id=1, source_target_pairs={{0,1},{1,0},{2,3},{3,2},{4,5},{5,4},{6,7},{7,6},{8,9},{9,8},{10,11... | collective-permute-start | bytes 4718600 | tf_op jit(solution)/shard_map/ppermute | solution.py:31
  4.1 19.9 %collective-permute-start.6 = (f32[1024,128]{1,0:T(8,128)S(1)}, f32[1024,128]{1,0:T(8,128)S(1)}, u32[]{:S(2)}, u32[]{:S(2)}) collective-permute-start(f32[1024,128]{1,0:T(8,128)S(1)} %get-tuple-element.52), channel_id=1, source_target_pairs={{0,2},{2,0},{1,3},{3,1},{4,6},{6,4},{5,7},{7,5},{8,10},{10,8},{9,1... | collective-permute-start | bytes 1572872 | tf_op jit(solution)/shard_map/ppermute | solution.py:31
  6.8 14.2 %collective-permute-start = (f32[336,128]{1,0:T(8,128)S(1)}, f32[336,128]{1,0:T(8,128)S(1)}, u32[]{:S(2)}, u32[]{:S(2)}) collective-permute-start(f32[336,128]{1,0:T(8,128)S(1)} %get-tuple-element.39), channel_id=1, source_target_pairs={{0,4},{4,0},{8,12},{12,8},{1,5},{5,1},{9,13},{13,9},{2,6},{6,2},{1... | collective-permute-start | bytes 516104 | tf_op jit(solution)/shard_map/ppermute | solution.py:31
  8.4 15.5 %collective-permute-start.1 = (f32[336,128]{1,0:T(8,128)S(1)}, f32[336,128]{1,0:T(8,128)S(1)}, u32[]{:S(2)}, u32[]{:S(2)}) collective-permute-start(f32[336,128]{1,0:T(8,128)S(1)} %get-tuple-element.40), channel_id=1, source_target_pairs={{0,8},{4,12},{8,0},{12,4},{1,9},{5,13},{9,1},{13,5},{2,10},{6,14},... | collective-permute-start | bytes 516104 | tf_op jit(solution)/shard_map/ppermute | solution.py:31
  11.0 12.9 %collective-permute-start.2 = (f32[336,128]{1,0:T(8,128)S(1)}, f32[336,128]{1,0:T(8,128)S(1)}, u32[]{:S(2)}, u32[]{:S(2)}) collective-permute-start(f32[336,128]{1,0:T(8,128)S(1)} %get-tuple-element.41), channel_id=1, source_target_pairs={{0,12},{4,8},{8,4},{12,0},{1,13},{5,9},{9,5},{13,1},{2,14},{6,10},... | collective-permute-start | bytes 516104 | tf_op jit(solution)/shard_map/ppermute | solution.py:31
  13.8 10.3 %collective-permute-start.4 = (f32[384,128]{1,0:T(8,128)S(1)}, f32[384,128]{1,0:T(8,128)S(1)}, u32[]{:S(2)}, u32[]{:S(2)}) collective-permute-start(f32[384,128]{1,0:T(8,128)S(1)} %get-tuple-element.47.refs_6_), channel_id=1, source_target_pairs={{0,1},{1,0},{2,3},{3,2},{4,5},{5,4},{6,7},{7,6},{8,9},{9,8},{10,11... | collective-permute-start | bytes 589832 | tf_op jit(solution)/shard_map/ppermute | solution.py:31
  24.0 1.3 %collective-permute-start.5 = (f32[128,128]{1,0:T(8,128)S(1)}, f32[128,128]{1,0:T(8,128)S(1)}, u32[]{:S(2)}, u32[]{:S(2)}) collective-permute-start(f32[128,128]{1,0:T(8,128)S(1)} %slice_add_fusion.1.refs_9_), channel_id=1, source_target_pairs={{0,1},{1,0},{2,3},{3,2},{4,5},{5,4},{6,7},{7,6},{8,9},{9,8},{10,11... | collective-permute-start | bytes 196616 | tf_op jit(solution)/shard_map/ppermute | solution.py:31
  30.0 17.5 %collective-permute-start.10 = (f32[3072,128]{1,0:T(8,128)S(1)}, f32[3072,128]{1,0:T(8,128)S(1)}, u32[]{:S(2)}, u32[]{:S(2)}) collective-permute-start(f32[3072,128]{1,0:T(8,128)S(1)} %get-tuple-element.56.own.refs_4_), channel_id=1, source_target_pairs={{0,1},{1,0},{2,3},{3,2},{4,5},{5,4},{6,7},{7,6},{8,9},{9,8},{10,11... | collective-permute-start | bytes 4718600 | tf_op jit(solution)/shard_map/ppermute | solution.py:31
  30.2 14.8 %collective-permute-start.11 = (f32[1024,128]{1,0:T(8,128)S(1)}, f32[1024,128]{1,0:T(8,128)S(1)}, u32[]{:S(2)}, u32[]{:S(2)}) collective-permute-start(f32[1024,128]{1,0:T(8,128)S(1)} %get-tuple-element.57), channel_id=1, source_target_pairs={{0,2},{2,0},{1,3},{3,1},{4,6},{6,4},{5,7},{7,5},{8,10},{10,8},{9,1... | collective-permute-start | bytes 1572872 | tf_op jit(solution)/shard_map/ppermute | solution.py:31
  30.8 29.3 %collective-permute-start.14 = (f32[1424,128]{1,0:T(8,128)S(1)}, f32[1424,128]{1,0:T(8,128)S(1)}, u32[]{:S(2)}, u32[]{:S(2)}) collective-permute-start(f32[1424,128]{1,0:T(8,128)S(1)} %get-tuple-element.64), channel_id=1, source_target_pairs={{0,2},{2,0},{1,3},{3,1},{4,6},{6,4},{5,7},{7,5},{8,10},{10,8},{9,1... | collective-permute-start | bytes 2187272 | tf_op jit(solution)/shard_map/ppermute | solution.py:31
  32.2 21.8 %collective-permute-start.7 = (f32[336,128]{1,0:T(8,128)S(1)}, f32[336,128]{1,0:T(8,128)S(1)}, u32[]{:S(2)}, u32[]{:S(2)}) collective-permute-start(f32[336,128]{1,0:T(8,128)S(1)} %get-tuple-element.53), channel_id=1, source_target_pairs={{0,4},{4,0},{8,12},{12,8},{1,5},{5,1},{9,13},{13,9},{2,6},{6,2},{1... | collective-permute-start | bytes 516104 | tf_op jit(solution)/shard_map/ppermute | solution.py:31
  35.4 18.7 %collective-permute-start.8 = (f32[336,128]{1,0:T(8,128)S(1)}, f32[336,128]{1,0:T(8,128)S(1)}, u32[]{:S(2)}, u32[]{:S(2)}) collective-permute-start(f32[336,128]{1,0:T(8,128)S(1)} %get-tuple-element.54), channel_id=1, source_target_pairs={{0,8},{4,12},{8,0},{12,4},{1,9},{5,13},{9,1},{13,5},{2,10},{6,14},... | collective-permute-start | bytes 516104 | tf_op jit(solution)/shard_map/ppermute | solution.py:31
  45.0 9.1 %collective-permute-start.9 = (f32[336,128]{1,0:T(8,128)S(1)}, f32[336,128]{1,0:T(8,128)S(1)}, u32[]{:S(2)}, u32[]{:S(2)}) collective-permute-start(f32[336,128]{1,0:T(8,128)S(1)} %get-tuple-element.55), channel_id=1, source_target_pairs={{0,12},{4,8},{8,4},{12,0},{1,13},{5,9},{9,5},{13,1},{2,14},{6,10},... | collective-permute-start | bytes 516104 | tf_op jit(solution)/shard_map/ppermute | solution.py:31
  47.5 7.2 %collective-permute-start.12 = (f32[384,128]{1,0:T(8,128)S(1)}, f32[384,128]{1,0:T(8,128)S(1)}, u32[]{:S(2)}, u32[]{:S(2)}) collective-permute-start(f32[384,128]{1,0:T(8,128)S(1)} %get-tuple-element.59.refs_5_), channel_id=1, source_target_pairs={{0,1},{1,0},{2,3},{3,2},{4,5},{5,4},{6,7},{7,6},{8,9},{9,8},{10,11... | collective-permute-start | bytes 589832 | tf_op jit(solution)/shard_map/ppermute | solution.py:31
  54.1 1.5 %collective-permute-start.13 = (f32[128,128]{1,0:T(8,128)S(1)}, f32[128,128]{1,0:T(8,128)S(1)}, u32[]{:S(2)}, u32[]{:S(2)}) collective-permute-start(f32[128,128]{1,0:T(8,128)S(1)} %slice_add_fusion.refs_8_), channel_id=1, source_target_pairs={{0,1},{1,0},{2,3},{3,2},{4,5},{5,4},{6,7},{7,6},{8,9},{9,8},{10,11... | collective-permute-start | bytes 196616 | tf_op jit(solution)/shard_map/ppermute | solution.py:31
